TPU v7x, 256 devices: a whole 4x4x8 slice. The times are simulated.
256 devices in a mesh: freq: 128 (over z, y_lo, x, core), col: 2 (over y_hi).
Axes of the slice: x: 4, y: 4 (y_hi: 2, y_lo: 2; y = y_hi * 2 + y_lo), z: 8, core: 2. Of those that a mesh axis runs over, the one named last changes fastest.
Arguments:
- traces: bfloat16 [1024, 1024, 1024], P('freq', 'col'), may hold values from -6 to 6
- source_row: int32 [1024], replicated, may hold values from 0 to 1023, each once
Outputs:
- multiples: bfloat16 [2, 128, 1024, 1024], P(None, 'freq', None, 'col')
Inputs may be any that keep to these rules, and one draw needn't show every extreme that they name: `source_row`: a permutation of the 1024 acquisition rows.
All inputs are finite; a program needn't handle non-finite values.
Results may differ from a plain program's by a relative error of at most 0.0079.
Values may be sent and summed in bfloat16 or wider, within the bound.
No kernel may reach another device: no remote copies, remote signals or barrier semaphores. Data moves between devices by JAX's collectives and lax.ppermute only.
A program may use at most 64 MiB of HBM per device.

v0:
```python
import math

import jax
import jax.numpy as jnp
from jax import lax
from jax.sharding import PartitionSpec as P


def partner(value, axis, bit):
    return lax.ppermute(value, axis, [(i, i ^ 1 << bit) for i in range(lax.axis_size(axis))])


def dft_table(samples, kept):
    row_index = jnp.arange(2 * kept)
    frequency = (row_index % kept)[:, None]
    sample_index = jnp.arange(samples)[None, :]
    phase = frequency * sample_index % samples
    angle = 2.0 * math.pi / samples * phase.astype(jnp.float32)
    table = jnp.where(row_index[:, None] < kept, jnp.cos(angle), -jnp.sin(angle))
    return (table / jnp.sqrt(jnp.float32(samples))).astype(jnp.bfloat16)


def single_product(first, second):
    return jnp.einsum("fnk,fkh->fnh", first, second, preferred_element_type=jnp.float32)


def complex_product(left, right):
    real_part = single_product(left[0], right[0]) - single_product(left[1], right[1])
    imag_part = single_product(left[0], right[1]) + single_product(left[1], right[0])
    return jnp.stack([real_part, imag_part])


def ordered(own_block, other_block, is_first, concat_axis):
    upper = jnp.where(is_first, own_block, other_block)
    lower = jnp.where(is_first, other_block, own_block)
    return jnp.concatenate([upper, lower], concat_axis)


def mirror(block):
    return jnp.swapaxes(block, 2, 3)


def average(first, second):
    return ((first.astype(jnp.float32) + second.astype(jnp.float32)) * 0.5).astype(jnp.bfloat16)


def shards(traces, source_row):
    samples = traces.shape[2]
    kept = samples // 8
    table = dft_table(samples, kept)
    spectrum = jnp.einsum("kt,srt->ksr", table, traces, preferred_element_type=jnp.float32).astype(
        jnp.bfloat16
    )
    spectrum = spectrum.reshape(2, kept, traces.shape[0], traces.shape[1])
    acquired = lax.all_to_all(spectrum, "freq", split_axis=1, concat_axis=2, tiled=True)
    arranged = jnp.take(acquired, source_row, axis=2)
    width = arranged.shape[3]
    column_half = lax.axis_index("col")
    is_first = column_half == 0
    mine = lax.dynamic_slice_in_dim(arranged, column_half * width, width, 2)
    theirs = lax.dynamic_slice_in_dim(arranged, (1 - column_half) * width, width, 2)
    mirrored = partner(theirs, "col", 0)
    transposed = ordered(mirror(mine), mirror(mirrored), is_first, 2)
    spectral = average(arranged, transposed)
    whole = lax.all_gather(spectral, "col", axis=3, tiled=True)
    scale = 1.0 / math.sqrt(spectral.shape[2])
    square = (scale * complex_product(whole, spectral)).astype(jnp.bfloat16)
    cube = scale * complex_product(whole, square)
    return (spectral.astype(jnp.float32) - square.astype(jnp.float32) + cube).astype(jnp.bfloat16)


def solution(mesh):
    in_specs = (P("freq", "col", None), P())
    out_specs = P(None, "freq", None, "col")
    return jax.shard_map(shards, mesh=mesh, in_specs=in_specs, out_specs=out_specs, check_vma=False)
```

profile of v0, /device:TPU:1, one launch (start us, length us, event | category | flops | bytes accessed | tf_op | source)
XLA Modules:
  0.0 218.2 jit_solution(4405129899482517952)
XLA Ops:
  6.5 9.8 %convolution_convert_fusion = bf16[256,8,512]{2,0,1:T(8,128)(2,1)S(1)} fusion(bf16[8,512,1024]{2,1,0:T(8,128)(2,1)} %param.2, s32[256]{0:T(256)S(1)} %and_select_fusion, pred[256]{0:T(512)(128)(4,1)S(1)} %iota_compare_fusion), kind=kOutput, calls=%fused_computation.15 | convolution fusion | flops 2153250816 | bytes 10487040 | tf_op jit(solution)/shard_map/kt,srt->ksr/dot_general | solution.py:51
  16.4 2.5 %copy.8 = bf16[2,128,8,512]{3,2,0,1:T(8,128)(2,1)} copy(bf16[2,128,8,512]{3,1,0,2:T(8,128)(2,1)S(1)} %bitcast.53) | data formatting | bytes 4194304 | tf_op jit(solution)/shard_map/reshape | solution.py:54
  18.9 0.0 copy-start.2
  18.9 14.9 %all-to-all-start = ((bf16[2,128,8,512]{3,2,0,1:T(8,128)(2,1)}), bf16[2,128,8,512]{3,2,0,1:T(8,128)(2,1)S(1)}, u32[]{:S(2)}, u32[]{:S(2)}) async-start(bf16[2,128,8,512]{3,2,0,1:T(8,128)(2,1)} %copy.8), calls=%async_computation | async-start | bytes 4194304 | tf_op jit(solution)/shard_map/all_to_all | solution.py:55
  33.8 0.2 all-gather.2.cloned.1.call-start
  34.0 0.0 copy-done.2
  34.1 50.9 %all-to-all-done = bf16[2,128,8,512]{3,2,0,1:T(8,128)(2,1)S(1)} async-done(((bf16[2,128,8,512]{3,2,0,1:T(8,128)(2,1)}), bf16[2,128,8,512]{3,2,0,1:T(8,128)(2,1)S(1)}, u32[]{:S(2)}, u32[]{:S(2)}) %all-to-all-start) | async-done | bytes 2097184 | tf_op jit(solution)/shard_map/all_to_all | solution.py:55
  85.0 0.2 copy.14
  85.1 2.2 copy.10
  87.3 10.9 %gather_fusion = bf16[1024,2,512]{2,1,0:T(2,128)(2,1)} fusion(bf16[2,1024,512]{2,0,1:T(2,128)(2,1)S(1)} %copy.10, s32[1024]{0:T(1024)S(1)} %fusion.22), kind=kCustom, calls=%fused_computation | custom fusion | bytes 4198400 | tf_op jit(solution)/shard_map/jit(_take)/gather | solution.py:56
  98.2 6.2 %copy.11 = bf16[1024,2,512]{0,2,1:T(8,128)(2,1)} copy(bf16[1024,2,512]{2,1,0:T(2,128)(2,1)} %gather_fusion) | data formatting | bytes 4194304 | tf_op jit(solution)/shard_map/jit(_take)/gather | solution.py:56
  104.5 1.8 bitcast_select_fusion
  106.3 1.1 constant_dynamic-slice_fusion
  107.3 2.6 %collective-permute-start = (bf16[2,1,512,512]{2,3,1,0:T(8,128)(2,1)}, bf16[2,1,512,512]{2,3,1,0:T(8,128)(2,1)S(1)}, u32[]{:S(2)}, u32[]{:S(2)}) collective-permute-start(bf16[2,1,512,512]{2,3,1,0:T(8,128)(2,1)} %constant_dynamic-slice_fusion), channel_id=1, source_target_pairs={{0,1},{1,0},{2,3},{3,2},{4,5},{5,4},{6,7},{7,6},{8,9},{9,8},{10,11... | collective-permute-start | bytes 3145736 | tf_op jit(solution)/shard_map/ppermute | solution.py:10
  110.0 3.0 %copy.12 = f32[2,1,1024,512]{3,2,1,0:T(8,128)} copy(bf16[2,1,1024,512]{2,3,1,0:T(8,128)(2,1)S(1)} %bitcast_select_fusion) | data formatting | bytes 6291456 | tf_op jit(solution)/shard_map/convert_element_type | solution.py:44
  112.9 0.0 copy-start.1
  112.9 20.4 %collective-permute-done = bf16[2,1,512,512]{2,3,1,0:T(8,128)(2,1)S(1)} collective-permute-done((bf16[2,1,512,512]{2,3,1,0:T(8,128)(2,1)}, bf16[2,1,512,512]{2,3,1,0:T(8,128)(2,1)S(1)}, u32[]{:S(2)}, u32[]{:S(2)}) %collective-permute-start) | collective-permute-done | bytes 1048608 | tf_op jit(solution)/shard_map/ppermute | solution.py:10
  133.4 0.5 select_bitcast_fusion.1
  133.9 0.0 copy-done.1
  133.9 2.1 multiply_convert_fusion
  136.0 0.0 copy-start
  136.0 0.0 all-gather.2.cloned.1.call-update
  136.0 60.8 %all-gather.2.cloned.1.call-done = bf16[2,1,1024,1024]{3,2,1,0:T(8,128)(2,1)} async-done(((bf16[2,1,1024,512]{3,2,1,0:T(8,128)(2,1)}), bf16[2,1,1024,1024]{3,2,1,0:T(8,128)(2,1)}) %all-gather.2.cloned.1.call-update) | async-done | bytes 4194320 | tf_op jit(solution)/shard_map/all_gather | solution.py:65
  196.7 0.0 copy-done
  196.8 0.0 copy-start.3
  196.8 3.0 %fusion.5 = f32[1024,512]{1,0:T(8,128)S(1)} fusion(bf16[2,1,1024,1024]{3,2,1,0:T(8,128)(2,1)} %all-gather.2.cloned.1.call-done, bf16[2,1,1024,512]{3,2,1,0:T(8,128)(2,1)S(1)} %copy-done), kind=kOutput, calls=%fused_computation.21 | convolution fusion | flops 1073741824 | bytes 5242880 | tf_op jit(solution)/shard_map/fnk,fkh->fnh/dot_general | solution.py:24
  199.7 0.0 copy-done.3
  199.8 1.2 fusion.6
  201.0 1.2 add_bitcast_fusion.1
  202.2 1.2 subtract_bitcast_fusion.1
  203.5 0.6 fusion
  204.1 1.2 fusion.4
  205.3 1.3 fusion.3
  206.6 1.2 subtract_bitcast_fusion
  207.8 1.3 add_bitcast_fusion
  209.1 2.3 %fusion.2 = bf16[2,1,1024,512]{3,2,1,0:T(8,128)(2,1)} fusion(f32[1,1,1024,512]{3,2,1,0:T(8,128)S(1)} %add_bitcast_fusion, f32[1,1,1024,512]{3,2,1,0:T(8,128)S(1)} %subtract_bitcast_fusion, bf16[2,1,1024,512]{3,2,1,0:T(8,128)(2,1)S(1)} %copy-done, f32[1,1,1024,512]{3,2,1,0:T(8,128)S(1)} %add_bitcast_fusion.1, f32[1,1,1024,512]{3,2,1,0:T(8,128)S(1)} %subtract_bitcast_fusion.1), kind=kLoop, calls=%fused_computation.5 | loop fusion | flops 10485760 | bytes 12582912 | tf_op jit(solution)/shard_map/convert_element_type | solution.py:69
  (4 shorter events, 0.0 us)
Async XLA Ops:
  18.9 15.1 %copy-start.2 = (s32[1024]{0:T(1024)S(1)}, s32[1024]{0:T(1024)}, u32[]{:S(2)}) copy-start(s32[1024]{0:T(1024)} %param.3) | copy-start | bytes 12292
  18.9 66.1 %all-to-all-start = ((bf16[2,128,8,512]{3,2,0,1:T(8,128)(2,1)}), bf16[2,128,8,512]{3,2,0,1:T(8,128)(2,1)S(1)}, u32[]{:S(2)}, u32[]{:S(2)}) async-start(bf16[2,128,8,512]{3,2,0,1:T(8,128)(2,1)} %copy.8), calls=%async_computation | async-start | bytes 4194304 | tf_op jit(solution)/shard_map/all_to_all | solution.py:55
  33.8 163.0 %all-gather.2.cloned.1.call-start = ((), (), s32[]{:S(2)}) async-start(), calls=%async_computation.1 | async-start | bytes 6291456 | tf_op jit(solution)/shard_map/all_gather | solution.py:65
  107.3 26.0 %collective-permute-start = (bf16[2,1,512,512]{2,3,1,0:T(8,128)(2,1)}, bf16[2,1,512,512]{2,3,1,0:T(8,128)(2,1)S(1)}, u32[]{:S(2)}, u32[]{:S(2)}) collective-permute-start(bf16[2,1,512,512]{2,3,1,0:T(8,128)(2,1)} %constant_dynamic-slice_fusion), channel_id=1, source_target_pairs={{0,1},{1,0},{2,3},{3,2},{4,5},{5,4},{6,7},{7,6},{8,9},{9,8},{10,11... | collective-permute-start | bytes 3145736 | tf_op jit(solution)/shard_map/ppermute | solution.py:10
  112.9 20.9 %copy-start.1 = (f32[2,1,1024,512]{3,2,1,0:T(8,128)S(1)}, f32[2,1,1024,512]{3,2,1,0:T(8,128)}, u32[]{:S(2)}) copy-start(f32[2,1,1024,512]{3,2,1,0:T(8,128)} %copy.12) | copy-start | bytes 12582916
  136.0 60.8 %copy-start = (bf16[2,1,1024,512]{3,2,1,0:T(8,128)(2,1)S(1)}, bf16[2,1,1024,512]{3,2,1,0:T(8,128)(2,1)}, u32[]{:S(2)}) copy-start(bf16[2,1,1024,512]{3,2,1,0:T(8,128)(2,1)} %multiply_convert_fusion) | copy-start | bytes 6291460
  196.8 3.0 %copy-start.3 = (bf16[2,1,1024,1024]{3,2,1,0:T(8,128)(2,1)S(1)}, bf16[2,1,1024,1024]{3,2,1,0:T(8,128)(2,1)}, u32[]{:S(2)}) copy-start(bf16[2,1,1024,1024]{3,2,1,0:T(8,128)(2,1)} %all-gather.2.cloned.1.call-done) | copy-start | bytes 12582916
Sparse Core Ops, SparseCore 0:
  136.1 60.5 all-gather.1
where the time goes:
time: 219 us; the launch traced here: 218 us
  waiting for transfers between devices  132 us (60%)
  local copies, waits for them, and re-layouts  26 us (12%)
  matrix products  21.6 us (10%)
  starting transfers between devices  17.7 us (8%)
  between operations  13.5 us (6%)
  other arithmetic  7.23 us (3%)
    all_gather x1, waiting for transfers between devices, shards(): whole = lax.all_gather(spectral, 'col', axis=3, tiled=True)  60.8 us
    all_to_all x1, waiting for transfers between devices, shards(): lax.all_to_all(spectrum, 'freq', split_axis=1, concat_axis=2, tiled=True)  50.9 us
    ppermute x1, waiting for transfers between devices, partner(): lax.ppermute(value, axis, [(i, i ^ 1 << bit) for i in range(lax.axis_size...  20.4 us
    gather x2, local copies, waits for them, and re-layouts, shards(): arranged = jnp.take(acquired, source_row, axis=2)  17.1 us
    all_to_all x1, starting transfers between devices, shards(): lax.all_to_all(spectrum, 'freq', split_axis=1, concat_axis=2, tiled=True)  14.9 us
    dot_general x8, matrix products, single_product(): jnp.einsum('fnk,fkh->fnh', first, second, preferred_element_type=jnp.floa...  11.7 us
    dot_general x1, matrix products, shards(): jnp.einsum('kt,srt->ksr', table, traces, preferred_element_type=jnp.float32)  9.83 us
  transfers between devices with their start and end apart: 3, of which 3 were waited for; matrix products, arithmetic and copies ran while one was open for 1% of the time, Pallas kernels for 0%

commit v1 on v0

v1 whole, which is shorter than its diff:
```python
import functools
import math

import jax
import jax.numpy as jnp
from jax import lax
from jax.experimental import pallas as pl
from jax.experimental.pallas import tpu as pltpu
from jax.sharding import PartitionSpec as P

BF16 = jnp.bfloat16
F32 = jnp.float32
VMEM = pl.BlockSpec(memory_space=pltpu.VMEM)
SMEM = pl.BlockSpec(memory_space=pltpu.SMEM)


def partner(value):
    return lax.ppermute(value, "col", [(0, 1), (1, 0)])


def dft_table(samples, kept):
    row_index = jnp.arange(2 * kept)
    frequency = (row_index % kept)[:, None]
    sample_index = jnp.arange(samples)[None, :]
    phase = frequency * sample_index % samples
    angle = 2.0 * math.pi / samples * phase.astype(F32)
    table = jnp.where(row_index[:, None] < kept, jnp.cos(angle), -jnp.sin(angle))
    return (table / jnp.sqrt(jnp.float32(samples))).astype(BF16)


def dot(a, b, dims=((1,), (0,))):
    return lax.dot_general(a, b, (dims, ((), ())), preferred_element_type=F32)


NT = ((1,), (1,))


def dft_kernel(table_ref, traces_ref, out_ref, stage_ref):
    sources = traces_ref.shape[0]
    rows = table_ref.shape[0]
    for s in range(sources):
        stage_ref[pl.ds(s, rows, stride=sources), :] = dot(table_ref[...], traces_ref[s], NT)
    out_ref[...] = stage_ref[...].reshape(rows, sources, traces_ref.shape[1]).astype(BF16)


def dft(table, traces):
    rows, samples = table.shape
    sources, receivers, _ = traces.shape
    width = 128
    return pl.pallas_call(
        dft_kernel,
        grid=(receivers // width,),
        in_specs=[
            pl.BlockSpec((rows, samples), lambda j: (0, 0)),
            pl.BlockSpec((sources, width, samples), lambda j: (0, j, 0)),
        ],
        out_specs=pl.BlockSpec((rows, sources, width), lambda j: (0, 0, j)),
        out_shape=jax.ShapeDtypeStruct((rows, sources, receivers), BF16),
        scratch_shapes=[pltpu.VMEM((rows * sources, width), F32)],
        cost_estimate=pl.CostEstimate(
            flops=2 * rows * samples * sources * receivers,
            bytes_accessed=2 * (sources * receivers * samples + rows * samples + rows * sources * receivers),
            transcendentals=0,
        ),
    )(table, traces)


def arrange_kernel(pick_ref, piece_ref, own_ref, off_ref):
    owners, sources, width = piece_ref.shape
    size = owners * sources
    half = size // 2
    rows = piece_ref[...].astype(F32).reshape(size, width).astype(BF16)
    off_ref[...] = dot(pick_ref[half:, :], rows).astype(BF16)
    block = dot(pick_ref[:half, :], rows)
    eye = (
        lax.broadcasted_iota(jnp.int32, (half, half), 0) == lax.broadcasted_iota(jnp.int32, (half, half), 1)
    ).astype(BF16)
    own_ref[...] = ((block + dot(eye, block.astype(BF16), NT)) * 0.5).astype(BF16)


def arrange(pick, piece):
    owners, sources, width = piece.shape
    half = owners * sources // 2
    shape = jax.ShapeDtypeStruct((half, width), BF16)
    return pl.pallas_call(
        arrange_kernel,
        in_specs=[VMEM, VMEM],
        out_specs=[VMEM, VMEM],
        out_shape=[shape, shape],
        cost_estimate=pl.CostEstimate(flops=4 * half * 2 * half * width, bytes_accessed=12 * half * width, transcendentals=0),
    )(pick, piece)


def predict_kernel(
    scale, col_ref, own_r, own_i, off_r, off_i, their_off_r, their_off_i, their_own_r, their_own_i, out_ref, left_ref, right_ref, square_ref
):
    half = own_r.shape[0]
    size = 2 * half
    eye = (
        lax.broadcasted_iota(jnp.int32, (half, half), 0) == lax.broadcasted_iota(jnp.int32, (half, half), 1)
    ).astype(BF16)
    parts = ((own_r, off_r, their_off_r, their_own_r), (own_i, off_i, their_off_i, their_own_i))
    for part, (own, off, their_off, their_own) in enumerate(parts):
        lower = ((off[...].astype(F32) + dot(eye, their_off[...], NT)) * 0.5).astype(BF16)
        upper = ((their_off[...].astype(F32) + dot(eye, off[...], NT)) * 0.5).astype(BF16)
        at = part * size
        left_ref[:half, at : at + half] = own[...]
        left_ref[half:, at : at + half] = lower
        left_ref[:half, at + half : at + size] = upper
        left_ref[half:, at + half : at + size] = their_own[...]
        cols = slice(part * half, (part + 1) * half)
        right_ref[:half, cols] = own[...]
        right_ref[half:size, cols] = lower
        if part == 0:
            right_ref[size : size + half, half:] = own[...]
            right_ref[size + half :, half:] = lower
        else:
            right_ref[size : size + half, :half] = -own[...]
            right_ref[size + half :, :half] = -lower
    for at in range(0, size, half):
        product = (scale * dot(left_ref[at : at + half, :], right_ref[...])).astype(BF16)
        square_ref[at : at + half, :] = product
        square_ref[size + at : size + at + half, half:] = product[:, :half]
        square_ref[size + at : size + at + half, :half] = -product[:, half:]
    for number, at in enumerate((0, half)):
        product = scale * dot(left_ref[at : at + half, :], square_ref[...])
        whole = right_ref[at : at + half, :].astype(F32) - square_ref[at : at + half, :].astype(F32) + product
        whole = whole.astype(BF16)
        row = pl.multiple_of((col_ref[0] ^ number) * half, half)
        out_ref[0, 0, pl.ds(row, half), :] = whole[:, :half]
        out_ref[1, 0, pl.ds(row, half), :] = whole[:, half:]


def predict(column_half, *blocks):
    half, width = blocks[0].shape
    size = 2 * half
    return pl.pallas_call(
        functools.partial(predict_kernel, 1.0 / math.sqrt(size)),
        in_specs=[SMEM] + [VMEM] * len(blocks),
        out_specs=VMEM,
        out_shape=jax.ShapeDtypeStruct((2, 1, size, width), BF16),
        scratch_shapes=[
            pltpu.VMEM((size, 2 * size), BF16),
            pltpu.VMEM((2 * size, 2 * width), BF16),
            pltpu.VMEM((2 * size, 2 * width), BF16),
        ],
        cost_estimate=pl.CostEstimate(flops=16 * size * size * width, bytes_accessed=12 * size * width, transcendentals=0),
    )(jnp.full((1,), column_half, jnp.int32), *blocks)


def shards(traces, source_row):
    sources, receivers, samples = traces.shape
    kept = samples // 8
    size = source_row.shape[0]
    table = dft_table(samples, kept)
    column_half = lax.axis_index("col")
    order = jnp.roll(source_row, -column_half * (size // 2))
    pick = (order[:, None] == jnp.arange(size)[None, :]).astype(BF16)
    own, off = [], []
    for part in range(2):
        piece = dft(table[part * kept : (part + 1) * kept], traces)
        piece = lax.all_to_all(piece, "freq", split_axis=0, concat_axis=0, tiled=True)
        block, rest = arrange(pick, piece)
        own.append(block)
        off.append(rest)
    their_off = [partner(value) for value in off]
    their_own = [partner(value) for value in own]
    return predict(column_half, *own, *off, *their_off, *their_own)


def solution(mesh):
    in_specs = (P("freq", "col", None), P())
    out_specs = P(None, "freq", None, "col")
    return jax.shard_map(shards, mesh=mesh, in_specs=in_specs, out_specs=out_specs, check_vma=False)
```

time: 219 us -> 141 us (0.64)
  waiting for transfers between devices: 132 us -> 68.5 us
  Pallas kernels: 0 us -> 35.1 us
  local copies, waits for them, and re-layouts: 26 us -> 2.63 us
  matrix products: 21.6 us -> 0 us
  between operations: 13.5 us -> 0.09 us
  starting transfers between devices: 17.7 us -> 27.9 us
    all_gather x1 -> x0, waiting for transfers between devices: 60.8 us -> none  [shards(): whole = lax.all_gather(spectral, 'col', axis=3, tiled=True)]
    pallas_call x0 -> x5, Pallas kernels: none -> 35.1 us  [the longest x1 13.6 us: predict(): pl.pallas_call(functools.partial(predict_kernel, 1.0 / math.sqrt(size)),...]
    dot_general x9 -> x0, matrix products: 21.6 us -> none  [the longest x8 11.7 us: single_product(): jnp.einsum('fnk,fkh->fnh', first, second, preferred_element_type=jnp.floa...]
    gather x2 -> x0, local copies, waits for them, and re-layouts: 17.1 us -> none  [shards(): arranged = jnp.take(acquired, source_row, axis=2)]
    all_to_all x1 -> x2, waiting for transfers between devices: 50.9 us -> 42 us  [shards(): lax.all_to_all(piece, 'freq', split_axis=0, concat_axis=0, tiled=True)]
    all_to_all x1 -> x2, starting transfers between devices: 14.9 us -> 22 us  [shards(): lax.all_to_all(piece, 'freq', split_axis=0, concat_axis=0, tiled=True)]
    ppermute x1 -> x4, waiting for transfers between devices: 20.4 us -> 26.4 us  [partner(): return lax.ppermute(value, 'col', [(0, 1), (1, 0)])]
    ppermute x1 -> x4, starting transfers between devices: 2.62 us -> 5.94 us  [partner(): return lax.ppermute(value, 'col', [(0, 1), (1, 0)])]
  transfers between devices with their start and end apart: 3 -> 6, of which waited for: 3 -> 5; matrix products, arithmetic and copies ran while one was open for 1% -> 1% of each run, Pallas kernels for 0% -> 11%
where the time goes in v1:
time: 141 us
  waiting for transfers between devices  68.5 us (49%)
  Pallas kernels  35.1 us (25%)
  starting transfers between devices  27.9 us (20%)
  other arithmetic  6.75 us (5%)
  local copies, waits for them, and re-layouts  2.63 us (2%)
    all_to_all x2, waiting for transfers between devices, shards(): lax.all_to_all(piece, 'freq', split_axis=0, concat_axis=0, tiled=True)  42 us
    ppermute x4, waiting for transfers between devices, partner(): return lax.ppermute(value, 'col', [(0, 1), (1, 0)])  26.4 us
    all_to_all x2, starting transfers between devices, shards(): lax.all_to_all(piece, 'freq', split_axis=0, concat_axis=0, tiled=True)  22 us
    pallas_call x1, Pallas kernels, predict(): pl.pallas_call(functools.partial(predict_kernel, 1.0 / math.sqrt(size)),...  13.6 us
    pallas_call x2, Pallas kernels, dft(): pl.pallas_call(dft_kernel, grid=(receivers // width,), in_specs=[pl.Block...  12.8 us
    pallas_call x2, Pallas kernels, arrange(): pl.pallas_call(arrange_kernel, in_specs=[VMEM, VMEM], out_specs=[VMEM, VM...  8.65 us
    ppermute x4, starting transfers between devices, partner(): return lax.ppermute(value, 'col', [(0, 1), (1, 0)])  5.94 us
    convert_element_type x1, other arithmetic, dft_table(): return (table / jnp.sqrt(jnp.float32(samples))).astype(BF16)  4.93 us
  transfers between devices with their start and end apart: 6, of which 5 were waited for; matrix products, arithmetic and copies ran while one was open for 1% of the time, Pallas kernels for 11%

profile of v1, /device:TPU:1, one launch (start us, length us, event | category | flops | bytes accessed | tf_op | source)
XLA Modules:
  0.0 140.9 jit_solution(9764543160774192)
XLA Ops:
  0.0 4.9 %multiply_convert_fusion = bf16[256,1024]{1,0:T(8,128)(2,1)S(1)} fusion(s32[256]{0:T(256)S(1)} %and_select_fusion, pred[256]{0:T(512)(128)(4,1)S(1)} %iota_compare_fusion.1), kind=kLoop, calls=%fused_computation.8 | loop fusion | flops 4718592 | bytes 525568 | tf_op jit(solution)/shard_map/convert_element_type | solution.py:28
  5.0 0.8 fusion.8
  5.8 6.4 %shard_map.30 = bf16[128,8,512]{2,1,0:T(8,128)(2,1)} custom-call(bf16[128,1024]{1,0:T(8,128)(2,1)} %get-tuple-element.13.table_ref, bf16[8,512,1024]{2,1,0:T(8,128)(2,1)} %traces_ref.3), custom_call_target="tpu_custom_call" | custom-call | flops 1073741824 | bytes 9699328 | tf_op jit(solution)/shard_map/pallas_call | solution.py:50
  12.2 14.8 %all-to-all-start.1 = ((bf16[128,8,512]{2,1,0:T(8,128)(2,1)}), bf16[128,8,512]{2,1,0:T(8,128)(2,1)S(1)}, u32[]{:S(2)}, u32[]{:S(2)}) async-start(bf16[128,8,512]{2,1,0:T(8,128)(2,1)} %shard_map.30), calls=%async_computation.1 | async-start | bytes 2097152 | tf_op jit(solution)/shard_map/all_to_all | solution.py:162
  26.9 0.0 copy-start.2
  26.9 6.4 %shard_map.28 = bf16[128,8,512]{2,1,0:T(8,128)(2,1)} custom-call(bf16[128,1024]{1,0:T(8,128)(2,1)} %get-tuple-element.14.table_ref, bf16[8,512,1024]{2,1,0:T(8,128)(2,1)} %traces_ref.3), custom_call_target="tpu_custom_call" | custom-call | flops 1073741824 | bytes 9699328 | tf_op jit(solution)/shard_map/pallas_call | solution.py:50
  33.4 22.4 %all-to-all-done.1.piece_ref = bf16[128,8,512]{2,1,0:T(8,128)(2,1)S(1)} async-done(((bf16[128,8,512]{2,1,0:T(8,128)(2,1)}), bf16[128,8,512]{2,1,0:T(8,128)(2,1)S(1)}, u32[]{:S(2)}, u32[]{:S(2)}) %all-to-all-start.1) | async-done | bytes 1048608 | tf_op jit(solution)/shard_map/all_to_all | solution.py:162
  55.7 0.0 copy-start.1
  55.7 7.2 %all-to-all-start = ((bf16[128,8,512]{2,1,0:T(8,128)(2,1)}), bf16[128,8,512]{2,1,0:T(8,128)(2,1)S(1)}, u32[]{:S(2)}, u32[]{:S(2)}) async-start(bf16[128,8,512]{2,1,0:T(8,128)(2,1)} %shard_map.28), calls=%async_computation | async-start | bytes 2097152 | tf_op jit(solution)/shard_map/all_to_all | solution.py:162
  63.0 0.0 copy-done.2
  63.0 0.1 fusion.7
  63.1 1.7 %fusion.pick_ref = bf16[1024,1024]{1,0:T(8,128)(2,1)} fusion(s32[1024]{0:T(1024)S(1)} %fusion.7), kind=kLoop, calls=%fused_computation.1 | loop fusion | flops 2097152 | bytes 2101248 | tf_op jit(solution)/shard_map/convert_element_type | solution.py:158
  64.8 0.0 copy-done.1
  64.8 4.3 %shard_map.31 = (bf16[512,512]{1,0:T(8,128)(2,1)}, bf16[512,512]{1,0:T(8,128)(2,1)}) custom-call(bf16[1024,1024]{1,0:T(8,128)(2,1)} %fusion.pick_ref, bf16[128,8,512]{2,1,0:T(8,128)(2,1)} %copy-done.1), custom_call_target="tpu_custom_call" | custom-call | flops 1073741824 | bytes 3145728 | tf_op jit(solution)/shard_map/pallas_call | solution.py:85
  69.1 2.6 %collective-permute-start.3 = (bf16[512,512]{1,0:T(8,128)(2,1)}, bf16[512,512]{1,0:T(8,128)(2,1)S(1)}, u32[]{:S(2)}, u32[]{:S(2)}) collective-permute-start(bf16[512,512]{1,0:T(8,128)(2,1)} %get-tuple-element.10.own_i), channel_id=1, source_target_pairs={{0,1},{1,0},{2,3},{3,2},{4,5},{5,4},{6,7},{7,6},{8,9},{9,8},{10,11... | collective-permute-start | bytes 1572872 | tf_op jit(solution)/shard_map/ppermute | solution.py:18
  71.8 0.3 collective-permute-start.1
  72.1 19.6 %all-to-all-done.piece_ref = bf16[128,8,512]{2,1,0:T(8,128)(2,1)S(1)} async-done(((bf16[128,8,512]{2,1,0:T(8,128)(2,1)}), bf16[128,8,512]{2,1,0:T(8,128)(2,1)S(1)}, u32[]{:S(2)}, u32[]{:S(2)}) %all-to-all-start) | async-done | bytes 1048608 | tf_op jit(solution)/shard_map/all_to_all | solution.py:162
  91.7 0.0 copy-start
  91.7 1.0 copy-done
  92.7 4.3 %shard_map.29 = (bf16[512,512]{1,0:T(8,128)(2,1)}, bf16[512,512]{1,0:T(8,128)(2,1)}) custom-call(bf16[1024,1024]{1,0:T(8,128)(2,1)} %fusion.pick_ref, bf16[128,8,512]{2,1,0:T(8,128)(2,1)} %copy-done), custom_call_target="tpu_custom_call" | custom-call | flops 1073741824 | bytes 3145728 | tf_op jit(solution)/shard_map/pallas_call | solution.py:85
  97.1 2.6 %collective-permute-start.2 = (bf16[512,512]{1,0:T(8,128)(2,1)}, bf16[512,512]{1,0:T(8,128)(2,1)S(1)}, u32[]{:S(2)}, u32[]{:S(2)}) collective-permute-start(bf16[512,512]{1,0:T(8,128)(2,1)} %get-tuple-element.9.own_r), channel_id=1, source_target_pairs={{0,1},{1,0},{2,3},{3,2},{4,5},{5,4},{6,7},{7,6},{8,9},{9,8},{10,11... | collective-permute-start | bytes 1572872 | tf_op jit(solution)/shard_map/ppermute | solution.py:18
  99.7 0.3 collective-permute-start
  100.0 0.0 collective-permute-done.3.their_own_i
  100.0 0.0 copy-start.3
  100.0 4.0 %collective-permute-done.1.their_off_i = bf16[512,512]{1,0:T(8,128)(2,1)S(1)} collective-permute-done((bf16[512,512]{1,0:T(8,128)(2,1)}, bf16[512,512]{1,0:T(8,128)(2,1)S(1)}, u32[]{:S(2)}, u32[]{:S(2)}) %collective-permute-start.1) | collective-permute-done | bytes 524320 | tf_op jit(solution)/shard_map/ppermute | solution.py:18
  104.0 0.0 copy-start.4
  104.0 11.2 %collective-permute-done.2.their_own_r = bf16[512,512]{1,0:T(8,128)(2,1)S(1)} collective-permute-done((bf16[512,512]{1,0:T(8,128)(2,1)}, bf16[512,512]{1,0:T(8,128)(2,1)S(1)}, u32[]{:S(2)}, u32[]{:S(2)}) %collective-permute-start.2) | collective-permute-done | bytes 524320 | tf_op jit(solution)/shard_map/ppermute | solution.py:18
  115.2 0.0 copy-start.5
  115.2 11.2 %collective-permute-done.their_off_r = bf16[512,512]{1,0:T(8,128)(2,1)S(1)} collective-permute-done((bf16[512,512]{1,0:T(8,128)(2,1)}, bf16[512,512]{1,0:T(8,128)(2,1)S(1)}, u32[]{:S(2)}, u32[]{:S(2)}) %collective-permute-start) | collective-permute-done | bytes 524320 | tf_op jit(solution)/shard_map/ppermute | solution.py:18
  126.5 0.0 copy-start.6
  126.5 0.0 copy-done.3
  126.5 0.0 copy-done.4
  126.5 0.0 copy-done.5
  126.5 0.8 copy-done.6
  127.3 13.6 %shard_map.32 = bf16[2,1,1024,512]{3,2,1,0:T(8,128)(2,1)} custom-call(s32[1]{0:T(128)} %bitcast.col_ref, bf16[512,512]{1,0:T(8,128)(2,1)} %get-tuple-element.9.own_r, bf16[512,512]{1,0:T(8,128)(2,1)} %get-tuple-element.10.own_i, bf16[512,512]{1,0:T(8,128)(2,1)} %get-tuple-element.11.off_r, bf16[512,512]{1,0:T(8,128)(2,1)} %get-tuple-element.12.off_i, ...), custom_call_target="tpu_custom_call" | custom-call | flops 8589934592 | bytes 6291456 | tf_op jit(solution)/shard_map/pallas_call | solution.py:137
  (2 shorter events, 0.0 us)
Async XLA Ops:
  12.2 43.6 %all-to-all-start.1 = ((bf16[128,8,512]{2,1,0:T(8,128)(2,1)}), bf16[128,8,512]{2,1,0:T(8,128)(2,1)S(1)}, u32[]{:S(2)}, u32[]{:S(2)}) async-start(bf16[128,8,512]{2,1,0:T(8,128)(2,1)} %shard_map.30), calls=%async_computation.1 | async-start | bytes 2097152 | tf_op jit(solution)/shard_map/all_to_all | solution.py:162
  26.9 36.0 %copy-start.2 = (s32[1024]{0:T(1024)S(1)}, s32[1024]{0:T(1024)}, u32[]{:S(2)}) copy-start(s32[1024]{0:T(1024)} %param.3) | copy-start | bytes 12292
  55.7 9.1 %copy-start.1 = (bf16[128,8,512]{2,1,0:T(8,128)(2,1)}, bf16[128,8,512]{2,1,0:T(8,128)(2,1)S(1)}, u32[]{:S(2)}) copy-start(bf16[128,8,512]{2,1,0:T(8,128)(2,1)S(1)} %all-to-all-done.1.piece_ref) | copy-start | bytes 3145732
  55.7 36.0 %all-to-all-start = ((bf16[128,8,512]{2,1,0:T(8,128)(2,1)}), bf16[128,8,512]{2,1,0:T(8,128)(2,1)S(1)}, u32[]{:S(2)}, u32[]{:S(2)}) async-start(bf16[128,8,512]{2,1,0:T(8,128)(2,1)} %shard_map.28), calls=%async_computation | async-start | bytes 2097152 | tf_op jit(solution)/shard_map/all_to_all | solution.py:162
  69.1 30.9 %collective-permute-start.3 = (bf16[512,512]{1,0:T(8,128)(2,1)}, bf16[512,512]{1,0:T(8,128)(2,1)S(1)}, u32[]{:S(2)}, u32[]{:S(2)}) collective-permute-start(bf16[512,512]{1,0:T(8,128)(2,1)} %get-tuple-element.10.own_i), channel_id=1, source_target_pairs={{0,1},{1,0},{2,3},{3,2},{4,5},{5,4},{6,7},{7,6},{8,9},{9,8},{10,11... | collective-permute-start | bytes 1572872 | tf_op jit(solution)/shard_map/ppermute | solution.py:18
  71.8 32.2 %collective-permute-start.1 = (bf16[512,512]{1,0:T(8,128)(2,1)}, bf16[512,512]{1,0:T(8,128)(2,1)S(1)}, u32[]{:S(2)}, u32[]{:S(2)}) collective-permute-start(bf16[512,512]{1,0:T(8,128)(2,1)} %get-tuple-element.12.off_i), channel_id=1, source_target_pairs={{0,1},{1,0},{2,3},{3,2},{4,5},{5,4},{6,7},{7,6},{8,9},{9,8},{10,11... | collective-permute-start | bytes 1572872 | tf_op jit(solution)/shard_map/ppermute | solution.py:18
  91.7 1.0 copy-start
  97.1 18.2 %collective-permute-start.2 = (bf16[512,512]{1,0:T(8,128)(2,1)}, bf16[512,512]{1,0:T(8,128)(2,1)S(1)}, u32[]{:S(2)}, u32[]{:S(2)}) collective-permute-start(bf16[512,512]{1,0:T(8,128)(2,1)} %get-tuple-element.9.own_r), channel_id=1, source_target_pairs={{0,1},{1,0},{2,3},{3,2},{4,5},{5,4},{6,7},{7,6},{8,9},{9,8},{10,11... | collective-permute-start | bytes 1572872 | tf_op jit(solution)/shard_map/ppermute | solution.py:18
  99.7 26.8 %collective-permute-start = (bf16[512,512]{1,0:T(8,128)(2,1)}, bf16[512,512]{1,0:T(8,128)(2,1)S(1)}, u32[]{:S(2)}, u32[]{:S(2)}) collective-permute-start(bf16[512,512]{1,0:T(8,128)(2,1)} %get-tuple-element.11.off_r), channel_id=1, source_target_pairs={{0,1},{1,0},{2,3},{3,2},{4,5},{5,4},{6,7},{7,6},{8,9},{9,8},{10,11... | collective-permute-start | bytes 1572872 | tf_op jit(solution)/shard_map/ppermute | solution.py:18
  100.0 26.5 %copy-start.3 = (bf16[512,512]{1,0:T(8,128)(2,1)}, bf16[512,512]{1,0:T(8,128)(2,1)S(1)}, u32[]{:S(2)}) copy-start(bf16[512,512]{1,0:T(8,128)(2,1)S(1)} %collective-permute-done.3.their_own_i) | copy-start | bytes 1572868
  104.0 22.5 %copy-start.4 = (bf16[512,512]{1,0:T(8,128)(2,1)}, bf16[512,512]{1,0:T(8,128)(2,1)S(1)}, u32[]{:S(2)}) copy-start(bf16[512,512]{1,0:T(8,128)(2,1)S(1)} %collective-permute-done.1.their_off_i) | copy-start | bytes 1572868
  115.2 11.2 %copy-start.5 = (bf16[512,512]{1,0:T(8,128)(2,1)}, bf16[512,512]{1,0:T(8,128)(2,1)S(1)}, u32[]{:S(2)}) copy-start(bf16[512,512]{1,0:T(8,128)(2,1)S(1)} %collective-permute-done.2.their_own_r) | copy-start | bytes 1572868
  126.5 0.8 copy-start.6

commit v2 on v0

v2 whole, which is shorter than its diff:
```python
import functools
import math

import jax
import jax.numpy as jnp
import numpy as np
from jax import lax
from jax.experimental import pallas as pl
from jax.experimental.pallas import tpu as pltpu
from jax.sharding import PartitionSpec as P

BF16 = jnp.bfloat16
F32 = jnp.float32
VMEM = pl.BlockSpec(memory_space=pltpu.VMEM)
SMEM = pl.BlockSpec(memory_space=pltpu.SMEM)
NT = ((1,), (1,))
PAD = 16


def partner(value):
    return lax.ppermute(value, "col", [(0, 1), (1, 0)])


def dft_table(samples, kept):
    phase = np.arange(kept)[:, None] * np.arange(samples)[None, :] % samples
    angle = np.float32(2.0 * math.pi / samples) * phase.astype(np.float32)
    table = np.stack([np.cos(angle), -np.sin(angle)], 1).reshape(2 * kept, samples)
    return jnp.asarray(table / np.sqrt(np.float32(samples)), dtype=BF16)


def dot(a, b, dims=((1,), (0,))):
    return lax.dot_general(a, b, (dims, ((), ())), preferred_element_type=F32)


def grid_of(size):
    return lax.broadcasted_iota(jnp.int32, (size, size), 0), lax.broadcasted_iota(jnp.int32, (size, size), 1)


def turn(block):
    row, col = grid_of(block.shape[0])
    return dot((row == col).astype(BF16), block, NT)


def call(kernel, out_shape, flops, moved, vmem_mib, **rest):
    return pl.pallas_call(
        kernel,
        out_shape=out_shape,
        cost_estimate=pl.CostEstimate(flops=flops, bytes_accessed=moved, transcendentals=0),
        compiler_params=pltpu.CompilerParams(vmem_limit_bytes=vmem_mib << 20),
        **rest,
    )


def dft_kernel(table_ref, traces_ref, out_ref, stage_ref):
    sources = traces_ref.shape[0]
    blocks, _, lanes = stage_ref.shape
    rows = table_ref.shape[0]
    for s in range(sources):
        value = dot(table_ref[...], traces_ref[s], NT)
        for b in range(blocks):
            stage_ref.at[b][pl.ds(s, rows, stride=sources), :] = value[:, b * lanes : (b + 1) * lanes]
    for b in range(blocks):
        out_ref[:, :, b * lanes : (b + 1) * lanes] = stage_ref[b].reshape(rows, sources, lanes).astype(BF16)


def dft(table, traces):
    rows, samples = table.shape
    sources, receivers, _ = traces.shape
    width, lanes = 256, 128
    return call(
        dft_kernel,
        jax.ShapeDtypeStruct((rows, sources, receivers), BF16),
        2 * rows * samples * sources * receivers,
        2 * (sources * receivers * samples + rows * samples + rows * sources * receivers),
        60,
        grid=(receivers // width,),
        in_specs=[
            pl.BlockSpec((rows, samples), lambda j: (0, 0)),
            pl.BlockSpec((sources, width, samples), lambda j: (0, j, 0)),
        ],
        out_specs=pl.BlockSpec((rows, sources, width), lambda j: (0, 0, j)),
        scratch_shapes=[pltpu.VMEM((width // lanes, rows * sources, lanes), F32)],
    )(table, traces)


def rows_of(piece_ref, part):
    owners, _, sources, width = piece_ref.shape
    return piece_ref[:, part].astype(F32).reshape(owners * sources, width).astype(BF16)


def off_kernel(pick_ref, piece_ref, off_r, off_i):
    half = off_r.shape[0]
    for part, off in enumerate((off_r, off_i)):
        off[...] = dot(pick_ref[half:, :], rows_of(piece_ref, part)).astype(BF16)


def own_kernel(pick_ref, piece_ref, own_r, own_i, packed_ref):
    half = own_r.shape[0]
    for part, own in enumerate((own_r, own_i)):
        block = dot(pick_ref[:half, :], rows_of(piece_ref, part))
        own[...] = ((block + turn(block.astype(BF16))) * 0.5).astype(BF16)
    row, col = grid_of(half)
    real, imag = own_r[...].astype(F32), own_i[...].astype(F32)
    packed_ref[:half, :] = jnp.where(row >= col, real, imag).astype(BF16)
    diagonal = jnp.sum(jnp.where(row == col, imag, 0.0), axis=0, keepdims=True)
    packed_ref[half:, :] = jnp.broadcast_to(diagonal, (PAD, half)).astype(BF16)


def put_right(right_ref, real, imag):
    half = real.shape[0]
    right_ref[:half, :half] = real
    right_ref[:half, half:] = imag
    right_ref[half:, :half] = -imag
    right_ref[half:, half:] = real


def first_kernel(
    scale, own_r, own_i, off_r, off_i, their_r, their_i,
    right_low, upper_ref, square_own, part_other, cube_own, cube_other, left_own, left_low, right_own, right_square,
):
    half = own_r.shape[0]
    for part, (own, off, their) in enumerate(((own_r, off_r, their_r), (own_i, off_i, their_i))):
        cols = slice(part * half, (part + 1) * half)
        left_own[:, cols] = own[...]
        left_low[:, cols] = ((off[...].astype(F32) + turn(their[...])) * 0.5).astype(BF16)
        upper_ref[:, cols] = ((their[...].astype(F32) + turn(off[...])) * 0.5).astype(BF16)
    put_right(right_own, own_r[...], own_i[...])
    put_right(right_low, left_low[:, :half], left_low[:, half:])
    product = dot(left_own[...], right_own[...]) + dot(upper_ref[...], right_low[...])
    square_own[...] = (scale * product).astype(BF16)
    put_right(right_square, square_own[:, :half], square_own[:, half:])
    part_other[...] = dot(left_low[...], right_own[...])
    cube_own[...] = dot(left_own[...], right_square[...])
    cube_other[...] = dot(left_low[...], right_square[...])


def first(*blocks):
    half = blocks[0].shape[0]
    wide = jax.ShapeDtypeStruct((half, 2 * half), BF16)
    long = jax.ShapeDtypeStruct((half, 2 * half), F32)
    square = jax.ShapeDtypeStruct((2 * half, 2 * half), BF16)
    return call(
        functools.partial(first_kernel, 1.0 / math.sqrt(2 * half)),
        [square, wide, wide, long, long, long],
        40 * half**3,
        60 * half**2,
        32,
        in_specs=[VMEM] * 6,
        out_specs=[VMEM] * 6,
        scratch_shapes=[pltpu.VMEM((half, 2 * half), BF16)] * 2 + [pltpu.VMEM((2 * half, 2 * half), BF16)] * 2,
    )(*blocks)


def second_kernel(
    scale, col_ref, packed_ref, own_r, own_i, right_low, upper_ref, square_own, part_other, cube_own, cube_other,
    out_ref, left_other, right_square,
):
    half = own_r.shape[0]
    row, col = grid_of(half)
    packed = packed_ref[:half, :]
    turned, packed = turn(packed), packed.astype(F32)
    diagonal = packed_ref[half : half + 1, :].astype(F32)
    left_other[:, :half] = jnp.where(row >= col, packed, turned).astype(BF16)
    left_other[:, half:] = jnp.where(row < col, packed, jnp.where(row > col, turned, diagonal)).astype(BF16)
    square = (scale * (part_other[...] + dot(left_other[...], right_low[...]))).astype(BF16)
    put_right(right_square, square[:, :half], square[:, half:])
    mine = pl.multiple_of(col_ref[0] * half, half)
    other = pl.multiple_of((1 - col_ref[0]) * half, half)
    cube = scale * (cube_own[...] + dot(upper_ref[...], right_square[...]))
    for part, own in enumerate((own_r, own_i)):
        cols = slice(part * half, (part + 1) * half)
        whole = own[...].astype(F32) - square_own[:, cols].astype(F32) + cube[:, cols]
        out_ref[part, 0, pl.ds(mine, half), :] = whole.astype(BF16)
    cube = scale * (cube_other[...] + dot(left_other[...], right_square[...]))
    for part in range(2):
        cols = slice(part * half, (part + 1) * half)
        whole = right_low[:half, cols].astype(F32) - square[:, cols].astype(F32) + cube[:, cols]
        out_ref[part, 0, pl.ds(other, half), :] = whole.astype(BF16)


def second(column_half, *blocks):
    half = blocks[1].shape[0]
    return call(
        functools.partial(second_kernel, 1.0 / math.sqrt(2 * half)),
        jax.ShapeDtypeStruct((2, 1, 2 * half, half), BF16),
        24 * half**3,
        60 * half**2,
        32,
        in_specs=[SMEM] + [VMEM] * len(blocks),
        out_specs=VMEM,
        scratch_shapes=[pltpu.VMEM((half, 2 * half), BF16), pltpu.VMEM((2 * half, 2 * half), BF16)],
    )(jnp.full((1,), column_half, jnp.int32), *blocks)


def shards(traces, source_row):
    sources, receivers, samples = traces.shape
    kept = samples // 8
    size = source_row.shape[0]
    half = size // 2
    column_half = lax.axis_index("col")
    order = jnp.roll(source_row, -column_half * half)
    pick = (order[:, None] == jnp.arange(size)[None, :]).astype(BF16)
    piece = dft(dft_table(samples, kept), traces).reshape(kept, 2, sources, receivers)
    piece = lax.all_to_all(piece, "freq", split_axis=0, concat_axis=0, tiled=True)
    block = jax.ShapeDtypeStruct((half, half), BF16)
    flops = 4 * half * size * half
    off = call(off_kernel, [block] * 2, flops, 14 * half**2, 24, in_specs=[VMEM] * 2, out_specs=[VMEM] * 2)(pick, piece)
    packed = jax.ShapeDtypeStruct((half + PAD, half), BF16)
    *own, packed = call(own_kernel, [block, block, packed], flops, 14 * half**2, 24, in_specs=[VMEM] * 2, out_specs=[VMEM] * 3)(pick, piece)
    their_off = [partner(value) for value in off]
    their_packed = partner(packed)
    return second(column_half, their_packed, *own, *first(*own, *off, *their_off))


def solution(mesh):
    in_specs = (P("freq", "col", None), P())
    out_specs = P(None, "freq", None, "col")
    return jax.shard_map(shards, mesh=mesh, in_specs=in_specs, out_specs=out_specs, check_vma=False)
```

time: 219 us -> 118 us (0.54)
  waiting for transfers between devices: 132 us -> 72.1 us
  local copies, waits for them, and re-layouts: 26 us -> 1.59 us
  matrix products: 21.6 us -> 0 us
  Pallas kernels: 0 us -> 21.3 us
  between operations: 13.5 us -> 0.06 us
  other arithmetic: 7.23 us -> 1.81 us
  starting transfers between devices: 17.7 us -> 20.8 us
    all_gather x1 -> x0, waiting for transfers between devices: 60.8 us -> none  [shards(): whole = lax.all_gather(spectral, 'col', axis=3, tiled=True)]
    dot_general x9 -> x0, matrix products: 21.6 us -> none  [the longest x8 11.7 us: single_product(): jnp.einsum('fnk,fkh->fnh', first, second, preferred_element_type=jnp.floa...]
    pallas_call x0 -> x5, Pallas kernels: none -> 21.3 us  [the longest x1 6.77 us: first(): call(functools.partial(first_kernel, 1.0 / math.sqrt(2 * half)), [square,...]
    gather x2 -> x0, local copies, waits for them, and re-layouts: 17.1 us -> none  [shards(): arranged = jnp.take(acquired, source_row, axis=2)]
    ppermute x1 -> x3, starting transfers between devices: 2.62 us -> 5.94 us  [partner(): return lax.ppermute(value, 'col', [(0, 1), (1, 0)])]
    convert_element_type x3 -> x1, other arithmetic: 4.94 us -> 1.73 us  [shards(): pick = (order[:, None] == jnp.arange(size)[None, :]).astype(BF16)]
    convert_element_type x1 -> x0, local copies, waits for them, and re-layouts: 2.98 us -> none  [average(): first.astype(jnp.float32) + second.astype(jnp.float32)]
    reshape x1 -> x0, local copies, waits for them, and re-layouts: 2.49 us -> none  [shards(): spectrum = spectrum.reshape(2, kept, traces.shape[0], traces.shape[1])]
  transfers between devices with their start and end apart: 3 -> 4, of which waited for: 3 -> 4; matrix products, arithmetic and copies ran while one was open for 1% -> 2% of each run, Pallas kernels for 0% -> 7%
where the time goes in v2:
time: 118 us
  waiting for transfers between devices  72.1 us (61%)
  Pallas kernels  21.3 us (18%)
  starting transfers between devices  20.8 us (18%)
  other arithmetic  1.81 us (2%)
  local copies, waits for them, and re-layouts  1.59 us (1%)
    all_to_all x1, waiting for transfers between devices, shards(): lax.all_to_all(piece, 'freq', split_axis=0, concat_axis=0, tiled=True)  49.4 us
    ppermute x3, waiting for transfers between devices, partner(): return lax.ppermute(value, 'col', [(0, 1), (1, 0)])  22.8 us
    all_to_all x1, starting transfers between devices, shards(): lax.all_to_all(piece, 'freq', split_axis=0, concat_axis=0, tiled=True)  14.9 us
    pallas_call x1, Pallas kernels, first(): call(functools.partial(first_kernel, 1.0 / math.sqrt(2 * half)), [square,...  6.77 us
    pallas_call x1, Pallas kernels, dft(): call(dft_kernel, jax.ShapeDtypeStruct((rows, sources, receivers), BF16),...  6.22 us
    ppermute x3, starting transfers between devices, partner(): return lax.ppermute(value, 'col', [(0, 1), (1, 0)])  5.94 us
    pallas_call x1, Pallas kernels, second(): call(functools.partial(second_kernel, 1.0 / math.sqrt(2 * half)), jax.Sha...  5.08 us
  transfers between devices with their start and end apart: 4, of which 4 were waited for; matrix products, arithmetic and copies ran while one was open for 2% of the time, Pallas kernels for 7%

profile of v2, /device:TPU:1, one launch (start us, length us, event | category | flops | bytes accessed | tf_op | source)
XLA Modules:
  0.0 117.8 jit_solution(11041711111644759323)
XLA Ops:
  0.0 6.2 %shard_map.37 = bf16[256,8,512]{2,1,0:T(8,128)(2,1)} custom-call(bf16[256,1024]{1,0:T(8,128)(2,1)} %constant.30.clone.table_ref, bf16[8,512,1024]{2,1,0:T(8,128)(2,1)} %traces_ref.1), custom_call_target="tpu_custom_call" | custom-call | flops 2147483648 | bytes 11010048 | tf_op jit(solution)/shard_map/pallas_call | solution.py:70
  6.2 0.0 copy-start.1
  6.2 14.9 %all-to-all-start = ((bf16[128,2,8,512]{3,2,1,0:T(8,128)(2,1)}), bf16[128,2,8,512]{3,2,1,0:T(8,128)(2,1)S(1)}, u32[]{:S(2)}, u32[]{:S(2)}) async-start(bf16[128,2,8,512]{3,2,1,0:T(8,128)(2,1)} %bitcast.2), calls=%async_computation | async-start | bytes 4194304 | tf_op jit(solution)/shard_map/all_to_all | solution.py:204
  21.2 0.0 copy-done.1
  21.2 0.1 fusion.1
  21.3 1.7 %fusion.pick_ref = bf16[1024,1024]{1,0:T(8,128)(2,1)} fusion(s32[1024]{0:T(1024)S(1)} %fusion.1), kind=kLoop, calls=%fused_computation.1 | loop fusion | flops 2097152 | bytes 2101248 | tf_op jit(solution)/shard_map/convert_element_type | solution.py:202
  23.0 49.4 %all-to-all-done.piece_ref = bf16[128,2,8,512]{3,2,1,0:T(8,128)(2,1)S(1)} async-done(((bf16[128,2,8,512]{3,2,1,0:T(8,128)(2,1)}), bf16[128,2,8,512]{3,2,1,0:T(8,128)(2,1)S(1)}, u32[]{:S(2)}, u32[]{:S(2)}) %all-to-all-start) | async-done | bytes 2097184 | tf_op jit(solution)/shard_map/all_to_all | solution.py:204
  72.3 0.0 copy-start
  72.3 1.6 %copy-done = bf16[1024,1024]{1,0:T(8,128)(2,1)S(1)} copy-done((bf16[1024,1024]{1,0:T(8,128)(2,1)S(1)}, bf16[1024,1024]{1,0:T(8,128)(2,1)}, u32[]{:S(2)}) %copy-start) | copy-done | bytes 2097176
  73.9 1.2 %shard_map.39 = (bf16[512,512]{1,0:T(8,128)(2,1)S(1)}, bf16[512,512]{1,0:T(8,128)(2,1)S(1)}) custom-call(bf16[1024,1024]{1,0:T(8,128)(2,1)S(1)} %copy-done, bf16[128,2,8,512]{3,2,1,0:T(8,128)(2,1)S(1)} %all-to-all-done.piece_ref), custom_call_target="tpu_custom_call" | custom-call | flops 1073741824 | bytes 3670016 | tf_op jit(solution)/shard_map/pallas_call | solution.py:207
  75.2 2.7 %collective-permute-start.1 = (bf16[512,512]{1,0:T(8,128)(2,1)S(1)}, bf16[512,512]{1,0:T(8,128)(2,1)S(1)}, u32[]{:S(2)}, u32[]{:S(2)}) collective-permute-start(bf16[512,512]{1,0:T(8,128)(2,1)S(1)} %get-tuple-element.19.off_r), channel_id=1, source_target_pairs={{0,1},{1,0},{2,3},{3,2},{4,5},{5,4},{6,7},{7,6},{8,9},{9,8},{10,11... | collective-permute-start | bytes 1572872 | tf_op jit(solution)/shard_map/ppermute | solution.py:21
  77.9 0.4 collective-permute-start.2
  78.2 2.0 %shard_map.38 = (bf16[512,512]{1,0:T(8,128)(2,1)S(1)}, bf16[512,512]{1,0:T(8,128)(2,1)S(1)}, bf16[528,512]{1,0:T(8,128)(2,1)S(1)}) custom-call(bf16[1024,1024]{1,0:T(8,128)(2,1)S(1)} %copy-done, bf16[128,2,8,512]{3,2,1,0:T(8,128)(2,1)S(1)} %all-to-all-done.piece_ref), custom_call_target="tpu_custom_call" | custom-call | flops 1073741824 | bytes 3670016 | tf_op jit(solution)/shard_map/pallas_call | solution.py:209
  80.2 2.9 %collective-permute-start = (bf16[528,512]{1,0:T(8,128)(2,1)S(1)}, bf16[528,512]{1,0:T(8,128)(2,1)S(1)}, u32[]{:S(2)}, u32[]{:S(2)}) collective-permute-start(bf16[528,512]{1,0:T(8,128)(2,1)S(1)} %get-tuple-element.16), channel_id=1, source_target_pairs={{0,1},{1,0},{2,3},{3,2},{4,5},{5,4},{6,7},{7,6},{8,9},{9,8},{10,11... | collective-permute-start | bytes 1622024 | tf_op jit(solution)/shard_map/ppermute | solution.py:21
  83.1 6.7 %collective-permute-done.1.their_r = bf16[512,512]{1,0:T(8,128)(2,1)S(1)} collective-permute-done((bf16[512,512]{1,0:T(8,128)(2,1)S(1)}, bf16[512,512]{1,0:T(8,128)(2,1)S(1)}, u32[]{:S(2)}, u32[]{:S(2)}) %collective-permute-start.1) | collective-permute-done | bytes 524320 | tf_op jit(solution)/shard_map/ppermute | solution.py:21
  89.9 11.2 %collective-permute-done.2.their_i = bf16[512,512]{1,0:T(8,128)(2,1)S(1)} collective-permute-done((bf16[512,512]{1,0:T(8,128)(2,1)S(1)}, bf16[512,512]{1,0:T(8,128)(2,1)S(1)}, u32[]{:S(2)}, u32[]{:S(2)}) %collective-permute-start.2) | collective-permute-done | bytes 524320 | tf_op jit(solution)/shard_map/ppermute | solution.py:21
  101.1 6.8 %shard_map.40 = (bf16[1024,1024]{1,0:T(8,128)(2,1)S(1)}, bf16[512,1024]{1,0:T(8,128)(2,1)S(1)}, bf16[512,1024]{1,0:T(8,128)(2,1)S(1)}, f32[512,1024]{1,0:T(8,128...) custom-call(bf16[512,512]{1,0:T(8,128)(2,1)S(1)} %get-tuple-element.17.own_r, ...), custom_call_target="tpu_custom_call" | custom-call | flops 5368709120 | bytes 15728640 | tf_op jit(solution)/shard_map/pallas_call | solution.py:142
  107.9 4.8 %collective-permute-done.packed_ref = bf16[528,512]{1,0:T(8,128)(2,1)S(1)} collective-permute-done((bf16[528,512]{1,0:T(8,128)(2,1)S(1)}, bf16[528,512]{1,0:T(8,128)(2,1)S(1)}, u32[]{:S(2)}, u32[]{:S(2)}) %collective-permute-start) | collective-permute-done | bytes 540704 | tf_op jit(solution)/shard_map/ppermute | solution.py:21
  112.7 5.1 %shard_map.41 = bf16[2,1,1024,512]{3,2,1,0:T(8,128)(2,1)} custom-call(s32[1]{0:T(128)} %bitcast.col_ref, bf16[528,512]{1,0:T(8,128)(2,1)S(1)} %collective-permute-done.packed_ref, bf16[512,512]{1,0:T(8,128)(2,1)S(1)} %get-tuple-element.17.own_r, bf16[512,512]{1,0:T(8,128)(2,1)S(1)} %get-tuple-element.18.own_i, ...), custom_call_target="tpu_custom_call" | custom-call | flops 3221225472 | bytes 15728640 | tf_op jit(solution)/shard_map/pallas_call | solution.py:183
Async XLA Ops:
  6.2 14.9 %copy-start.1 = (s32[1024]{0:T(1024)S(1)}, s32[1024]{0:T(1024)}, u32[]{:S(2)}) copy-start(s32[1024]{0:T(1024)} %param.4) | copy-start | bytes 12292
  6.2 66.1 %all-to-all-start = ((bf16[128,2,8,512]{3,2,1,0:T(8,128)(2,1)}), bf16[128,2,8,512]{3,2,1,0:T(8,128)(2,1)S(1)}, u32[]{:S(2)}, u32[]{:S(2)}) async-start(bf16[128,2,8,512]{3,2,1,0:T(8,128)(2,1)} %bitcast.2), calls=%async_computation | async-start | bytes 4194304 | tf_op jit(solution)/shard_map/all_to_all | solution.py:204
  72.3 1.6 %copy-start = (bf16[1024,1024]{1,0:T(8,128)(2,1)S(1)}, bf16[1024,1024]{1,0:T(8,128)(2,1)}, u32[]{:S(2)}) copy-start(bf16[1024,1024]{1,0:T(8,128)(2,1)} %fusion.pick_ref) | copy-start | bytes 6291460
  75.2 14.7 %collective-permute-start.1 = (bf16[512,512]{1,0:T(8,128)(2,1)S(1)}, bf16[512,512]{1,0:T(8,128)(2,1)S(1)}, u32[]{:S(2)}, u32[]{:S(2)}) collective-permute-start(bf16[512,512]{1,0:T(8,128)(2,1)S(1)} %get-tuple-element.19.off_r), channel_id=1, source_target_pairs={{0,1},{1,0},{2,3},{3,2},{4,5},{5,4},{6,7},{7,6},{8,9},{9,8},{10,11... | collective-permute-start | bytes 1572872 | tf_op jit(solution)/shard_map/ppermute | solution.py:21
  77.9 23.2 %collective-permute-start.2 = (bf16[512,512]{1,0:T(8,128)(2,1)S(1)}, bf16[512,512]{1,0:T(8,128)(2,1)S(1)}, u32[]{:S(2)}, u32[]{:S(2)}) collective-permute-start(bf16[512,512]{1,0:T(8,128)(2,1)S(1)} %get-tuple-element.20.off_i), channel_id=1, source_target_pairs={{0,1},{1,0},{2,3},{3,2},{4,5},{5,4},{6,7},{7,6},{8,9},{9,8},{10,11... | collective-permute-start | bytes 1572872 | tf_op jit(solution)/shard_map/ppermute | solution.py:21
  80.2 32.5 %collective-permute-start = (bf16[528,512]{1,0:T(8,128)(2,1)S(1)}, bf16[528,512]{1,0:T(8,128)(2,1)S(1)}, u32[]{:S(2)}, u32[]{:S(2)}) collective-permute-start(bf16[528,512]{1,0:T(8,128)(2,1)S(1)} %get-tuple-element.16), channel_id=1, source_target_pairs={{0,1},{1,0},{2,3},{3,2},{4,5},{5,4},{6,7},{7,6},{8,9},{9,8},{10,11... | collective-permute-start | bytes 1622024 | tf_op jit(solution)/shard_map/ppermute | solution.py:21

commit v3 on v2

v3 whole, which is shorter than its diff:
```python
import functools
import math

import jax
import jax.numpy as jnp
import numpy as np
from jax import lax
from jax.experimental import pallas as pl
from jax.experimental.pallas import tpu as pltpu
from jax.sharding import PartitionSpec as P


BF16 = jnp.bfloat16
F32 = jnp.float32
VMEM = pl.BlockSpec(memory_space=pltpu.VMEM)
SMEM = pl.BlockSpec(memory_space=pltpu.SMEM)
NT = ((1,), (1,))
PAD = 16


def partner(value):
    return lax.ppermute(value, "col", [(0, 1), (1, 0)])


WIDE, NARROW = 384, 128
NEAR, NEAR_BITS = 4, 9


def dft_table(samples, kept):
    phase = np.arange(kept)[:, None] * np.arange(samples)[None, :] % samples
    angle = np.float32(2.0 * math.pi / samples) * phase.astype(np.float32)
    table = np.stack([np.cos(angle), -np.sin(angle)], 1).reshape(2 * kept, samples)
    return jnp.asarray(table / np.sqrt(np.float32(samples)), dtype=BF16)


def dot(a, b, dims=((1,), (0,))):
    return lax.dot_general(a, b, (dims, ((), ())), preferred_element_type=F32)


def grid_of(size):
    return lax.broadcasted_iota(jnp.int32, (size, size), 0), lax.broadcasted_iota(jnp.int32, (size, size), 1)


def turn(block):
    row, col = grid_of(block.shape[1])
    return dot((row == col).astype(BF16), block, NT)


def call(kernel, out_shape, flops, moved, vmem_mib, **rest):
    return pl.pallas_call(
        kernel,
        out_shape=out_shape,
        cost_estimate=pl.CostEstimate(flops=flops, bytes_accessed=moved, transcendentals=0),
        compiler_params=pltpu.CompilerParams(vmem_limit_bytes=vmem_mib << 20),
        **rest,
    )


def far_owner(index):
    return index // 4 * 16 + index % 4 * 2


def near_bits(k):
    return k // 2 * 8 + k % 2


def dft_kernel(near_ref, table_ref, traces_ref, wide_ref, *rest):
    *narrow_refs, stage_ref = rest
    sources = traces_ref.shape[0]
    blocks, rows, lanes = stage_ref.shape
    rows //= sources
    for s in range(sources):
        value = dot(table_ref[...], traces_ref[s], NT)
        for b in range(blocks):
            stage_ref.at[b][pl.ds(s, rows, stride=sources), :] = value[:, b * lanes : (b + 1) * lanes]
    for b in range(blocks):
        wide_ref[:, :, b * lanes : (b + 1) * lanes] = stage_ref[b].reshape(rows, sources, lanes).astype(BF16)

    @pl.when(pl.program_id(0) == pl.num_programs(0) - 1)
    def _():
        step = 2 * sources
        for k, narrow_ref in enumerate(narrow_refs):
            near = near_ref[0] ^ near_bits(k)
            for index in range(narrow_ref.shape[0]):
                at = pl.multiple_of((far_owner(index) + near) * step, step)
                narrow_ref[index] = stage_ref[blocks - 1, pl.ds(at, step), :].reshape(2, sources, lanes).astype(BF16)


def dft(near, table, traces):
    rows, samples = table.shape
    sources, receivers, _ = traces.shape
    width = 2 * NARROW
    assert receivers == WIDE + NARROW == 2 * width
    wide = jax.ShapeDtypeStruct((rows, sources, WIDE), BF16)
    narrow = (rows // 2 // NEAR, 2, sources, NARROW)
    return call(
        dft_kernel,
        [wide] + [jax.ShapeDtypeStruct(narrow, BF16)] * NEAR,
        2 * rows * samples * sources * receivers,
        2 * (sources * receivers * samples + rows * samples + rows * sources * receivers),
        60,
        grid=(receivers // width,),
        in_specs=[
            SMEM,
            pl.BlockSpec((rows, samples), lambda j: (0, 0)),
            pl.BlockSpec((sources, width, samples), lambda j: (0, j, 0)),
        ],
        out_specs=[pl.BlockSpec((rows, sources, width), lambda j: (0, 0, j))]
        + [pl.BlockSpec(narrow, lambda j: (0, 0, 0, 0))] * NEAR,
        scratch_shapes=[pltpu.VMEM((2, rows * sources, NARROW), F32)],
    )(near, table, traces)


def join_kernel(*refs):
    *in_refs, out_ref = refs
    for k, in_ref in enumerate(in_refs):
        out_ref[:, k] = in_ref[...]


def join(pieces):
    count, *rest = pieces[0].shape
    shape = (count, len(pieces), *rest)
    return call(
        join_kernel,
        jax.ShapeDtypeStruct(shape, BF16),
        0,
        4 * math.prod(shape),
        60,
        in_specs=[VMEM] * len(pieces),
        out_specs=VMEM,
    )(*pieces)


def pick_rows(order_ref, at, count):
    lanes, size = 128, order_ref.shape[1]
    row = order_ref[:, at : at + count].astype(F32)
    column = jnp.broadcast_to(row, (lanes, count)).T
    lane = lax.broadcasted_iota(jnp.int32, (count, lanes), 1).astype(F32)
    picks = [jnp.where(column == lane + float(b), 1.0, 0.0).astype(BF16) for b in range(0, size, lanes)]
    return jnp.concatenate(picks, axis=1)


def rows_of(piece_ref, part):
    owners, _, sources, width = piece_ref.shape
    return piece_ref[:, part].astype(F32).reshape(owners * sources, width).astype(BF16)


def off_kernel(order_ref, piece_ref, off_ref):
    half = off_ref.shape[1]
    pick = pick_rows(order_ref, half, half)
    for part in range(2):
        off_ref[part] = dot(pick, rows_of(piece_ref, part)).astype(BF16)


def off_block(order, piece):
    half, width = order.shape[1] // 2, piece.shape[3]
    return call(
        off_kernel,
        jax.ShapeDtypeStruct((2, half, width), BF16),
        8 * half * half * width,
        14 * half * width,
        16,
        in_specs=[VMEM] * 2,
        out_specs=VMEM,
    )(order, piece)


def mix(real, imag):
    row, col = grid_of(real.shape[0])
    diagonal = jnp.sum(jnp.where(row == col, imag, 0.0), axis=0, keepdims=True)
    return jnp.where(row >= col, real, imag).astype(BF16), jnp.broadcast_to(diagonal, (PAD, real.shape[0])).astype(BF16)


def unmix(mixed, diagonal):
    row, col = grid_of(mixed.shape[0])
    turned, mixed, diagonal = turn(mixed), mixed.astype(F32), diagonal.astype(F32)
    real = jnp.where(row >= col, mixed, turned)
    imag = jnp.where(row < col, mixed, jnp.where(row > col, turned, diagonal))
    return real.astype(BF16), imag.astype(BF16)


def wide_kernel(order_ref, piece_ref, square_ref, below_ref, packed_ref):
    pick = pick_rows(order_ref, 0, WIDE + NARROW)
    parts = []
    for part in range(2):
        block = dot(pick, rows_of(piece_ref, part))
        below_ref[part] = block[WIDE:].astype(BF16)
        parts.append((block[:WIDE] + turn(block[:WIDE].astype(BF16))) * 0.5)
        square_ref[part] = parts[part].astype(BF16)
    packed_ref[:WIDE, :], packed_ref[WIDE:, :] = mix(*parts)


def wide_block(order, piece):
    half = WIDE + NARROW
    return call(
        wide_kernel,
        [jax.ShapeDtypeStruct(shape, BF16) for shape in ((2, WIDE, WIDE), (2, NARROW, WIDE), (WIDE + PAD, WIDE))],
        8 * half * half * WIDE,
        14 * half * WIDE,
        20,
        in_specs=[VMEM] * 2,
        out_specs=[VMEM] * 3,
    )(order, piece)


CUT = 48


def narrow_kernel(order_ref, piece_ref, square_ref, below_ref, own_ref, packed_ref):
    pick = pick_rows(order_ref, 0, WIDE + NARROW)
    corners = []
    for part in range(2):
        block = dot(pick, rows_of(piece_ref, part))
        beside, corner = block[:WIDE].astype(BF16), block[WIDE:]
        low = ((below_ref[part].astype(F32) + turn(beside)) * 0.5).astype(BF16)
        corners.append((corner + turn(corner.astype(BF16))) * 0.5)
        own_ref[part, :WIDE, :WIDE] = square_ref[part]
        own_ref[part, WIDE:, :WIDE] = low
        own_ref[part, :WIDE, WIDE:] = turn(low).astype(BF16)
        own_ref[part, WIDE:, WIDE:] = corners[part].astype(BF16)
        packed_ref[part * NARROW : (part + 1) * NARROW, :] = low
    mixed, diagonal = mix(*corners)
    at = 2 * NARROW
    packed_ref[at:, :NARROW] = mixed[:CUT]
    packed_ref[at:, NARROW : 2 * NARROW] = mixed[CUT : 2 * CUT]
    packed_ref[at:, 2 * NARROW :] = jnp.concatenate([mixed[2 * CUT :], diagonal], axis=0)


def narrow_block(order, piece, square, below):
    half = WIDE + NARROW
    return call(
        narrow_kernel,
        [jax.ShapeDtypeStruct(shape, BF16) for shape in ((2, half, half), (2 * NARROW + CUT, WIDE))],
        8 * half * half * NARROW,
        14 * half * half,
        20,
        in_specs=[VMEM] * 4,
        out_specs=[VMEM] * 2,
    )(order, piece, square, below)


def unpack(left_wide, left_narrow, wide_ref, narrow_ref):
    squares = unmix(wide_ref[:WIDE, :], wide_ref[WIDE : WIDE + 1, :])
    cuts = narrow_ref[2 * NARROW :, :]
    rest = NARROW - 2 * CUT
    mixed = jnp.concatenate([cuts[:, :NARROW], cuts[:, NARROW : 2 * NARROW], cuts[:rest, 2 * NARROW :]], axis=0)
    corners = unmix(mixed, cuts[rest : rest + 1, 2 * NARROW :])
    for part in range(2):
        low = narrow_ref[part * NARROW : (part + 1) * NARROW, :]
        at = slice(part * WIDE, (part + 1) * WIDE)
        left_wide[:WIDE, at] = squares[part]
        left_wide[WIDE:, at] = low
        at = slice(part * NARROW, (part + 1) * NARROW)
        left_narrow[:WIDE, at] = turn(low).astype(BF16)
        left_narrow[WIDE:, at] = corners[part]


def put_right(right_ref, real, imag):
    rows, cols = real.shape
    right_ref[:rows, :cols] = real
    right_ref[:rows, cols:] = imag
    right_ref[rows:, :cols] = -imag
    right_ref[rows:, cols:] = real


def average(block, turned):
    return ((block.astype(F32) + turn(turned)) * 0.5).astype(BF16)


def early_kernel(own_ref, off_wide, off_narrow, their_wide, right_own, upper_wide, right_wide, part_own, part_other):
    half = own_ref.shape[1]
    put_right(right_own, own_ref[0], own_ref[1])
    lows = []
    for part in range(2):
        off = jnp.concatenate([off_wide[part, :WIDE, :], off_narrow[part, :WIDE, :]], axis=1)
        lows.append(average(off, their_wide[part]))
        upper_wide[:, part * WIDE : (part + 1) * WIDE] = average(their_wide[part], off)
    put_right(right_wide, *lows)
    part_own[...] = dot(right_own[:half, :], right_own[...]) + dot(upper_wide[...], right_wide[...])
    part_other[...] = dot(right_wide[:WIDE, :], right_own[...])


def early(*blocks):
    half = WIDE + NARROW
    shapes = [
        jax.ShapeDtypeStruct((2 * half, 2 * half), BF16),
        jax.ShapeDtypeStruct((half, 2 * WIDE), BF16),
        jax.ShapeDtypeStruct((2 * WIDE, 2 * half), BF16),
        jax.ShapeDtypeStruct((half, 2 * half), F32),
        jax.ShapeDtypeStruct((WIDE, 2 * half), F32),
    ]
    return call(
        early_kernel, shapes, 24 * half**3, 60 * half**2, 24, in_specs=[VMEM] * len(blocks), out_specs=[VMEM] * len(shapes)
    )(*blocks)


def first_kernel(
    scale, off_wide, off_narrow, their_narrow, right_own, right_wide, part_own,
    upper_narrow, right_narrow, square_own, part_other, cube_own, cube_wide, cube_narrow, right_square,
):
    half = off_wide.shape[1]
    lows = []
    for part in range(2):
        off = jnp.concatenate([off_wide[part, WIDE:, :], off_narrow[part, WIDE:, :]], axis=1)
        lows.append(average(off, their_narrow[part]))
        upper_narrow[:, part * NARROW : (part + 1) * NARROW] = average(their_narrow[part], off)
    put_right(right_narrow, *lows)
    square = (scale * (part_own[...] + dot(upper_narrow[...], right_narrow[...]))).astype(BF16)
    square_own[...] = square
    put_right(right_square, square[:, :half], square[:, half:])
    part_other[...] = dot(right_narrow[:NARROW, :], right_own[...])
    cube_own[...] = dot(right_own[:half, :], right_square[...])
    cube_wide[...] = dot(right_wide[:WIDE, :], right_square[...])
    cube_narrow[...] = dot(right_narrow[:NARROW, :], right_square[...])


def first(*blocks):
    half = WIDE + NARROW
    shapes = [
        jax.ShapeDtypeStruct((half, 2 * NARROW), BF16),
        jax.ShapeDtypeStruct((2 * NARROW, 2 * half), BF16),
        jax.ShapeDtypeStruct((half, 2 * half), BF16),
        jax.ShapeDtypeStruct((NARROW, 2 * half), F32),
        jax.ShapeDtypeStruct((half, 2 * half), F32),
        jax.ShapeDtypeStruct((WIDE, 2 * half), F32),
        jax.ShapeDtypeStruct((NARROW, 2 * half), F32),
    ]
    return call(
        functools.partial(first_kernel, 1.0 / math.sqrt(2 * half)),
        shapes,
        22 * half**3,
        60 * half**2,
        28,
        in_specs=[VMEM] * len(blocks),
        out_specs=[VMEM] * len(shapes),
        scratch_shapes=[pltpu.VMEM((2 * half, 2 * half), BF16)],
    )(*blocks)


def second_kernel(
    scale, col_ref, packed_wide, packed_narrow, right_own, square_own, cube_own,
    upper_wide, right_wide, other_wide, cube_wide, upper_narrow, right_narrow, other_narrow, cube_narrow,
    out_ref, left_wide, left_narrow, next_wide, next_narrow, whole_ref, sems,
):
    half = WIDE + NARROW
    unpack(left_wide, left_narrow, packed_wide, packed_narrow)

    def product(wide, narrow):
        return dot(left_wide[...], wide[...]) + dot(left_narrow[...], narrow[...])

    def send(number, values):
        row = pl.multiple_of(lax.rem(col_ref[0] + number, 2) * half, half)
        copies = []
        for part in range(2):
            whole_ref[number, part] = values[:, part * half : (part + 1) * half].astype(BF16)
            copies.append(
                pltpu.make_async_copy(
                    whole_ref.at[number, part], out_ref.at[part, 0, pl.ds(row, half)], sems.at[2 * number + part]
                )
            )
            copies[-1].start()
        return copies

    other = jnp.concatenate([other_wide[...], other_narrow[...]], axis=0)
    square = (scale * (other + product(right_wide, right_narrow))).astype(BF16)
    put_right(next_wide, square[:WIDE, :half], square[:WIDE, half:])
    put_right(next_narrow, square[WIDE:, :half], square[WIDE:, half:])
    cube = scale * (cube_own[...] + dot(upper_wide[...], next_wide[...]) + dot(upper_narrow[...], next_narrow[...]))
    copies = send(0, right_own[:half, :].astype(F32) - square_own[...].astype(F32) + cube)
    other = jnp.concatenate([cube_wide[...], cube_narrow[...]], axis=0)
    cube = scale * (other + product(next_wide, next_narrow))
    low = jnp.concatenate([right_wide[:WIDE, :], right_narrow[:NARROW, :]], axis=0)
    copies += send(1, low.astype(F32) - square.astype(F32) + cube)
    for copy in copies:
        copy.wait()


def second(column_half, *blocks):
    half = WIDE + NARROW
    return call(
        functools.partial(second_kernel, 1.0 / math.sqrt(2 * half)),
        jax.ShapeDtypeStruct((2, 1, 2 * half, half), BF16),
        24 * half**3,
        60 * half**2,
        32,
        in_specs=[SMEM] + [VMEM] * len(blocks),
        out_specs=pl.BlockSpec(memory_space=pl.ANY),
        scratch_shapes=[
            pltpu.VMEM((half, 2 * WIDE), BF16),
            pltpu.VMEM((half, 2 * NARROW), BF16),
            pltpu.VMEM((2 * WIDE, 2 * half), BF16),
            pltpu.VMEM((2 * NARROW, 2 * half), BF16),
            pltpu.VMEM((2, 2, half, half), BF16),
            pltpu.SemaphoreType.DMA((4,)),
        ],
    )(scalar(column_half), *blocks)


def scalar(value):
    return jnp.full((1,), value, jnp.int32)


def swap(piece, groups=None):
    return lax.all_to_all(piece, "freq", split_axis=0, concat_axis=0, tiled=True, axis_index_groups=groups)


def swap_near(value, bits):
    return lax.ppermute(value, "freq", [(i, i ^ bits) for i in range(lax.axis_size("freq"))])


def body(traces, source_row):
    sources, _, samples = traces.shape
    kept = samples // 8
    size = source_row.shape[0]
    assert lax.axis_size("freq") == kept == 128
    column_half = lax.axis_index("col")
    owner = lax.axis_index("freq")
    order = jnp.roll(source_row, -column_half * (size // 2))[None, :]
    source_owner = order // sources
    apart = source_owner ^ owner
    near = (apart // 8 & 1) * 2 + (apart & 1)
    far = source_owner // 16 * 4 + (source_owner // 2 & 3)
    mixed_order = (far * NEAR + near) * sources + order % sources
    wide, *narrow = dft(scalar(owner & NEAR_BITS), dft_table(samples, kept), traces)
    wide = swap(wide.reshape(kept, 2, sources, WIDE))
    for k in range(1, NEAR):
        narrow[k] = swap_near(narrow[k], near_bits(k))
    narrow = join(narrow)
    off_wide = off_block(order, wide)
    their_off_wide = partner(off_wide)
    groups = [[far_owner(i) + near_bits(k) for i in range(kept // NEAR)] for k in range(NEAR)]
    narrow = swap(narrow, groups).reshape(kept, 2, sources, NARROW)
    square, below, packed_wide = wide_block(order, wide)
    packed_wide = partner(packed_wide)
    off_narrow = off_block(mixed_order, narrow)
    their_off_narrow = partner(off_narrow)
    own, packed_narrow = narrow_block(mixed_order, narrow, square, below)
    packed_narrow = partner(packed_narrow)
    right_own, upper_wide, right_wide, part_own, other_wide = early(own, off_wide, off_narrow, their_off_wide)
    upper_narrow, right_narrow, square_own, other_narrow, cube_own, cube_wide, cube_narrow = first(
        off_wide, off_narrow, their_off_narrow, right_own, right_wide, part_own
    )
    return second(
        column_half, packed_wide, packed_narrow, right_own, square_own, cube_own,
        upper_wide, right_wide, other_wide, cube_wide, upper_narrow, right_narrow, other_narrow, cube_narrow,
    )


def solution(mesh):
    in_specs = (P("freq", "col", None), P())
    out_specs = P(None, "freq", None, "col")
    return jax.shard_map(body, mesh=mesh, in_specs=in_specs, out_specs=out_specs, check_vma=False)
```

time: 118 us -> 111 us (0.941)
  waiting for transfers between devices: 72.1 us -> 49.7 us
  starting transfers between devices: 20.8 us -> 31.6 us
  Pallas kernels: 21.3 us -> 27.2 us
  other arithmetic: 1.81 us -> 0.1 us
    ppermute x3 -> x4, waiting for transfers between devices: 22.8 us -> 2.67 us  [partner(): return lax.ppermute(value, 'col', [(0, 1), (1, 0)])]
    all_to_all x1 -> x2, waiting for transfers between devices: 49.4 us -> 34.5 us  [swap(): lax.all_to_all(piece, 'freq', split_axis=0, concat_axis=0, tiled=True, ax...]
    ppermute x0 -> x3, waiting for transfers between devices: none -> 12.5 us  [swap_near(): lax.ppermute(value, 'freq', [(i, i ^ bits) for i in range(lax.axis_size('...]
    pallas_call x4 -> x8, Pallas kernels: 16.2 us -> 22.4 us  [the longest x1 6.28 us: dft(): call(dft_kernel, [wide] + [jax.ShapeDtypeStruct(narrow, BF16)] * NEAR, 2...]
    all_to_all x1 -> x2, starting transfers between devices: 14.9 us -> 20.2 us  [swap(): lax.all_to_all(piece, 'freq', split_axis=0, concat_axis=0, tiled=True, ax...]
    ppermute x3 -> x4, starting transfers between devices: 5.94 us -> 8.74 us  [partner(): return lax.ppermute(value, 'col', [(0, 1), (1, 0)])]
    ppermute x0 -> x3, starting transfers between devices: none -> 2.72 us  [swap_near(): lax.ppermute(value, 'freq', [(i, i ^ bits) for i in range(lax.axis_size('...]
    convert_element_type x1 -> x0, other arithmetic: 1.73 us -> none  [shards(): pick = (order[:, None] == jnp.arange(size)[None, :]).astype(BF16)]
  transfers between devices with their start and end apart: 4 -> 9, of which waited for: 4 -> 5; matrix products, arithmetic and copies ran while one was open for 2% -> 0% of each run, Pallas kernels for 7% -> 15%
where the time goes in v3:
time: 111 us; the launch traced here: 110 us
  waiting for transfers between devices  49.7 us (45%)
  starting transfers between devices  31.6 us (28%)
  Pallas kernels  27.2 us (25%)
    all_to_all x2, waiting for transfers between devices, swap(): lax.all_to_all(piece, 'freq', split_axis=0, concat_axis=0, tiled=True, ax...  34.5 us
    all_to_all x2, starting transfers between devices, swap(): lax.all_to_all(piece, 'freq', split_axis=0, concat_axis=0, tiled=True, ax...  20.2 us
    ppermute x3, waiting for transfers between devices, swap_near(): lax.ppermute(value, 'freq', [(i, i ^ bits) for i in range(lax.axis_size('...  12.5 us
    ppermute x4, starting transfers between devices, partner(): return lax.ppermute(value, 'col', [(0, 1), (1, 0)])  8.74 us
    pallas_call x1, Pallas kernels, dft(): call(dft_kernel, [wide] + [jax.ShapeDtypeStruct(narrow, BF16)] * NEAR, 2...  6.28 us
    pallas_call x1, Pallas kernels, early(): call(early_kernel, shapes, 24 * half ** 3, 60 * half ** 2, 24, in_specs=[...  5.01 us
    pallas_call x1, Pallas kernels, second(): call(functools.partial(second_kernel, 1.0 / math.sqrt(2 * half)), jax.Sha...  4.83 us
    pallas_call x1, Pallas kernels, first(): call(functools.partial(first_kernel, 1.0 / math.sqrt(2 * half)), shapes,...  3.27 us
  transfers between devices with their start and end apart: 9, of which 5 were waited for; matrix products, arithmetic and copies ran while one was open for 0% of the time, Pallas kernels for 15%

profile of v3, /device:TPU:1, one launch (start us, length us, event | category | flops | bytes accessed | tf_op | source)
XLA Modules:
  0.0 109.6 jit_solution(7402662649208781059)
XLA Ops:
  0.0 6.3 %shard_map.37 = (bf16[256,8,384]{2,1,0:T(8,128)(2,1)}, bf16[32,2,8,128]{3,2,1,0:T(8,128)(2,1)}, bf16[32,2,8,128]{3,2,1,0:T(8,128)(2,1)}, bf16[32,2,8,128]{3,2,1,0:T(8,128)(2,1)}, bf16[32,2,8,128]{3,2,1,0:T(8,128)(2,1)}) custom-call(s32[1]{0:T(128)} %bitcast.2.near_ref, bf16[256,1024]{1,0:T(8,128)(2,1)} %constant.96.clone.table_ref, ...), custom_call_target="tpu_custom_call" | custom-call | flops 2147483648 | bytes 11010048 | tf_op jit(solution)/shard_map/pallas_call | solution.py:96
  6.3 0.0 copy-start.6
  6.3 0.0 copy-start.5
  6.3 0.0 copy-start.4
  6.3 0.0 copy-start.3
  6.3 14.9 %all-to-all-start = ((bf16[128,2,8,384]{3,2,1,0:T(8,128)(2,1)}), bf16[128,2,8,384]{3,2,1,0:T(8,128)(2,1)S(1)}, u32[]{:S(2)}, u32[]{:S(2)}) async-start(bf16[128,2,8,384]{3,2,1,0:T(8,128)(2,1)} %bitcast.12), calls=%async_computation | async-start | bytes 3145728 | tf_op jit(solution)/shard_map/all_to_all | solution.py:404
  21.2 0.0 copy-done.6
  21.2 1.0 collective-permute-start.1
  22.2 0.0 copy-done.5
  22.2 0.9 collective-permute-start.2
  23.1 0.0 copy-done.4
  23.1 0.9 collective-permute-start.3
  24.0 0.0 collective-permute-done.1.refs_1_
  24.0 0.0 copy-start
  24.0 5.7 %collective-permute-done.2.refs_2_ = bf16[32,2,8,128]{3,2,1,0:T(8,128)(2,1)S(1)} collective-permute-done((bf16[32,2,8,128]{3,2,1,0:T(8,128)(2,1)S(1)}, bf16[32,2,8,128]{3,2,1,0:T(8,128)(2,1)S(1)}, u32[]{:S(2)}, u32[]{:S(2)}) %collective-permute-start.2) | collective-permute-done | bytes 131104 | tf_op jit(solution)/shard_map/ppermute | solution.py:408
  29.7 0.0 copy-start.1
  29.7 6.8 %collective-permute-done.3.refs_3_ = bf16[32,2,8,128]{3,2,1,0:T(8,128)(2,1)S(1)} collective-permute-done((bf16[32,2,8,128]{3,2,1,0:T(8,128)(2,1)S(1)}, bf16[32,2,8,128]{3,2,1,0:T(8,128)(2,1)S(1)}, u32[]{:S(2)}, u32[]{:S(2)}) %collective-permute-start.3) | collective-permute-done | bytes 131104 | tf_op jit(solution)/shard_map/ppermute | solution.py:408
  36.5 0.0 copy-start.2
  36.5 0.0 copy-done
  36.5 0.0 copy-done.1
  36.5 0.6 copy-done.2
  37.2 2.0 %shard_map.39 = bf16[32,4,2,8,128]{4,3,2,1,0:T(8,128)(2,1)} custom-call(bf16[32,2,8,128]{3,2,1,0:T(8,128)(2,1)} %get-tuple-element.29.refs_0_, bf16[32,2,8,128]{3,2,1,0:T(8,128)(2,1)} %copy-done, bf16[32,2,8,128]{3,2,1,0:T(8,128)(2,1)} %copy-done.1, bf16[32,2,8,128]{3,2,1,0:T(8,128)(2,1)} %copy-done.2), custom_call_target="tpu_custom_call" | custom-call | bytes 1048576 | tf_op jit(solution)/shard_map/pallas_call | solution.py:123
  39.1 22.1 %all-to-all-done.piece_ref = bf16[128,2,8,384]{3,2,1,0:T(8,128)(2,1)S(1)} async-done(((bf16[128,2,8,384]{3,2,1,0:T(8,128)(2,1)}), bf16[128,2,8,384]{3,2,1,0:T(8,128)(2,1)S(1)}, u32[]{:S(2)}, u32[]{:S(2)}) %all-to-all-start) | async-done | bytes 1572896 | tf_op jit(solution)/shard_map/all_to_all | solution.py:404
  61.2 5.3 %all-to-all-start.1 = ((bf16[32,4,2,8,128]{4,3,2,1,0:T(8,128)(2,1)}), bf16[32,4,2,8,128]{4,3,2,1,0:T(8,128)(2,1)S(1)}, u32[]{:S(2)}, u32[]{:S(2)}) async-start(bf16[32,4,2,8,128]{4,3,2,1,0:T(8,128)(2,1)} %shard_map.39), calls=%async_computation.1 | async-start | bytes 1048576 | tf_op jit(solution)/shard_map/all_to_all | solution.py:404
  66.5 0.0 copy-done.3
  66.5 0.1 fusion.6
  66.6 1.3 %shard_map.41.off_wide = bf16[2,512,384]{2,1,0:T(8,128)(2,1)S(1)} custom-call(s32[1,1024]{1,0:T(1,128)S(1)} %bitcast.10, bf16[128,2,8,384]{3,2,1,0:T(8,128)(2,1)S(1)} %all-to-all-done.piece_ref), custom_call_target="tpu_custom_call" | custom-call | flops 805306368 | bytes 2752512 | tf_op jit(solution)/shard_map/pallas_call | solution.py:157
  67.9 2.7 %collective-permute-start.5 = (bf16[2,512,384]{2,1,0:T(8,128)(2,1)S(1)}, bf16[2,512,384]{2,1,0:T(8,128)(2,1)}, u32[]{:S(2)}, u32[]{:S(2)}) collective-permute-start(bf16[2,512,384]{2,1,0:T(8,128)(2,1)S(1)} %shard_map.41.off_wide), channel_id=1, source_target_pairs={{0,1},{1,0},{2,3},{3,2},{4,5},{5,4},{6,7},{7,6},{8,9},{9,8},{10,11... | collective-permute-start | bytes 2359304 | tf_op jit(solution)/shard_map/ppermute | solution.py:22
  70.6 12.4 %all-to-all-done.1 = bf16[32,4,2,8,128]{4,3,2,1,0:T(8,128)(2,1)S(1)} async-done(((bf16[32,4,2,8,128]{4,3,2,1,0:T(8,128)(2,1)}), bf16[32,4,2,8,128]{4,3,2,1,0:T(8,128)(2,1)S(1)}, u32[]{:S(2)}, u32[]{:S(2)}) %all-to-all-start.1) | async-done | bytes 524320 | tf_op jit(solution)/shard_map/all_to_all | solution.py:404
  83.0 0.8 shard_map.42.off_narrow
  83.8 2.7 %collective-permute-start.6 = (bf16[2,512,128]{2,1,0:T(8,128)(2,1)S(1)}, bf16[2,512,128]{2,1,0:T(8,128)(2,1)S(1)}, u32[]{:S(2)}, u32[]{:S(2)}) collective-permute-start(bf16[2,512,128]{2,1,0:T(8,128)(2,1)S(1)} %shard_map.42.off_narrow), channel_id=1, source_target_pairs={{0,1},{1,0},{2,3},{3,2},{4,5},{5,4},{6,7},{7,6},{8,9},{9,8},{10,11... | collective-permute-start | bytes 786440 | tf_op jit(solution)/shard_map/ppermute | solution.py:22
  86.5 1.8 %shard_map.38 = (bf16[2,384,384]{2,1,0:T(8,128)(2,1)S(1)}, bf16[2,128,384]{2,1,0:T(8,128)(2,1)S(1)}, bf16[400,384]{1,0:T(8,128)(2,1)S(1)}) custom-call(s32[1,1024]{1,0:T(1,128)S(1)} %bitcast.11, bf16[128,2,8,384]{3,2,1,0:T(8,128)(2,1)S(1)} %all-to-all-done.piece_ref), custom_call_target="tpu_custom_call" | custom-call | flops 805306368 | bytes 2752512 | tf_op jit(solution)/shard_map/pallas_call | solution.py:195
  88.4 0.4 collective-permute-start
  88.8 2.0 %shard_map.40 = (bf16[2,512,512]{2,1,0:T(8,128)(2,1)S(1)}, bf16[304,384]{1,0:T(8,128)(2,1)S(1)}) custom-call(s32[1,1024]{1,0:T(1,128)S(1)} %bitcast.9, bf16[128,2,8,128]{3,2,1,0:T(8,128)(2,1)S(1)} %bitcast.7, bf16[2,384,384]{2,1,0:T(8,128)(2,1)S(1)} %get-tuple-element.33.square_ref, bf16[2,128,384]{2,1,0:T(8,128)(2,1)S(1)} %get-tuple-element.34.below_ref), custom_call_target="tpu_custom_call" | custom-call | flops 268435456 | bytes 3670016 | tf_op jit(solution)/shard_map/pallas_call | solution.py:231
  90.8 2.9 %collective-permute-start.4 = (bf16[304,384]{1,0:T(8,128)(2,1)S(1)}, bf16[304,384]{1,0:T(8,128)(2,1)S(1)}, u32[]{:S(2)}, u32[]{:S(2)}) collective-permute-start(bf16[304,384]{1,0:T(8,128)(2,1)S(1)} %get-tuple-element.35), channel_id=1, source_target_pairs={{0,1},{1,0},{2,3},{3,2},{4,5},{5,4},{6,7},{7,6},{8,9},{9,8},{10,11... | collective-permute-start | bytes 700424 | tf_op jit(solution)/shard_map/ppermute | solution.py:22
  93.7 0.0 collective-permute-done.5.their_wide
  93.7 5.0 %shard_map.43 = (bf16[1024,1024]{1,0:T(8,128)(2,1)S(1)}, bf16[512,768]{1,0:T(8,128)(2,1)S(1)}, bf16[768,1024]{1,0:T(8,128)(2,1)S(1)}, f32[512,1024]{1,0:T(8,128)S(1)}, f32[384,1024]{1,0:T(8,128)S(1)}) custom-call(bf16[2,512,512]{2,1,0:T(8,128)(2,1)S(1)} %get-tuple-element.36.own_ref, bf16[2,512,384]{2,1,0:T(8,128)(2,1)S(1)} %shard_map.41.off_wide, ...), custom_call_target="tpu_custom_call" | custom-call | flops 3221225472 | bytes 15728640 | tf_op jit(solution)/shard_map/pallas_call | solution.py:292
  98.7 0.0 collective-permute-done.6.their_narrow
  98.7 3.3 %shard_map.44 = (bf16[512,256]{1,0:T(8,128)(2,1)S(1)}, bf16[256,1024]{1,0:T(8,128)(2,1)S(1)}, bf16[512,1024]{1,0:T(8,128)(2,1)S(1)}, f32[128,1024]{1,0:T(8,128)S...) custom-call(bf16[2,512,384]{2,1,0:T(8,128)(2,1)S(1)} %shard_map.41.off_wide, ...), custom_call_target="tpu_custom_call" | custom-call | flops 2952790016 | bytes 15728640 | tf_op jit(solution)/shard_map/pallas_call | solution.py:328
  102.0 2.7 %collective-permute-done.4.packed_narrow = bf16[304,384]{1,0:T(8,128)(2,1)S(1)} collective-permute-done((bf16[304,384]{1,0:T(8,128)(2,1)S(1)}, bf16[304,384]{1,0:T(8,128)(2,1)S(1)}, u32[]{:S(2)}, u32[]{:S(2)}) %collective-permute-start.4) | collective-permute-done | bytes 233504 | tf_op jit(solution)/shard_map/ppermute | solution.py:22
  104.6 0.0 collective-permute-done.packed_wide
  104.7 4.8 %shard_map.45 = bf16[2,1,1024,512]{3,2,1,0:T(8,128)(2,1)} custom-call(s32[1]{0:T(128)} %bitcast.col_ref, bf16[400,384]{1,0:T(8,128)(2,1)S(1)} %collective-permute-done.packed_wide, bf16[304,384]{1,0:T(8,128)(2,1)S(1)} %collective-permute-done.4.packed_narrow, bf16[1024,1024]{1,0:T(8,128)(2,1)S(1)} %get-tuple-element.37.right_own, ...), custom_call_target="tpu_custom_call" | custom-call | flops 3221225472 | bytes 15728640 | tf_op jit(solution)/shard_map/pallas_call | solution.py:380
Async XLA Ops:
  6.3 14.9 %copy-start.6 = (bf16[32,2,8,128]{3,2,1,0:T(8,128)(2,1)S(1)}, bf16[32,2,8,128]{3,2,1,0:T(8,128)(2,1)}, u32[]{:S(2)}) copy-start(bf16[32,2,8,128]{3,2,1,0:T(8,128)(2,1)} %get-tuple-element.30) | copy-start | bytes 393220
  6.3 15.9 %copy-start.5 = (bf16[32,2,8,128]{3,2,1,0:T(8,128)(2,1)S(1)}, bf16[32,2,8,128]{3,2,1,0:T(8,128)(2,1)}, u32[]{:S(2)}) copy-start(bf16[32,2,8,128]{3,2,1,0:T(8,128)(2,1)} %get-tuple-element.31) | copy-start | bytes 393220
  6.3 16.8 %copy-start.4 = (bf16[32,2,8,128]{3,2,1,0:T(8,128)(2,1)S(1)}, bf16[32,2,8,128]{3,2,1,0:T(8,128)(2,1)}, u32[]{:S(2)}) copy-start(bf16[32,2,8,128]{3,2,1,0:T(8,128)(2,1)} %get-tuple-element.32) | copy-start | bytes 393220
  6.3 60.2 %copy-start.3 = (s32[1024]{0:T(1024)S(1)}, s32[1024]{0:T(1024)}, u32[]{:S(2)}) copy-start(s32[1024]{0:T(1024)} %param.4) | copy-start | bytes 12292
  6.3 54.9 %all-to-all-start = ((bf16[128,2,8,384]{3,2,1,0:T(8,128)(2,1)}), bf16[128,2,8,384]{3,2,1,0:T(8,128)(2,1)S(1)}, u32[]{:S(2)}, u32[]{:S(2)}) async-start(bf16[128,2,8,384]{3,2,1,0:T(8,128)(2,1)} %bitcast.12), calls=%async_computation | async-start | bytes 3145728 | tf_op jit(solution)/shard_map/all_to_all | solution.py:404
  21.2 2.7 %collective-permute-start.1 = (bf16[32,2,8,128]{3,2,1,0:T(8,128)(2,1)S(1)}, bf16[32,2,8,128]{3,2,1,0:T(8,128)(2,1)S(1)}, u32[]{:S(2)}, u32[]{:S(2)}) collective-permute-start(bf16[32,2,8,128]{3,2,1,0:T(8,128)(2,1)S(1)} %copy-done.6), channel_id=1, source_target_pairs={{0,2},{2,0},{4,6},{6,4},{8,10},{10,8},{12,14},{14,12},{16,18},{18,... | collective-permute-start | bytes 393224 | tf_op jit(solution)/shard_map/ppermute | solution.py:408
  22.2 7.5 %collective-permute-start.2 = (bf16[32,2,8,128]{3,2,1,0:T(8,128)(2,1)S(1)}, bf16[32,2,8,128]{3,2,1,0:T(8,128)(2,1)S(1)}, u32[]{:S(2)}, u32[]{:S(2)}) collective-permute-start(bf16[32,2,8,128]{3,2,1,0:T(8,128)(2,1)S(1)} %copy-done.5), channel_id=1, source_target_pairs={{0,16},{2,18},{4,20},{6,22},{8,24},{10,26},{12,28},{14,30},{16,0},... | collective-permute-start | bytes 393224 | tf_op jit(solution)/shard_map/ppermute | solution.py:408
  23.1 13.4 %collective-permute-start.3 = (bf16[32,2,8,128]{3,2,1,0:T(8,128)(2,1)S(1)}, bf16[32,2,8,128]{3,2,1,0:T(8,128)(2,1)S(1)}, u32[]{:S(2)}, u32[]{:S(2)}) collective-permute-start(bf16[32,2,8,128]{3,2,1,0:T(8,128)(2,1)S(1)} %copy-done.4), channel_id=1, source_target_pairs={{0,18},{2,16},{4,22},{6,20},{8,26},{10,24},{12,30},{14,28},{16,2},... | collective-permute-start | bytes 393224 | tf_op jit(solution)/shard_map/ppermute | solution.py:408
  24.0 12.5 %copy-start = (bf16[32,2,8,128]{3,2,1,0:T(8,128)(2,1)}, bf16[32,2,8,128]{3,2,1,0:T(8,128)(2,1)S(1)}, u32[]{:S(2)}) copy-start(bf16[32,2,8,128]{3,2,1,0:T(8,128)(2,1)S(1)} %collective-permute-done.1.refs_1_) | copy-start | bytes 393220
  29.7 6.8 %copy-start.1 = (bf16[32,2,8,128]{3,2,1,0:T(8,128)(2,1)}, bf16[32,2,8,128]{3,2,1,0:T(8,128)(2,1)S(1)}, u32[]{:S(2)}) copy-start(bf16[32,2,8,128]{3,2,1,0:T(8,128)(2,1)S(1)} %collective-permute-done.2.refs_2_) | copy-start | bytes 393220
  36.5 0.6 copy-start.2
  61.2 21.8 %all-to-all-start.1 = ((bf16[32,4,2,8,128]{4,3,2,1,0:T(8,128)(2,1)}), bf16[32,4,2,8,128]{4,3,2,1,0:T(8,128)(2,1)S(1)}, u32[]{:S(2)}, u32[]{:S(2)}) async-start(bf16[32,4,2,8,128]{4,3,2,1,0:T(8,128)(2,1)} %shard_map.39), calls=%async_computation.1 | async-start | bytes 1048576 | tf_op jit(solution)/shard_map/all_to_all | solution.py:404
  67.9 25.8 %collective-permute-start.5 = (bf16[2,512,384]{2,1,0:T(8,128)(2,1)S(1)}, bf16[2,512,384]{2,1,0:T(8,128)(2,1)}, u32[]{:S(2)}, u32[]{:S(2)}) collective-permute-start(bf16[2,512,384]{2,1,0:T(8,128)(2,1)S(1)} %shard_map.41.off_wide), channel_id=1, source_target_pairs={{0,1},{1,0},{2,3},{3,2},{4,5},{5,4},{6,7},{7,6},{8,9},{9,8},{10,11... | collective-permute-start | bytes 2359304 | tf_op jit(solution)/shard_map/ppermute | solution.py:22
  83.8 14.9 %collective-permute-start.6 = (bf16[2,512,128]{2,1,0:T(8,128)(2,1)S(1)}, bf16[2,512,128]{2,1,0:T(8,128)(2,1)S(1)}, u32[]{:S(2)}, u32[]{:S(2)}) collective-permute-start(bf16[2,512,128]{2,1,0:T(8,128)(2,1)S(1)} %shard_map.42.off_narrow), channel_id=1, source_target_pairs={{0,1},{1,0},{2,3},{3,2},{4,5},{5,4},{6,7},{7,6},{8,9},{9,8},{10,11... | collective-permute-start | bytes 786440 | tf_op jit(solution)/shard_map/ppermute | solution.py:22
  88.4 16.3 %collective-permute-start = (bf16[400,384]{1,0:T(8,128)(2,1)S(1)}, bf16[400,384]{1,0:T(8,128)(2,1)S(1)}, u32[]{:S(2)}, u32[]{:S(2)}) collective-permute-start(bf16[400,384]{1,0:T(8,128)(2,1)S(1)} %get-tuple-element.28), channel_id=1, source_target_pairs={{0,1},{1,0},{2,3},{3,2},{4,5},{5,4},{6,7},{7,6},{8,9},{9,8},{10,11... | collective-permute-start | bytes 921608 | tf_op jit(solution)/shard_map/ppermute | solution.py:22
  90.8 13.9 %collective-permute-start.4 = (bf16[304,384]{1,0:T(8,128)(2,1)S(1)}, bf16[304,384]{1,0:T(8,128)(2,1)S(1)}, u32[]{:S(2)}, u32[]{:S(2)}) collective-permute-start(bf16[304,384]{1,0:T(8,128)(2,1)S(1)} %get-tuple-element.35), channel_id=1, source_target_pairs={{0,1},{1,0},{2,3},{3,2},{4,5},{5,4},{6,7},{7,6},{8,9},{9,8},{10,11... | collective-permute-start | bytes 700424 | tf_op jit(solution)/shard_map/ppermute | solution.py:22

commit v4 on v3

--- a/solution.py
+++ b/solution.py
@@ -42,8 +42,7 @@
 
 
 def turn(block):
-    row, col = grid_of(block.shape[1])
-    return dot((row == col).astype(BF16), block, NT)
+    return block.T.astype(F32)
 
 
 def call(kernel, out_shape, flops, moved, vmem_mib, **rest):
@@ -145,11 +144,16 @@
     return piece_ref[:, part].astype(F32).reshape(owners * sources, width).astype(BF16)
 
 
+def both_of(piece_ref):
+    return jnp.concatenate([rows_of(piece_ref, part) for part in range(2)], axis=1)
+
+
 def off_kernel(order_ref, piece_ref, off_ref):
     half = off_ref.shape[1]
-    pick = pick_rows(order_ref, half, half)
-    for part in range(2):
-        off_ref[part] = dot(pick, rows_of(piece_ref, part)).astype(BF16)
+    width = off_ref.shape[2]
+    block = dot(pick_rows(order_ref, half, half), both_of(piece_ref)).astype(BF16)
+    for part in range(2):
+        off_ref[part] = block[:, part * width : (part + 1) * width]
 
 
 def off_block(order, piece):
@@ -180,10 +184,10 @@
 
 
 def wide_kernel(order_ref, piece_ref, square_ref, below_ref, packed_ref):
-    pick = pick_rows(order_ref, 0, WIDE + NARROW)
+    both = dot(pick_rows(order_ref, 0, WIDE + NARROW), both_of(piece_ref))
     parts = []
     for part in range(2):
-        block = dot(pick, rows_of(piece_ref, part))
+        block = both[:, part * WIDE : (part + 1) * WIDE]
         below_ref[part] = block[WIDE:].astype(BF16)
         parts.append((block[:WIDE] + turn(block[:WIDE].astype(BF16))) * 0.5)
         square_ref[part] = parts[part].astype(BF16)
@@ -207,10 +211,10 @@
 
 
 def narrow_kernel(order_ref, piece_ref, square_ref, below_ref, own_ref, packed_ref):
-    pick = pick_rows(order_ref, 0, WIDE + NARROW)
+    both = dot(pick_rows(order_ref, 0, WIDE + NARROW), both_of(piece_ref))
     corners = []
     for part in range(2):
-        block = dot(pick, rows_of(piece_ref, part))
+        block = both[:, part * NARROW : (part + 1) * NARROW]
         beside, corner = block[:WIDE].astype(BF16), block[WIDE:]
         low = ((below_ref[part].astype(F32) + turn(beside)) * 0.5).astype(BF16)
         corners.append((corner + turn(corner.astype(BF16))) * 0.5)

time: 111 us -> 110 us (level)
  Pallas kernels: 27.2 us -> 23.4 us
  waiting for transfers between devices: 49.7 us -> 52.7 us
    ppermute x4, waiting for transfers between devices: 2.67 us -> 5.38 us  [partner(): return lax.ppermute(value, 'col', [(0, 1), (1, 0)])]
    pallas_call x1, Pallas kernels: 1.99 us -> 0.69 us  [narrow_block(): call(narrow_kernel, [jax.ShapeDtypeStruct(shape, BF16) for shape in ((2,...]
  transfers between devices with their start and end apart: 9 -> 9, of which waited for: 5 -> 5; matrix products, arithmetic and copies ran while one was open for 0% -> 0% of each run, Pallas kernels for 15% -> 12%
where the time goes in v4:
time: 110 us; the launch traced here: 109 us
  waiting for transfers between devices  52.7 us (48%)
  starting transfers between devices  31.6 us (29%)
  Pallas kernels  23.4 us (21%)
    all_to_all x2, waiting for transfers between devices, swap(): lax.all_to_all(piece, 'freq', split_axis=0, concat_axis=0, tiled=True, ax...  34.7 us
    all_to_all x2, starting transfers between devices, swap(): lax.all_to_all(piece, 'freq', split_axis=0, concat_axis=0, tiled=True, ax...  20.2 us
    ppermute x3, waiting for transfers between devices, swap_near(): lax.ppermute(value, 'freq', [(i, i ^ bits) for i in range(lax.axis_size('...  12.5 us
    ppermute x4, starting transfers between devices, partner(): return lax.ppermute(value, 'col', [(0, 1), (1, 0)])  8.74 us
    pallas_call x1, Pallas kernels, dft(): call(dft_kernel, [wide] + [jax.ShapeDtypeStruct(narrow, BF16)] * NEAR, 2...  6.28 us
    ppermute x4, waiting for transfers between devices, partner(): return lax.ppermute(value, 'col', [(0, 1), (1, 0)])  5.38 us
    pallas_call x1, Pallas kernels, early(): call(early_kernel, shapes, 24 * half ** 3, 60 * half ** 2, 24, in_specs=[...  4.39 us
    pallas_call x1, Pallas kernels, second(): call(functools.partial(second_kernel, 1.0 / math.sqrt(2 * half)), jax.Sha...  4.33 us
  transfers between devices with their start and end apart: 9, of which 5 were waited for; matrix products, arithmetic and copies ran while one was open for 0% of the time, Pallas kernels for 12%

profile of v4, /device:TPU:1, one launch (start us, length us, event | category | flops | bytes accessed | tf_op | source)
XLA Modules:
  0.0 108.8 jit_solution(8453774326208284824)
XLA Ops:
  0.0 6.3 %shard_map.37 = (bf16[256,8,384]{2,1,0:T(8,128)(2,1)}, bf16[32,2,8,128]{3,2,1,0:T(8,128)(2,1)}, bf16[32,2,8,128]{3,2,1,0:T(8,128)(2,1)}, bf16[32,2,8,128]{3,2,1,0:T(8,128)(2,1)}, bf16[32,2,8,128]{3,2,1,0:T(8,128)(2,1)}) custom-call(s32[1]{0:T(128)} %bitcast.2.near_ref, bf16[256,1024]{1,0:T(8,128)(2,1)} %constant.96.clone.table_ref, ...), custom_call_target="tpu_custom_call" | custom-call | flops 2147483648 | bytes 11010048 | tf_op jit(solution)/shard_map/pallas_call | solution.py:95
  6.3 0.0 copy-start.6
  6.3 0.0 copy-start.5
  6.3 0.0 copy-start.4
  6.3 0.0 copy-start.3
  6.3 14.9 %all-to-all-start = ((bf16[128,2,8,384]{3,2,1,0:T(8,128)(2,1)}), bf16[128,2,8,384]{3,2,1,0:T(8,128)(2,1)S(1)}, u32[]{:S(2)}, u32[]{:S(2)}) async-start(bf16[128,2,8,384]{3,2,1,0:T(8,128)(2,1)} %bitcast.12), calls=%async_computation | async-start | bytes 3145728 | tf_op jit(solution)/shard_map/all_to_all | solution.py:408
  21.2 0.0 copy-done.6
  21.2 1.0 collective-permute-start.1
  22.2 0.0 copy-done.5
  22.2 0.9 collective-permute-start.2
  23.1 0.0 copy-done.4
  23.1 0.9 collective-permute-start.3
  24.0 0.0 collective-permute-done.1.refs_1_
  24.0 0.0 copy-start
  24.0 5.7 %collective-permute-done.2.refs_2_ = bf16[32,2,8,128]{3,2,1,0:T(8,128)(2,1)S(1)} collective-permute-done((bf16[32,2,8,128]{3,2,1,0:T(8,128)(2,1)S(1)}, bf16[32,2,8,128]{3,2,1,0:T(8,128)(2,1)S(1)}, u32[]{:S(2)}, u32[]{:S(2)}) %collective-permute-start.2) | collective-permute-done | bytes 131104 | tf_op jit(solution)/shard_map/ppermute | solution.py:412
  29.7 0.0 copy-start.1
  29.7 6.8 %collective-permute-done.3.refs_3_ = bf16[32,2,8,128]{3,2,1,0:T(8,128)(2,1)S(1)} collective-permute-done((bf16[32,2,8,128]{3,2,1,0:T(8,128)(2,1)S(1)}, bf16[32,2,8,128]{3,2,1,0:T(8,128)(2,1)S(1)}, u32[]{:S(2)}, u32[]{:S(2)}) %collective-permute-start.3) | collective-permute-done | bytes 131104 | tf_op jit(solution)/shard_map/ppermute | solution.py:412
  36.5 0.0 copy-start.2
  36.5 0.0 copy-done
  36.5 0.0 copy-done.1
  36.5 0.6 copy-done.2
  37.2 2.0 %shard_map.39 = bf16[32,4,2,8,128]{4,3,2,1,0:T(8,128)(2,1)} custom-call(bf16[32,2,8,128]{3,2,1,0:T(8,128)(2,1)} %get-tuple-element.29.refs_0_, bf16[32,2,8,128]{3,2,1,0:T(8,128)(2,1)} %copy-done, bf16[32,2,8,128]{3,2,1,0:T(8,128)(2,1)} %copy-done.1, bf16[32,2,8,128]{3,2,1,0:T(8,128)(2,1)} %copy-done.2), custom_call_target="tpu_custom_call" | custom-call | bytes 1048576 | tf_op jit(solution)/shard_map/pallas_call | solution.py:122
  39.1 22.1 %all-to-all-done.piece_ref = bf16[128,2,8,384]{3,2,1,0:T(8,128)(2,1)S(1)} async-done(((bf16[128,2,8,384]{3,2,1,0:T(8,128)(2,1)}), bf16[128,2,8,384]{3,2,1,0:T(8,128)(2,1)S(1)}, u32[]{:S(2)}, u32[]{:S(2)}) %all-to-all-start) | async-done | bytes 1572896 | tf_op jit(solution)/shard_map/all_to_all | solution.py:408
  61.2 5.3 %all-to-all-start.1 = ((bf16[32,4,2,8,128]{4,3,2,1,0:T(8,128)(2,1)}), bf16[32,4,2,8,128]{4,3,2,1,0:T(8,128)(2,1)S(1)}, u32[]{:S(2)}, u32[]{:S(2)}) async-start(bf16[32,4,2,8,128]{4,3,2,1,0:T(8,128)(2,1)} %shard_map.39), calls=%async_computation.1 | async-start | bytes 1048576 | tf_op jit(solution)/shard_map/all_to_all | solution.py:408
  66.5 0.0 copy-done.3
  66.5 0.1 fusion.6
  66.6 1.0 shard_map.41.off_wide
  67.7 2.7 %collective-permute-start.5 = (bf16[2,512,384]{2,1,0:T(8,128)(2,1)S(1)}, bf16[2,512,384]{2,1,0:T(8,128)(2,1)}, u32[]{:S(2)}, u32[]{:S(2)}) collective-permute-start(bf16[2,512,384]{2,1,0:T(8,128)(2,1)S(1)} %shard_map.41.off_wide), channel_id=1, source_target_pairs={{0,1},{1,0},{2,3},{3,2},{4,5},{5,4},{6,7},{7,6},{8,9},{9,8},{10,11... | collective-permute-start | bytes 2359304 | tf_op jit(solution)/shard_map/ppermute | solution.py:22
  70.4 12.7 %all-to-all-done.1 = bf16[32,4,2,8,128]{4,3,2,1,0:T(8,128)(2,1)S(1)} async-done(((bf16[32,4,2,8,128]{4,3,2,1,0:T(8,128)(2,1)}), bf16[32,4,2,8,128]{4,3,2,1,0:T(8,128)(2,1)S(1)}, u32[]{:S(2)}, u32[]{:S(2)}) %all-to-all-start.1) | async-done | bytes 524320 | tf_op jit(solution)/shard_map/all_to_all | solution.py:408
  83.0 0.6 shard_map.42.off_narrow
  83.6 2.7 %collective-permute-start.6 = (bf16[2,512,128]{2,1,0:T(8,128)(2,1)S(1)}, bf16[2,512,128]{2,1,0:T(8,128)(2,1)S(1)}, u32[]{:S(2)}, u32[]{:S(2)}) collective-permute-start(bf16[2,512,128]{2,1,0:T(8,128)(2,1)S(1)} %shard_map.42.off_narrow), channel_id=1, source_target_pairs={{0,1},{1,0},{2,3},{3,2},{4,5},{5,4},{6,7},{7,6},{8,9},{9,8},{10,11... | collective-permute-start | bytes 786440 | tf_op jit(solution)/shard_map/ppermute | solution.py:22
  86.3 1.2 %shard_map.38 = (bf16[2,384,384]{2,1,0:T(8,128)(2,1)S(1)}, bf16[2,128,384]{2,1,0:T(8,128)(2,1)S(1)}, bf16[400,384]{1,0:T(8,128)(2,1)S(1)}) custom-call(s32[1,1024]{1,0:T(1,128)S(1)} %bitcast.11, bf16[128,2,8,384]{3,2,1,0:T(8,128)(2,1)S(1)} %all-to-all-done.piece_ref), custom_call_target="tpu_custom_call" | custom-call | flops 805306368 | bytes 2752512 | tf_op jit(solution)/shard_map/pallas_call | solution.py:199
  87.5 0.4 collective-permute-start
  87.9 0.7 shard_map.40
  88.6 2.9 %collective-permute-start.4 = (bf16[304,384]{1,0:T(8,128)(2,1)S(1)}, bf16[304,384]{1,0:T(8,128)(2,1)S(1)}, u32[]{:S(2)}, u32[]{:S(2)}) collective-permute-start(bf16[304,384]{1,0:T(8,128)(2,1)S(1)} %get-tuple-element.35), channel_id=1, source_target_pairs={{0,1},{1,0},{2,3},{3,2},{4,5},{5,4},{6,7},{7,6},{8,9},{9,8},{10,11... | collective-permute-start | bytes 700424 | tf_op jit(solution)/shard_map/ppermute | solution.py:22
  91.5 0.0 collective-permute-done.5.their_wide
  91.5 4.4 %shard_map.43 = (bf16[1024,1024]{1,0:T(8,128)(2,1)S(1)}, bf16[512,768]{1,0:T(8,128)(2,1)S(1)}, bf16[768,1024]{1,0:T(8,128)(2,1)S(1)}, f32[512,1024]{1,0:T(8,128)S(1)}, f32[384,1024]{1,0:T(8,128)S(1)}) custom-call(bf16[2,512,512]{2,1,0:T(8,128)(2,1)S(1)} %get-tuple-element.36.own_ref, bf16[2,512,384]{2,1,0:T(8,128)(2,1)S(1)} %shard_map.41.off_wide, ...), custom_call_target="tpu_custom_call" | custom-call | flops 3221225472 | bytes 15728640 | tf_op jit(solution)/shard_map/pallas_call | solution.py:296
  95.9 0.0 collective-permute-done.6.their_narrow
  95.9 3.0 %shard_map.44 = (bf16[512,256]{1,0:T(8,128)(2,1)S(1)}, bf16[256,1024]{1,0:T(8,128)(2,1)S(1)}, bf16[512,1024]{1,0:T(8,128)(2,1)S(1)}, f32[128,1024]{1,0:T(8,128)S...) custom-call(bf16[2,512,384]{2,1,0:T(8,128)(2,1)S(1)} %shard_map.41.off_wide, ...), custom_call_target="tpu_custom_call" | custom-call | flops 2952790016 | bytes 15728640 | tf_op jit(solution)/shard_map/pallas_call | solution.py:332
  98.9 5.4 %collective-permute-done.4.packed_narrow = bf16[304,384]{1,0:T(8,128)(2,1)S(1)} collective-permute-done((bf16[304,384]{1,0:T(8,128)(2,1)S(1)}, bf16[304,384]{1,0:T(8,128)(2,1)S(1)}, u32[]{:S(2)}, u32[]{:S(2)}) %collective-permute-start.4) | collective-permute-done | bytes 233504 | tf_op jit(solution)/shard_map/ppermute | solution.py:22
  104.3 0.0 collective-permute-done.packed_wide
  104.3 4.3 %shard_map.45 = bf16[2,1,1024,512]{3,2,1,0:T(8,128)(2,1)} custom-call(s32[1]{0:T(128)} %bitcast.col_ref, bf16[400,384]{1,0:T(8,128)(2,1)S(1)} %collective-permute-done.packed_wide, bf16[304,384]{1,0:T(8,128)(2,1)S(1)} %collective-permute-done.4.packed_narrow, bf16[1024,1024]{1,0:T(8,128)(2,1)S(1)} %get-tuple-element.37.right_own, ...), custom_call_target="tpu_custom_call" | custom-call | flops 3221225472 | bytes 15728640 | tf_op jit(solution)/shard_map/pallas_call | solution.py:384
Async XLA Ops:
  6.3 14.9 %copy-start.6 = (bf16[32,2,8,128]{3,2,1,0:T(8,128)(2,1)S(1)}, bf16[32,2,8,128]{3,2,1,0:T(8,128)(2,1)}, u32[]{:S(2)}) copy-start(bf16[32,2,8,128]{3,2,1,0:T(8,128)(2,1)} %get-tuple-element.30) | copy-start | bytes 393220
  6.3 15.9 %copy-start.5 = (bf16[32,2,8,128]{3,2,1,0:T(8,128)(2,1)S(1)}, bf16[32,2,8,128]{3,2,1,0:T(8,128)(2,1)}, u32[]{:S(2)}) copy-start(bf16[32,2,8,128]{3,2,1,0:T(8,128)(2,1)} %get-tuple-element.31) | copy-start | bytes 393220
  6.3 16.8 %copy-start.4 = (bf16[32,2,8,128]{3,2,1,0:T(8,128)(2,1)S(1)}, bf16[32,2,8,128]{3,2,1,0:T(8,128)(2,1)}, u32[]{:S(2)}) copy-start(bf16[32,2,8,128]{3,2,1,0:T(8,128)(2,1)} %get-tuple-element.32) | copy-start | bytes 393220
  6.3 60.2 %copy-start.3 = (s32[1024]{0:T(1024)S(1)}, s32[1024]{0:T(1024)}, u32[]{:S(2)}) copy-start(s32[1024]{0:T(1024)} %param.4) | copy-start | bytes 12292
  6.3 54.9 %all-to-all-start = ((bf16[128,2,8,384]{3,2,1,0:T(8,128)(2,1)}), bf16[128,2,8,384]{3,2,1,0:T(8,128)(2,1)S(1)}, u32[]{:S(2)}, u32[]{:S(2)}) async-start(bf16[128,2,8,384]{3,2,1,0:T(8,128)(2,1)} %bitcast.12), calls=%async_computation | async-start | bytes 3145728 | tf_op jit(solution)/shard_map/all_to_all | solution.py:408
  21.2 2.7 %collective-permute-start.1 = (bf16[32,2,8,128]{3,2,1,0:T(8,128)(2,1)S(1)}, bf16[32,2,8,128]{3,2,1,0:T(8,128)(2,1)S(1)}, u32[]{:S(2)}, u32[]{:S(2)}) collective-permute-start(bf16[32,2,8,128]{3,2,1,0:T(8,128)(2,1)S(1)} %copy-done.6), channel_id=1, source_target_pairs={{0,2},{2,0},{4,6},{6,4},{8,10},{10,8},{12,14},{14,12},{16,18},{18,... | collective-permute-start | bytes 393224 | tf_op jit(solution)/shard_map/ppermute | solution.py:412
  22.2 7.5 %collective-permute-start.2 = (bf16[32,2,8,128]{3,2,1,0:T(8,128)(2,1)S(1)}, bf16[32,2,8,128]{3,2,1,0:T(8,128)(2,1)S(1)}, u32[]{:S(2)}, u32[]{:S(2)}) collective-permute-start(bf16[32,2,8,128]{3,2,1,0:T(8,128)(2,1)S(1)} %copy-done.5), channel_id=1, source_target_pairs={{0,16},{2,18},{4,20},{6,22},{8,24},{10,26},{12,28},{14,30},{16,0},... | collective-permute-start | bytes 393224 | tf_op jit(solution)/shard_map/ppermute | solution.py:412
  23.1 13.4 %collective-permute-start.3 = (bf16[32,2,8,128]{3,2,1,0:T(8,128)(2,1)S(1)}, bf16[32,2,8,128]{3,2,1,0:T(8,128)(2,1)S(1)}, u32[]{:S(2)}, u32[]{:S(2)}) collective-permute-start(bf16[32,2,8,128]{3,2,1,0:T(8,128)(2,1)S(1)} %copy-done.4), channel_id=1, source_target_pairs={{0,18},{2,16},{4,22},{6,20},{8,26},{10,24},{12,30},{14,28},{16,2},... | collective-permute-start | bytes 393224 | tf_op jit(solution)/shard_map/ppermute | solution.py:412
  24.0 12.5 %copy-start = (bf16[32,2,8,128]{3,2,1,0:T(8,128)(2,1)}, bf16[32,2,8,128]{3,2,1,0:T(8,128)(2,1)S(1)}, u32[]{:S(2)}) copy-start(bf16[32,2,8,128]{3,2,1,0:T(8,128)(2,1)S(1)} %collective-permute-done.1.refs_1_) | copy-start | bytes 393220
  29.7 6.8 %copy-start.1 = (bf16[32,2,8,128]{3,2,1,0:T(8,128)(2,1)}, bf16[32,2,8,128]{3,2,1,0:T(8,128)(2,1)S(1)}, u32[]{:S(2)}) copy-start(bf16[32,2,8,128]{3,2,1,0:T(8,128)(2,1)S(1)} %collective-permute-done.2.refs_2_) | copy-start | bytes 393220
  36.5 0.6 copy-start.2
  61.2 21.8 %all-to-all-start.1 = ((bf16[32,4,2,8,128]{4,3,2,1,0:T(8,128)(2,1)}), bf16[32,4,2,8,128]{4,3,2,1,0:T(8,128)(2,1)S(1)}, u32[]{:S(2)}, u32[]{:S(2)}) async-start(bf16[32,4,2,8,128]{4,3,2,1,0:T(8,128)(2,1)} %shard_map.39), calls=%async_computation.1 | async-start | bytes 1048576 | tf_op jit(solution)/shard_map/all_to_all | solution.py:408
  67.7 23.8 %collective-permute-start.5 = (bf16[2,512,384]{2,1,0:T(8,128)(2,1)S(1)}, bf16[2,512,384]{2,1,0:T(8,128)(2,1)}, u32[]{:S(2)}, u32[]{:S(2)}) collective-permute-start(bf16[2,512,384]{2,1,0:T(8,128)(2,1)S(1)} %shard_map.41.off_wide), channel_id=1, source_target_pairs={{0,1},{1,0},{2,3},{3,2},{4,5},{5,4},{6,7},{7,6},{8,9},{9,8},{10,11... | collective-permute-start | bytes 2359304 | tf_op jit(solution)/shard_map/ppermute | solution.py:22
  83.6 12.3 %collective-permute-start.6 = (bf16[2,512,128]{2,1,0:T(8,128)(2,1)S(1)}, bf16[2,512,128]{2,1,0:T(8,128)(2,1)S(1)}, u32[]{:S(2)}, u32[]{:S(2)}) collective-permute-start(bf16[2,512,128]{2,1,0:T(8,128)(2,1)S(1)} %shard_map.42.off_narrow), channel_id=1, source_target_pairs={{0,1},{1,0},{2,3},{3,2},{4,5},{5,4},{6,7},{7,6},{8,9},{9,8},{10,11... | collective-permute-start | bytes 786440 | tf_op jit(solution)/shard_map/ppermute | solution.py:22
  87.5 16.8 %collective-permute-start = (bf16[400,384]{1,0:T(8,128)(2,1)S(1)}, bf16[400,384]{1,0:T(8,128)(2,1)S(1)}, u32[]{:S(2)}, u32[]{:S(2)}) collective-permute-start(bf16[400,384]{1,0:T(8,128)(2,1)S(1)} %get-tuple-element.28), channel_id=1, source_target_pairs={{0,1},{1,0},{2,3},{3,2},{4,5},{5,4},{6,7},{7,6},{8,9},{9,8},{10,11... | collective-permute-start | bytes 921608 | tf_op jit(solution)/shard_map/ppermute | solution.py:22
  88.6 15.7 %collective-permute-start.4 = (bf16[304,384]{1,0:T(8,128)(2,1)S(1)}, bf16[304,384]{1,0:T(8,128)(2,1)S(1)}, u32[]{:S(2)}, u32[]{:S(2)}) collective-permute-start(bf16[304,384]{1,0:T(8,128)(2,1)S(1)} %get-tuple-element.35), channel_id=1, source_target_pairs={{0,1},{1,0},{2,3},{3,2},{4,5},{5,4},{6,7},{7,6},{8,9},{9,8},{10,11... | collective-permute-start | bytes 700424 | tf_op jit(solution)/shard_map/ppermute | solution.py:22

commit v5 on v4

--- a/solution.py
+++ b/solution.py
@@ -63,50 +63,69 @@
     return k // 2 * 8 + k % 2
 
 
-def dft_kernel(near_ref, table_ref, traces_ref, wide_ref, *rest):
+def transform(table_ref, traces_ref, stage_ref):
+    sources, width, samples = traces_ref.shape
+    rows = table_ref.shape[0]
+    value = dot(table_ref[...], traces_ref[...].reshape(sources * width, samples), NT)
+    for s in range(sources):
+        stage_ref[pl.ds(s, rows, stride=sources), :] = value[:, s * width : (s + 1) * width]
+
+
+def wide_dft_kernel(table_ref, traces_ref, out_ref, stage_ref):
+    transform(table_ref, traces_ref, stage_ref)
+    out_ref[...] = stage_ref[...].reshape(out_ref.shape).astype(BF16)
+
+
+def narrow_dft_kernel(near_ref, table_ref, traces_ref, *rest):
     *narrow_refs, stage_ref = rest
-    sources = traces_ref.shape[0]
-    blocks, rows, lanes = stage_ref.shape
-    rows //= sources
-    for s in range(sources):
-        value = dot(table_ref[...], traces_ref[s], NT)
-        for b in range(blocks):
-            stage_ref.at[b][pl.ds(s, rows, stride=sources), :] = value[:, b * lanes : (b + 1) * lanes]
-    for b in range(blocks):
-        wide_ref[:, :, b * lanes : (b + 1) * lanes] = stage_ref[b].reshape(rows, sources, lanes).astype(BF16)
-
-    @pl.when(pl.program_id(0) == pl.num_programs(0) - 1)
-    def _():
-        step = 2 * sources
-        for k, narrow_ref in enumerate(narrow_refs):
-            near = near_ref[0] ^ near_bits(k)
-            for index in range(narrow_ref.shape[0]):
-                at = pl.multiple_of((far_owner(index) + near) * step, step)
-                narrow_ref[index] = stage_ref[blocks - 1, pl.ds(at, step), :].reshape(2, sources, lanes).astype(BF16)
-
-
-def dft(near, table, traces):
+    transform(table_ref, traces_ref, stage_ref)
+    _, parts, sources, width = narrow_refs[0].shape
+    step = parts * sources
+    for k, narrow_ref in enumerate(narrow_refs):
+        near = near_ref[0] ^ near_bits(k)
+        for index in range(narrow_ref.shape[0]):
+            at = pl.multiple_of((far_owner(index) + near) * step, step)
+            narrow_ref[index] = stage_ref[pl.ds(at, step), :].reshape(parts, sources, width).astype(BF16)
+
+
+def wide_dft(table, traces):
     rows, samples = table.shape
     sources, receivers, _ = traces.shape
-    width = 2 * NARROW
-    assert receivers == WIDE + NARROW == 2 * width
-    wide = jax.ShapeDtypeStruct((rows, sources, WIDE), BF16)
+    assert receivers == WIDE + NARROW
+    return call(
+        wide_dft_kernel,
+        jax.ShapeDtypeStruct((rows, sources, WIDE), BF16),
+        2 * rows * samples * sources * WIDE,
+        2 * (sources * WIDE * samples + rows * samples + rows * sources * WIDE),
+        60,
+        grid=(WIDE // NARROW,),
+        in_specs=[
+            pl.BlockSpec((rows, samples), lambda j: (0, 0)),
+            pl.BlockSpec((sources, NARROW, samples), lambda j: (0, j, 0)),
+        ],
+        out_specs=pl.BlockSpec((rows, sources, NARROW), lambda j: (0, 0, j)),
+        scratch_shapes=[pltpu.VMEM((rows * sources, NARROW), F32)],
+    )(table, traces)
+
+
+def narrow_dft(near, table, traces):
+    rows, samples = table.shape
+    sources = traces.shape[0]
     narrow = (rows // 2 // NEAR, 2, sources, NARROW)
     return call(
-        dft_kernel,
-        [wide] + [jax.ShapeDtypeStruct(narrow, BF16)] * NEAR,
-        2 * rows * samples * sources * receivers,
-        2 * (sources * receivers * samples + rows * samples + rows * sources * receivers),
+        narrow_dft_kernel,
+        [jax.ShapeDtypeStruct(narrow, BF16)] * NEAR,
+        2 * rows * samples * sources * NARROW,
+        2 * (sources * NARROW * samples + rows * samples + rows * sources * NARROW),
         60,
-        grid=(receivers // width,),
+        grid=(1,),
         in_specs=[
             SMEM,
             pl.BlockSpec((rows, samples), lambda j: (0, 0)),
-            pl.BlockSpec((sources, width, samples), lambda j: (0, j, 0)),
+            pl.BlockSpec((sources, NARROW, samples), lambda j: (0, WIDE // NARROW, 0)),
         ],
-        out_specs=[pl.BlockSpec((rows, sources, width), lambda j: (0, 0, j))]
-        + [pl.BlockSpec(narrow, lambda j: (0, 0, 0, 0))] * NEAR,
-        scratch_shapes=[pltpu.VMEM((2, rows * sources, NARROW), F32)],
+        out_specs=[pl.BlockSpec(narrow, lambda j: (0, 0, 0, 0))] * NEAR,
+        scratch_shapes=[pltpu.VMEM((rows * sources, NARROW), F32)],
     )(near, table, traces)
 
 
@@ -243,8 +262,8 @@
     )(order, piece, square, below)
 
 
-def unpack(left_wide, left_narrow, wide_ref, narrow_ref):
-    squares = unmix(wide_ref[:WIDE, :], wide_ref[WIDE : WIDE + 1, :])
+def unpack(left_wide, left_narrow, left_square, narrow_ref):
+    left_wide[:WIDE, :] = left_square[...]
     cuts = narrow_ref[2 * NARROW :, :]
     rest = NARROW - 2 * CUT
     mixed = jnp.concatenate([cuts[:, :NARROW], cuts[:, NARROW : 2 * NARROW], cuts[:rest, 2 * NARROW :]], axis=0)
@@ -252,7 +271,6 @@
     for part in range(2):
         low = narrow_ref[part * NARROW : (part + 1) * NARROW, :]
         at = slice(part * WIDE, (part + 1) * WIDE)
-        left_wide[:WIDE, at] = squares[part]
         left_wide[WIDE:, at] = low
         at = slice(part * NARROW, (part + 1) * NARROW)
         left_narrow[:WIDE, at] = turn(low).astype(BF16)
@@ -271,7 +289,9 @@
     return ((block.astype(F32) + turn(turned)) * 0.5).astype(BF16)
 
 
-def early_kernel(own_ref, off_wide, off_narrow, their_wide, right_own, upper_wide, right_wide, part_own, part_other):
+def early_kernel(
+    own_ref, off_wide, off_narrow, their_wide, packed_wide, right_own, upper_wide, right_wide, left_square, part_own, part_other
+):
     half = own_ref.shape[1]
     put_right(right_own, own_ref[0], own_ref[1])
     lows = []
@@ -281,7 +301,10 @@
         upper_wide[:, part * WIDE : (part + 1) * WIDE] = average(their_wide[part], off)
     put_right(right_wide, *lows)
     part_own[...] = dot(right_own[:half, :], right_own[...]) + dot(upper_wide[...], right_wide[...])
-    part_other[...] = dot(right_wide[:WIDE, :], right_own[...])
+    squares = unmix(packed_wide[:WIDE, :], packed_wide[WIDE : WIDE + 1, :])
+    for part in range(2):
+        left_square[:, part * WIDE : (part + 1) * WIDE] = squares[part]
+    part_other[...] = dot(right_wide[:WIDE, :], right_own[...]) + dot(left_square[...], right_wide[...])
 
 
 def early(*blocks):
@@ -290,6 +313,7 @@
         jax.ShapeDtypeStruct((2 * half, 2 * half), BF16),
         jax.ShapeDtypeStruct((half, 2 * WIDE), BF16),
         jax.ShapeDtypeStruct((2 * WIDE, 2 * half), BF16),
+        jax.ShapeDtypeStruct((WIDE, 2 * WIDE), BF16),
         jax.ShapeDtypeStruct((half, 2 * half), F32),
         jax.ShapeDtypeStruct((WIDE, 2 * half), F32),
     ]
@@ -342,12 +366,12 @@
 
 
 def second_kernel(
-    scale, col_ref, packed_wide, packed_narrow, right_own, square_own, cube_own,
+    scale, col_ref, packed_narrow, left_square, right_own, square_own, cube_own,
     upper_wide, right_wide, other_wide, cube_wide, upper_narrow, right_narrow, other_narrow, cube_narrow,
     out_ref, left_wide, left_narrow, next_wide, next_narrow, whole_ref, sems,
 ):
     half = WIDE + NARROW
-    unpack(left_wide, left_narrow, packed_wide, packed_narrow)
+    unpack(left_wide, left_narrow, left_square, packed_narrow)
 
     def product(wide, narrow):
         return dot(left_wide[...], wide[...]) + dot(left_narrow[...], narrow[...])
@@ -365,8 +389,9 @@
             copies[-1].start()
         return copies
 
-    other = jnp.concatenate([other_wide[...], other_narrow[...]], axis=0)
-    square = (scale * (other + product(right_wide, right_narrow))).astype(BF16)
+    above = other_wide[...] + dot(left_narrow[:WIDE, :], right_narrow[...])
+    below = other_narrow[...] + dot(left_wide[WIDE:, :], right_wide[...]) + dot(left_narrow[WIDE:, :], right_narrow[...])
+    square = (scale * jnp.concatenate([above, below], axis=0)).astype(BF16)
     put_right(next_wide, square[:WIDE, :half], square[:WIDE, half:])
     put_right(next_narrow, square[WIDE:, :half], square[WIDE:, half:])
     cube = scale * (cube_own[...] + dot(upper_wide[...], next_wide[...]) + dot(upper_narrow[...], next_narrow[...]))
@@ -425,8 +450,10 @@
     near = (apart // 8 & 1) * 2 + (apart & 1)
     far = source_owner // 16 * 4 + (source_owner // 2 & 3)
     mixed_order = (far * NEAR + near) * sources + order % sources
-    wide, *narrow = dft(scalar(owner & NEAR_BITS), dft_table(samples, kept), traces)
+    table = dft_table(samples, kept)
+    wide = wide_dft(table, traces)
     wide = swap(wide.reshape(kept, 2, sources, WIDE))
+    narrow = list(narrow_dft(scalar(owner & NEAR_BITS), table, traces))
     for k in range(1, NEAR):
         narrow[k] = swap_near(narrow[k], near_bits(k))
     narrow = join(narrow)
@@ -440,12 +467,14 @@
     their_off_narrow = partner(off_narrow)
     own, packed_narrow = narrow_block(mixed_order, narrow, square, below)
     packed_narrow = partner(packed_narrow)
-    right_own, upper_wide, right_wide, part_own, other_wide = early(own, off_wide, off_narrow, their_off_wide)
+    right_own, upper_wide, right_wide, left_square, part_own, other_wide = early(
+        own, off_wide, off_narrow, their_off_wide, packed_wide
+    )
     upper_narrow, right_narrow, square_own, other_narrow, cube_own, cube_wide, cube_narrow = first(
         off_wide, off_narrow, their_off_narrow, right_own, right_wide, part_own
     )
     return second(
-        column_half, packed_wide, packed_narrow, right_own, square_own, cube_own,
+        column_half, packed_narrow, left_square, right_own, square_own, cube_own,
         upper_wide, right_wide, other_wide, cube_wide, upper_narrow, right_narrow, other_narrow, cube_narrow,
     )
 

time: 110 us -> 111 us (level)
  Pallas kernels: 23.4 us -> 29 us
  starting transfers between devices: 31.6 us -> 29 us
  waiting for transfers between devices: 52.7 us -> 50.3 us
    all_to_all x2, waiting for transfers between devices: 34.7 us -> 29.7 us  [swap(): lax.all_to_all(piece, 'freq', split_axis=0, concat_axis=0, tiled=True, ax...]
    ppermute x4, waiting for transfers between devices: 5.38 us -> 8.64 us  [partner(): return lax.ppermute(value, 'col', [(0, 1), (1, 0)])]
    pallas_call x1 -> x2, Pallas kernels: 6.28 us -> 9.33 us  [the longest x1 5.93 us: wide_dft(): call(wide_dft_kernel, jax.ShapeDtypeStruct((rows, sources, WIDE), BF16),...]
    ppermute x4, starting transfers between devices: 8.74 us -> 6.38 us  [partner(): return lax.ppermute(value, 'col', [(0, 1), (1, 0)])]
    pallas_call x1, Pallas kernels: 3.02 us -> 4.22 us  [first(): call(functools.partial(first_kernel, 1.0 / math.sqrt(2 * half)), shapes,...]
  transfers between devices with their start and end apart: 9 -> 9, of which waited for: 5 -> 7; matrix products, arithmetic and copies ran while one was open for 0% -> 0% of each run, Pallas kernels for 12% -> 18%
where the time goes in v5:
time: 111 us; the launch traced here: 109 us
  waiting for transfers between devices  50.3 us (45%)
  Pallas kernels  29 us (26%)
  starting transfers between devices  29 us (26%)
    all_to_all x2, waiting for transfers between devices, swap(): lax.all_to_all(piece, 'freq', split_axis=0, concat_axis=0, tiled=True, ax...  29.7 us
    all_to_all x2, starting transfers between devices, swap(): lax.all_to_all(piece, 'freq', split_axis=0, concat_axis=0, tiled=True, ax...  20 us
    ppermute x3, waiting for transfers between devices, swap_near(): lax.ppermute(value, 'freq', [(i, i ^ bits) for i in range(lax.axis_size('...  11.9 us
    ppermute x4, waiting for transfers between devices, partner(): return lax.ppermute(value, 'col', [(0, 1), (1, 0)])  8.64 us
    ppermute x4, starting transfers between devices, partner(): return lax.ppermute(value, 'col', [(0, 1), (1, 0)])  6.38 us
    pallas_call x1, Pallas kernels, wide_dft(): call(wide_dft_kernel, jax.ShapeDtypeStruct((rows, sources, WIDE), BF16),...  5.93 us
    pallas_call x1, Pallas kernels, early(): call(early_kernel, shapes, 24 * half ** 3, 60 * half ** 2, 24, in_specs=[...  5.27 us
    pallas_call x1, Pallas kernels, first(): call(functools.partial(first_kernel, 1.0 / math.sqrt(2 * half)), shapes,...  4.22 us
  transfers between devices with their start and end apart: 9, of which 7 were waited for; matrix products, arithmetic and copies ran while one was open for 0% of the time, Pallas kernels for 18%

profile of v5, /device:TPU:1, one launch (start us, length us, event | category | flops | bytes accessed | tf_op | source)
XLA Modules:
  0.0 109.4 jit_solution(11513493074779256033)
XLA Ops:
  0.0 5.9 %shard_map.39 = bf16[256,8,384]{2,1,0:T(8,128)(2,1)} custom-call(bf16[256,1024]{1,0:T(8,128)(2,1)} %constant.96.clone.table_ref, bf16[8,512,1024]{2,1,0:T(8,128)(2,1)} %traces_ref.3), custom_call_target="tpu_custom_call" | custom-call | flops 1610612736 | bytes 8388608 | tf_op jit(solution)/shard_map/pallas_call | solution.py:95
  5.9 14.8 %all-to-all-start.1 = ((bf16[128,2,8,384]{3,2,1,0:T(8,128)(2,1)}), bf16[128,2,8,384]{3,2,1,0:T(8,128)(2,1)S(1)}, u32[]{:S(2)}, u32[]{:S(2)}) async-start(bf16[128,2,8,384]{3,2,1,0:T(8,128)(2,1)} %bitcast.12), calls=%async_computation.1 | async-start | bytes 3145728 | tf_op jit(solution)/shard_map/all_to_all | solution.py:433
  20.7 3.4 %shard_map.37 = (bf16[32,2,8,128]{3,2,1,0:T(8,128)(2,1)}, bf16[32,2,8,128]{3,2,1,0:T(8,128)(2,1)}, bf16[32,2,8,128]{3,2,1,0:T(8,128)(2,1)}, bf16[32,2,8,128]{3,2,1,0:T(8,128)(2,1)}) custom-call(s32[1]{0:T(128)} %bitcast.2.near_ref, bf16[256,1024]{1,0:T(8,128)(2,1)} %constant.96.clone.table_ref, bf16[8,512,1024]{2,1,0:T(8,128)(2,1)} %traces_ref.3), custom_call_target="tpu_custom_call" | custom-call | flops 536870912 | bytes 3145728 | tf_op jit(solution)/shard_map/pallas_call | solution.py:115
  24.1 0.0 copy-start.3
  24.1 0.9 collective-permute-start
  25.0 0.9 collective-permute-start.1
  25.9 0.8 collective-permute-start.2
  26.7 0.0 collective-permute-done.refs_1_
  26.7 0.0 copy-start
  26.7 6.7 %collective-permute-done.1.refs_2_ = bf16[32,2,8,128]{3,2,1,0:T(8,128)(2,1)S(1)} collective-permute-done((bf16[32,2,8,128]{3,2,1,0:T(8,128)(2,1)}, bf16[32,2,8,128]{3,2,1,0:T(8,128)(2,1)S(1)}, u32[]{:S(2)}, u32[]{:S(2)}) %collective-permute-start.1) | collective-permute-done | bytes 131104 | tf_op jit(solution)/shard_map/ppermute | solution.py:437
  33.4 0.0 copy-start.1
  33.4 5.3 %collective-permute-done.2.refs_3_ = bf16[32,2,8,128]{3,2,1,0:T(8,128)(2,1)S(1)} collective-permute-done((bf16[32,2,8,128]{3,2,1,0:T(8,128)(2,1)}, bf16[32,2,8,128]{3,2,1,0:T(8,128)(2,1)S(1)}, u32[]{:S(2)}, u32[]{:S(2)}) %collective-permute-start.2) | collective-permute-done | bytes 131104 | tf_op jit(solution)/shard_map/ppermute | solution.py:437
  38.6 0.0 copy-start.2
  38.7 0.0 copy-done
  38.7 0.0 copy-done.1
  38.7 0.7 copy-done.2
  39.3 2.0 %shard_map.38 = bf16[32,4,2,8,128]{4,3,2,1,0:T(8,128)(2,1)} custom-call(bf16[32,2,8,128]{3,2,1,0:T(8,128)(2,1)} %get-tuple-element.27.refs_0_, bf16[32,2,8,128]{3,2,1,0:T(8,128)(2,1)} %copy-done, bf16[32,2,8,128]{3,2,1,0:T(8,128)(2,1)} %copy-done.1, bf16[32,2,8,128]{3,2,1,0:T(8,128)(2,1)} %copy-done.2), custom_call_target="tpu_custom_call" | custom-call | bytes 1048576 | tf_op jit(solution)/shard_map/pallas_call | solution.py:141
  41.3 19.4 %all-to-all-done.1.piece_ref = bf16[128,2,8,384]{3,2,1,0:T(8,128)(2,1)S(1)} async-done(((bf16[128,2,8,384]{3,2,1,0:T(8,128)(2,1)}), bf16[128,2,8,384]{3,2,1,0:T(8,128)(2,1)S(1)}, u32[]{:S(2)}, u32[]{:S(2)}) %all-to-all-start.1) | async-done | bytes 1572896 | tf_op jit(solution)/shard_map/all_to_all | solution.py:433
  60.7 5.2 %all-to-all-start = ((bf16[32,4,2,8,128]{4,3,2,1,0:T(8,128)(2,1)}), bf16[32,4,2,8,128]{4,3,2,1,0:T(8,128)(2,1)S(1)}, u32[]{:S(2)}, u32[]{:S(2)}) async-start(bf16[32,4,2,8,128]{4,3,2,1,0:T(8,128)(2,1)} %shard_map.38), calls=%async_computation | async-start | bytes 1048576 | tf_op jit(solution)/shard_map/all_to_all | solution.py:433
  66.0 0.0 copy-done.3
  66.0 0.1 fusion.6
  66.1 1.9 %shard_map.42.off_wide = bf16[2,512,384]{2,1,0:T(8,128)(2,1)} custom-call(s32[1,1024]{1,0:T(1,128)S(1)} %bitcast.10, bf16[128,2,8,384]{3,2,1,0:T(8,128)(2,1)S(1)} %all-to-all-done.1.piece_ref), custom_call_target="tpu_custom_call" | custom-call | flops 805306368 | bytes 2752512 | tf_op jit(solution)/shard_map/pallas_call | solution.py:180
  68.0 2.6 %collective-permute-start.4 = (bf16[2,512,384]{2,1,0:T(8,128)(2,1)}, bf16[2,512,384]{2,1,0:T(8,128)(2,1)}, u32[]{:S(2)}, u32[]{:S(2)}) collective-permute-start(bf16[2,512,384]{2,1,0:T(8,128)(2,1)} %shard_map.42.off_wide), channel_id=1, source_target_pairs={{0,1},{1,0},{2,3},{3,2},{4,5},{5,4},{6,7},{7,6},{8,9},{9,8},{10,11... | collective-permute-start | bytes 2359304 | tf_op jit(solution)/shard_map/ppermute | solution.py:22
  70.6 1.1 %shard_map.40 = (bf16[2,384,384]{2,1,0:T(8,128)(2,1)S(1)}, bf16[2,128,384]{2,1,0:T(8,128)(2,1)S(1)}, bf16[400,384]{1,0:T(8,128)(2,1)S(1)}) custom-call(s32[1,1024]{1,0:T(1,128)S(1)} %bitcast.11, bf16[128,2,8,384]{3,2,1,0:T(8,128)(2,1)S(1)} %all-to-all-done.1.piece_ref), custom_call_target="tpu_custom_call" | custom-call | flops 805306368 | bytes 2752512 | tf_op jit(solution)/shard_map/pallas_call | solution.py:218
  71.8 0.4 collective-permute-start.5
  72.2 10.3 %all-to-all-done = bf16[32,4,2,8,128]{4,3,2,1,0:T(8,128)(2,1)S(1)} async-done(((bf16[32,4,2,8,128]{4,3,2,1,0:T(8,128)(2,1)}), bf16[32,4,2,8,128]{4,3,2,1,0:T(8,128)(2,1)S(1)}, u32[]{:S(2)}, u32[]{:S(2)}) %all-to-all-start) | async-done | bytes 524320 | tf_op jit(solution)/shard_map/all_to_all | solution.py:433
  82.5 0.6 shard_map.43.off_narrow
  83.1 2.7 %collective-permute-start.6 = (bf16[2,512,128]{2,1,0:T(8,128)(2,1)S(1)}, bf16[2,512,128]{2,1,0:T(8,128)(2,1)S(1)}, u32[]{:S(2)}, u32[]{:S(2)}) collective-permute-start(bf16[2,512,128]{2,1,0:T(8,128)(2,1)S(1)} %shard_map.43.off_narrow), channel_id=1, source_target_pairs={{0,1},{1,0},{2,3},{3,2},{4,5},{5,4},{6,7},{7,6},{8,9},{9,8},{10,11... | collective-permute-start | bytes 786440 | tf_op jit(solution)/shard_map/ppermute | solution.py:22
  85.8 0.7 shard_map.41
  86.5 0.6 collective-permute-start.3
  87.1 7.5 %collective-permute-done.5.packed_wide = bf16[400,384]{1,0:T(8,128)(2,1)S(1)} collective-permute-done((bf16[400,384]{1,0:T(8,128)(2,1)S(1)}, bf16[400,384]{1,0:T(8,128)(2,1)S(1)}, u32[]{:S(2)}, u32[]{:S(2)}) %collective-permute-start.5) | collective-permute-done | bytes 307232 | tf_op jit(solution)/shard_map/ppermute | solution.py:22
  94.6 0.0 collective-permute-done.4.their_wide
  94.6 5.3 %shard_map.44 = (bf16[1024,1024]{1,0:T(8,128)(2,1)S(1)}, bf16[512,768]{1,0:T(8,128)(2,1)S(1)}, bf16[768,1024]{1,0:T(8,128)(2,1)S(1)}, bf16[384,768]{1,0:T(8,128)...) custom-call(bf16[2,512,512]{2,1,0:T(8,128)(2,1)S(1)} %get-tuple-element.34.own_ref, ...), custom_call_target="tpu_custom_call" | custom-call | flops 3221225472 | bytes 15728640 | tf_op jit(solution)/shard_map/pallas_call | solution.py:320
  99.9 0.3 collective-permute-done.6.their_narrow
  100.3 4.2 %shard_map.45 = (bf16[512,256]{1,0:T(8,128)(2,1)S(1)}, bf16[256,1024]{1,0:T(8,128)(2,1)S(1)}, bf16[512,1024]{1,0:T(8,128)(2,1)S(1)}, f32[128,1024]{1,0:T(8,128)S...) custom-call(bf16[2,512,384]{2,1,0:T(8,128)(2,1)} %shard_map.42.off_wide, ...), custom_call_target="tpu_custom_call" | custom-call | flops 2952790016 | bytes 15728640 | tf_op jit(solution)/shard_map/pallas_call | solution.py:356
  104.5 0.8 collective-permute-done.3.packed_narrow
  105.3 3.9 %shard_map.46 = bf16[2,1,1024,512]{3,2,1,0:T(8,128)(2,1)} custom-call(s32[1]{0:T(128)} %bitcast.col_ref, bf16[304,384]{1,0:T(8,128)(2,1)S(1)} %collective-permute-done.3.packed_narrow, bf16[384,768]{1,0:T(8,128)(2,1)S(1)} %get-tuple-element.36.left_square, bf16[1024,1024]{1,0:T(8,128)(2,1)S(1)} %get-tuple-element.37.right_own, ...), custom_call_target="tpu_custom_call" | custom-call | flops 3221225472 | bytes 15728640 | tf_op jit(solution)/shard_map/pallas_call | solution.py:409
Async XLA Ops:
  5.9 54.8 %all-to-all-start.1 = ((bf16[128,2,8,384]{3,2,1,0:T(8,128)(2,1)}), bf16[128,2,8,384]{3,2,1,0:T(8,128)(2,1)S(1)}, u32[]{:S(2)}, u32[]{:S(2)}) async-start(bf16[128,2,8,384]{3,2,1,0:T(8,128)(2,1)} %bitcast.12), calls=%async_computation.1 | async-start | bytes 3145728 | tf_op jit(solution)/shard_map/all_to_all | solution.py:433
  24.1 41.9 %copy-start.3 = (s32[1024]{0:T(1024)S(1)}, s32[1024]{0:T(1024)}, u32[]{:S(2)}) copy-start(s32[1024]{0:T(1024)} %param.4) | copy-start | bytes 12292
  24.1 2.6 %collective-permute-start = (bf16[32,2,8,128]{3,2,1,0:T(8,128)(2,1)}, bf16[32,2,8,128]{3,2,1,0:T(8,128)(2,1)S(1)}, u32[]{:S(2)}, u32[]{:S(2)}) collective-permute-start(bf16[32,2,8,128]{3,2,1,0:T(8,128)(2,1)} %get-tuple-element.28), channel_id=1, source_target_pairs={{0,2},{2,0},{4,6},{6,4},{8,10},{10,8},{12,14},{14,12},{16,18},{18,... | collective-permute-start | bytes 393224 | tf_op jit(solution)/shard_map/ppermute | solution.py:437
  25.0 8.4 %collective-permute-start.1 = (bf16[32,2,8,128]{3,2,1,0:T(8,128)(2,1)}, bf16[32,2,8,128]{3,2,1,0:T(8,128)(2,1)S(1)}, u32[]{:S(2)}, u32[]{:S(2)}) collective-permute-start(bf16[32,2,8,128]{3,2,1,0:T(8,128)(2,1)} %get-tuple-element.29), channel_id=1, source_target_pairs={{0,16},{2,18},{4,20},{6,22},{8,24},{10,26},{12,28},{14,30},{16,0},... | collective-permute-start | bytes 393224 | tf_op jit(solution)/shard_map/ppermute | solution.py:437
  25.9 12.8 %collective-permute-start.2 = (bf16[32,2,8,128]{3,2,1,0:T(8,128)(2,1)}, bf16[32,2,8,128]{3,2,1,0:T(8,128)(2,1)S(1)}, u32[]{:S(2)}, u32[]{:S(2)}) collective-permute-start(bf16[32,2,8,128]{3,2,1,0:T(8,128)(2,1)} %get-tuple-element.30), channel_id=1, source_target_pairs={{0,18},{2,16},{4,22},{6,20},{8,26},{10,24},{12,30},{14,28},{16,2},... | collective-permute-start | bytes 393224 | tf_op jit(solution)/shard_map/ppermute | solution.py:437
  26.7 11.9 %copy-start = (bf16[32,2,8,128]{3,2,1,0:T(8,128)(2,1)}, bf16[32,2,8,128]{3,2,1,0:T(8,128)(2,1)S(1)}, u32[]{:S(2)}) copy-start(bf16[32,2,8,128]{3,2,1,0:T(8,128)(2,1)S(1)} %collective-permute-done.refs_1_) | copy-start | bytes 393220
  33.4 5.3 %copy-start.1 = (bf16[32,2,8,128]{3,2,1,0:T(8,128)(2,1)}, bf16[32,2,8,128]{3,2,1,0:T(8,128)(2,1)S(1)}, u32[]{:S(2)}) copy-start(bf16[32,2,8,128]{3,2,1,0:T(8,128)(2,1)S(1)} %collective-permute-done.1.refs_2_) | copy-start | bytes 393220
  38.6 0.7 copy-start.2
  60.7 21.8 %all-to-all-start = ((bf16[32,4,2,8,128]{4,3,2,1,0:T(8,128)(2,1)}), bf16[32,4,2,8,128]{4,3,2,1,0:T(8,128)(2,1)S(1)}, u32[]{:S(2)}, u32[]{:S(2)}) async-start(bf16[32,4,2,8,128]{4,3,2,1,0:T(8,128)(2,1)} %shard_map.38), calls=%async_computation | async-start | bytes 1048576 | tf_op jit(solution)/shard_map/all_to_all | solution.py:433
  68.0 26.6 %collective-permute-start.4 = (bf16[2,512,384]{2,1,0:T(8,128)(2,1)}, bf16[2,512,384]{2,1,0:T(8,128)(2,1)}, u32[]{:S(2)}, u32[]{:S(2)}) collective-permute-start(bf16[2,512,384]{2,1,0:T(8,128)(2,1)} %shard_map.42.off_wide), channel_id=1, source_target_pairs={{0,1},{1,0},{2,3},{3,2},{4,5},{5,4},{6,7},{7,6},{8,9},{9,8},{10,11... | collective-permute-start | bytes 2359304 | tf_op jit(solution)/shard_map/ppermute | solution.py:22
  71.8 22.8 %collective-permute-start.5 = (bf16[400,384]{1,0:T(8,128)(2,1)S(1)}, bf16[400,384]{1,0:T(8,128)(2,1)S(1)}, u32[]{:S(2)}, u32[]{:S(2)}) collective-permute-start(bf16[400,384]{1,0:T(8,128)(2,1)S(1)} %get-tuple-element.35), channel_id=1, source_target_pairs={{0,1},{1,0},{2,3},{3,2},{4,5},{5,4},{6,7},{7,6},{8,9},{9,8},{10,11... | collective-permute-start | bytes 921608 | tf_op jit(solution)/shard_map/ppermute | solution.py:22
  83.1 17.2 %collective-permute-start.6 = (bf16[2,512,128]{2,1,0:T(8,128)(2,1)S(1)}, bf16[2,512,128]{2,1,0:T(8,128)(2,1)S(1)}, u32[]{:S(2)}, u32[]{:S(2)}) collective-permute-start(bf16[2,512,128]{2,1,0:T(8,128)(2,1)S(1)} %shard_map.43.off_narrow), channel_id=1, source_target_pairs={{0,1},{1,0},{2,3},{3,2},{4,5},{5,4},{6,7},{7,6},{8,9},{9,8},{10,11... | collective-permute-start | bytes 786440 | tf_op jit(solution)/shard_map/ppermute | solution.py:22
  86.5 18.8 %collective-permute-start.3 = (bf16[304,384]{1,0:T(8,128)(2,1)S(1)}, bf16[304,384]{1,0:T(8,128)(2,1)S(1)}, u32[]{:S(2)}, u32[]{:S(2)}) collective-permute-start(bf16[304,384]{1,0:T(8,128)(2,1)S(1)} %get-tuple-element.33), channel_id=1, source_target_pairs={{0,1},{1,0},{2,3},{3,2},{4,5},{5,4},{6,7},{7,6},{8,9},{9,8},{10,11... | collective-permute-start | bytes 700424 | tf_op jit(solution)/shard_map/ppermute | solution.py:22

commit v6 on v5

--- a/solution.py
+++ b/solution.py
@@ -23,7 +23,7 @@
 
 
 WIDE, NARROW = 384, 128
-NEAR, NEAR_BITS = 4, 9
+NEAR = 16
 
 
 def dft_table(samples, kept):
@@ -55,14 +55,6 @@
     )
 
 
-def far_owner(index):
-    return index // 4 * 16 + index % 4 * 2
-
-
-def near_bits(k):
-    return k // 2 * 8 + k % 2
-
-
 def transform(table_ref, traces_ref, stage_ref):
     sources, width, samples = traces_ref.shape
     rows = table_ref.shape[0]
@@ -82,9 +74,9 @@
     _, parts, sources, width = narrow_refs[0].shape
     step = parts * sources
     for k, narrow_ref in enumerate(narrow_refs):
-        near = near_ref[0] ^ near_bits(k)
+        near = near_ref[0] ^ k
         for index in range(narrow_ref.shape[0]):
-            at = pl.multiple_of((far_owner(index) + near) * step, step)
+            at = pl.multiple_of((index * NEAR + near) * step, step)
             narrow_ref[index] = stage_ref[pl.ds(at, step), :].reshape(parts, sources, width).astype(BF16)
 
 
@@ -446,20 +438,17 @@
     owner = lax.axis_index("freq")
     order = jnp.roll(source_row, -column_half * (size // 2))[None, :]
     source_owner = order // sources
-    apart = source_owner ^ owner
-    near = (apart // 8 & 1) * 2 + (apart & 1)
-    far = source_owner // 16 * 4 + (source_owner // 2 & 3)
-    mixed_order = (far * NEAR + near) * sources + order % sources
+    mixed_order = (source_owner ^ owner % NEAR) * sources + order % sources
     table = dft_table(samples, kept)
     wide = wide_dft(table, traces)
     wide = swap(wide.reshape(kept, 2, sources, WIDE))
-    narrow = list(narrow_dft(scalar(owner & NEAR_BITS), table, traces))
+    narrow = list(narrow_dft(scalar(owner % NEAR), table, traces))
     for k in range(1, NEAR):
-        narrow[k] = swap_near(narrow[k], near_bits(k))
+        narrow[k] = swap_near(narrow[k], k)
     narrow = join(narrow)
     off_wide = off_block(order, wide)
     their_off_wide = partner(off_wide)
-    groups = [[far_owner(i) + near_bits(k) for i in range(kept // NEAR)] for k in range(NEAR)]
+    groups = [[i * NEAR + k for i in range(kept // NEAR)] for k in range(NEAR)]
     narrow = swap(narrow, groups).reshape(kept, 2, sources, NARROW)
     square, below, packed_wide = wide_block(order, wide)
     packed_wide = partner(packed_wide)

time: 111 us -> 110 us (level)
  waiting for transfers between devices: 50.3 us -> 31.4 us
  starting transfers between devices: 29 us -> 46.6 us
    ppermute x3 -> x15, starting transfers between devices: 2.59 us -> 21.4 us  [swap_near(): lax.ppermute(value, 'freq', [(i, i ^ bits) for i in range(lax.axis_size('...]
    all_to_all x2, waiting for transfers between devices: 29.7 us -> 18.9 us  [swap(): lax.all_to_all(piece, 'freq', split_axis=0, concat_axis=0, tiled=True, ax...]
    ppermute x3 -> x15, waiting for transfers between devices: 11.9 us -> 5.39 us  [swap_near(): lax.ppermute(value, 'freq', [(i, i ^ bits) for i in range(lax.axis_size('...]
    ppermute x4, waiting for transfers between devices: 8.64 us -> 7.16 us  [partner(): return lax.ppermute(value, 'col', [(0, 1), (1, 0)])]
  transfers between devices with their start and end apart: 9 -> 21, of which waited for: 7 -> 10; matrix products, arithmetic and copies ran while one was open for 0% -> 0% of each run, Pallas kernels for 18% -> 18%
where the time goes in v6:
time: 110 us; the launch traced here: 108 us
  starting transfers between devices  46.6 us (42%)
  waiting for transfers between devices  31.4 us (29%)
  Pallas kernels  28.6 us (26%)
    ppermute x15, starting transfers between devices, swap_near(): lax.ppermute(value, 'freq', [(i, i ^ bits) for i in range(lax.axis_size('...  21.4 us
    all_to_all x2, starting transfers between devices, swap(): lax.all_to_all(piece, 'freq', split_axis=0, concat_axis=0, tiled=True, ax...  19 us
    all_to_all x2, waiting for transfers between devices, swap(): lax.all_to_all(piece, 'freq', split_axis=0, concat_axis=0, tiled=True, ax...  18.9 us
    ppermute x4, waiting for transfers between devices, partner(): return lax.ppermute(value, 'col', [(0, 1), (1, 0)])  7.16 us
    ppermute x4, starting transfers between devices, partner(): return lax.ppermute(value, 'col', [(0, 1), (1, 0)])  6.2 us
    pallas_call x1, Pallas kernels, wide_dft(): call(wide_dft_kernel, jax.ShapeDtypeStruct((rows, sources, WIDE), BF16),...  5.93 us
    ppermute x15, waiting for transfers between devices, swap_near(): lax.ppermute(value, 'freq', [(i, i ^ bits) for i in range(lax.axis_size('...  5.39 us
    pallas_call x1, Pallas kernels, early(): call(early_kernel, shapes, 24 * half ** 3, 60 * half ** 2, 24, in_specs=[...  5.25 us
  transfers between devices with their start and end apart: 21, of which 10 were waited for; matrix products, arithmetic and copies ran while one was open for 0% of the time, Pallas kernels for 18%

profile of v6, /device:TPU:1, one launch (start us, length us, event | category | flops | bytes accessed | tf_op | source)
XLA Modules:
  0.0 107.7 jit_solution(13326950515355093175)
XLA Ops:
  0.0 5.9 %shard_map.39 = bf16[256,8,384]{2,1,0:T(8,128)(2,1)} custom-call(bf16[256,1024]{1,0:T(8,128)(2,1)} %constant.76.clone.table_ref, bf16[8,512,1024]{2,1,0:T(8,128)(2,1)} %traces_ref.3), custom_call_target="tpu_custom_call" | custom-call | flops 1610612736 | bytes 8388608 | tf_op jit(solution)/shard_map/pallas_call | solution.py:87
  5.9 14.8 %all-to-all-start.1 = ((bf16[128,2,8,384]{3,2,1,0:T(8,128)(2,1)}), bf16[128,2,8,384]{3,2,1,0:T(8,128)(2,1)S(1)}, u32[]{:S(2)}, u32[]{:S(2)}) async-start(bf16[128,2,8,384]{3,2,1,0:T(8,128)(2,1)} %bitcast.12), calls=%async_computation.1 | async-start | bytes 3145728 | tf_op jit(solution)/shard_map/all_to_all | solution.py:425
  20.7 3.4 %shard_map.37 = (bf16[8,2,8,128]{3,2,1,0:T(8,128)(2,1)}, bf16[8,2,8,128]{3,2,1,0:T(8,128)(2,1)}, bf16[8,2,8,128]{3,2,1,0:T(8,128)(2,1)}, bf16[8,2,8,128]{3,2,1,0...) custom-call(s32[1]{0:T(128)} %bitcast.2.near_ref, ...), custom_call_target="tpu_custom_call" | custom-call | flops 536870912 | bytes 3145728 | tf_op jit(solution)/shard_map/pallas_call | solution.py:107
  24.1 1.0 collective-permute-start
  25.1 0.9 collective-permute-start.1
  26.0 0.9 collective-permute-start.2
  26.8 2.4 %collective-permute-start.3 = (bf16[8,2,8,128]{3,2,1,0:T(8,128)(2,1)}, bf16[8,2,8,128]{3,2,1,0:T(8,128)(2,1)S(1)}, u32[]{:S(2)}, u32[]{:S(2)}) collective-permute-start(bf16[8,2,8,128]{3,2,1,0:T(8,128)(2,1)} %get-tuple-element.43), channel_id=1, source_target_pairs={{0,8},{2,10},{4,12},{6,14},{8,0},{10,2},{12,4},{14,6},{16,24},{18,... | collective-permute-start | bytes 98312 | tf_op jit(solution)/shard_map/ppermute | solution.py:429
  29.2 0.9 collective-permute-start.4
  30.1 0.0 collective-permute-done.refs_1_
  30.1 2.1 %collective-permute-start.5 = (bf16[8,2,8,128]{3,2,1,0:T(8,128)(2,1)}, bf16[8,2,8,128]{3,2,1,0:T(8,128)(2,1)S(1)}, u32[]{:S(2)}, u32[]{:S(2)}) collective-permute-start(bf16[8,2,8,128]{3,2,1,0:T(8,128)(2,1)} %get-tuple-element.45), channel_id=1, source_target_pairs={{0,12},{2,14},{4,8},{6,10},{8,4},{10,6},{12,0},{14,2},{16,28},{18,... | collective-permute-start | bytes 98312 | tf_op jit(solution)/shard_map/ppermute | solution.py:429
  32.2 0.9 collective-permute-start.6
  33.1 0.9 collective-permute-start.7
  33.9 1.2 %collective-permute-start.8 = (bf16[8,2,8,128]{3,2,1,0:T(8,128)(2,1)}, bf16[8,2,8,128]{3,2,1,0:T(8,128)(2,1)S(1)}, u32[]{:S(2)}, u32[]{:S(2)}) collective-permute-start(bf16[8,2,8,128]{3,2,1,0:T(8,128)(2,1)} %get-tuple-element.48), channel_id=1, source_target_pairs={{0,18},{2,16},{4,22},{6,20},{8,26},{10,24},{12,30},{14,28},{16,2},... | collective-permute-start | bytes 98312 | tf_op jit(solution)/shard_map/ppermute | solution.py:429
  35.1 0.6 collective-permute-done.4.refs_5_
  35.8 0.4 collective-permute-start.9
  36.2 0.3 collective-permute-done.5.refs_6_
  36.5 2.0 %collective-permute-start.10 = (bf16[8,2,8,128]{3,2,1,0:T(8,128)(2,1)}, bf16[8,2,8,128]{3,2,1,0:T(8,128)(2,1)S(1)}, u32[]{:S(2)}, u32[]{:S(2)}) collective-permute-start(bf16[8,2,8,128]{3,2,1,0:T(8,128)(2,1)} %get-tuple-element.50), channel_id=1, source_target_pairs={{0,22},{2,20},{4,18},{6,16},{8,30},{10,28},{12,26},{14,24},{16,6},... | collective-permute-start | bytes 98312 | tf_op jit(solution)/shard_map/ppermute | solution.py:429
  38.5 0.0 collective-permute-done.6.refs_7_
  38.5 2.3 %collective-permute-start.11 = (bf16[8,2,8,128]{3,2,1,0:T(8,128)(2,1)}, bf16[8,2,8,128]{3,2,1,0:T(8,128)(2,1)S(1)}, u32[]{:S(2)}, u32[]{:S(2)}) collective-permute-start(bf16[8,2,8,128]{3,2,1,0:T(8,128)(2,1)} %get-tuple-element.51), channel_id=1, source_target_pairs={{0,24},{2,26},{4,28},{6,30},{8,16},{10,18},{12,20},{14,22},{16,8},... | collective-permute-start | bytes 98312 | tf_op jit(solution)/shard_map/ppermute | solution.py:429
  40.8 1.7 %collective-permute-start.12 = (bf16[8,2,8,128]{3,2,1,0:T(8,128)(2,1)}, bf16[8,2,8,128]{3,2,1,0:T(8,128)(2,1)S(1)}, u32[]{:S(2)}, u32[]{:S(2)}) collective-permute-start(bf16[8,2,8,128]{3,2,1,0:T(8,128)(2,1)} %get-tuple-element.52), channel_id=1, source_target_pairs={{0,26},{2,24},{4,30},{6,28},{8,18},{10,16},{12,22},{14,20},{16,10}... | collective-permute-start | bytes 98312 | tf_op jit(solution)/shard_map/ppermute | solution.py:429
  42.6 0.0 collective-permute-done.8.refs_9_
  42.6 2.1 %collective-permute-start.13 = (bf16[8,2,8,128]{3,2,1,0:T(8,128)(2,1)}, bf16[8,2,8,128]{3,2,1,0:T(8,128)(2,1)S(1)}, u32[]{:S(2)}, u32[]{:S(2)}) collective-permute-start(bf16[8,2,8,128]{3,2,1,0:T(8,128)(2,1)} %get-tuple-element.53), channel_id=1, source_target_pairs={{0,28},{2,30},{4,24},{6,26},{8,20},{10,22},{12,16},{14,18},{16,12}... | collective-permute-start | bytes 98312 | tf_op jit(solution)/shard_map/ppermute | solution.py:429
  44.6 1.9 %collective-permute-start.14 = (bf16[8,2,8,128]{3,2,1,0:T(8,128)(2,1)}, bf16[8,2,8,128]{3,2,1,0:T(8,128)(2,1)S(1)}, u32[]{:S(2)}, u32[]{:S(2)}) collective-permute-start(bf16[8,2,8,128]{3,2,1,0:T(8,128)(2,1)} %get-tuple-element.54), channel_id=1, source_target_pairs={{0,30},{2,28},{4,26},{6,24},{8,22},{10,20},{12,18},{14,16},{16,14}... | collective-permute-start | bytes 98312 | tf_op jit(solution)/shard_map/ppermute | solution.py:429
  46.5 0.0 collective-permute-done.10.refs_11_
  46.5 0.0 collective-permute-done.11.refs_12_
  46.6 1.3 %collective-permute-done.12.refs_13_ = bf16[8,2,8,128]{3,2,1,0:T(8,128)(2,1)S(1)} collective-permute-done((bf16[8,2,8,128]{3,2,1,0:T(8,128)(2,1)}, bf16[8,2,8,128]{3,2,1,0:T(8,128)(2,1)S(1)}, u32[]{:S(2)}, u32[]{:S(2)}) %collective-permute-start.12) | collective-permute-done | bytes 32800 | tf_op jit(solution)/shard_map/ppermute | solution.py:429
  47.8 0.7 collective-permute-done.13.refs_14_
  48.5 2.5 %collective-permute-done.14.refs_15_ = bf16[8,2,8,128]{3,2,1,0:T(8,128)(2,1)S(1)} collective-permute-done((bf16[8,2,8,128]{3,2,1,0:T(8,128)(2,1)}, bf16[8,2,8,128]{3,2,1,0:T(8,128)(2,1)S(1)}, u32[]{:S(2)}, u32[]{:S(2)}) %collective-permute-start.14) | collective-permute-done | bytes 32800 | tf_op jit(solution)/shard_map/ppermute | solution.py:429
  51.1 0.5 copy-done.14
  51.6 1.8 %shard_map.38 = bf16[8,16,2,8,128]{4,3,2,1,0:T(8,128)(2,1)} custom-call(bf16[8,2,8,128]{3,2,1,0:T(8,128)(2,1)} %get-tuple-element.39.refs_0_, bf16[8,2,8,128]{3,2,1,0:T(8,128)(2,1)} %copy-done, bf16[8,2,8,128]{3,2,1,0:T(8,128)(2,1)} %copy-done.1, bf16[8,2,8,128]{3,2,1,0:T(8,128)(2,1)} %copy-done.2, bf16[8,2,8,128]{3,2,1,0:T(8,128)(2,1)} %copy-done.3, ...), custom_call_target="tpu_custom_call" | custom-call | bytes 1048576 | tf_op jit(solution)/shard_map/pallas_call | solution.py:133
  53.4 7.3 %all-to-all-done.1.piece_ref = bf16[128,2,8,384]{3,2,1,0:T(8,128)(2,1)S(1)} async-done(((bf16[128,2,8,384]{3,2,1,0:T(8,128)(2,1)}), bf16[128,2,8,384]{3,2,1,0:T(8,128)(2,1)S(1)}, u32[]{:S(2)}, u32[]{:S(2)}) %all-to-all-start.1) | async-done | bytes 1572896 | tf_op jit(solution)/shard_map/all_to_all | solution.py:425
  60.7 4.2 %all-to-all-start = ((bf16[8,16,2,8,128]{4,3,2,1,0:T(8,128)(2,1)}), bf16[8,16,2,8,128]{4,3,2,1,0:T(8,128)(2,1)S(1)}, u32[]{:S(2)}, u32[]{:S(2)}) async-start(bf16[8,16,2,8,128]{4,3,2,1,0:T(8,128)(2,1)} %shard_map.38), calls=%async_computation | async-start | bytes 1048576 | tf_op jit(solution)/shard_map/all_to_all | solution.py:425
  64.9 0.1 fusion.2
  65.0 1.9 %shard_map.42.off_wide = bf16[2,512,384]{2,1,0:T(8,128)(2,1)} custom-call(s32[1,1024]{1,0:T(1,128)S(1)} %bitcast.10, bf16[128,2,8,384]{3,2,1,0:T(8,128)(2,1)S(1)} %all-to-all-done.1.piece_ref), custom_call_target="tpu_custom_call" | custom-call | flops 805306368 | bytes 2752512 | tf_op jit(solution)/shard_map/pallas_call | solution.py:172
  66.9 2.6 %collective-permute-start.16 = (bf16[2,512,384]{2,1,0:T(8,128)(2,1)}, bf16[2,512,384]{2,1,0:T(8,128)(2,1)}, u32[]{:S(2)}, u32[]{:S(2)}) collective-permute-start(bf16[2,512,384]{2,1,0:T(8,128)(2,1)} %shard_map.42.off_wide), channel_id=1, source_target_pairs={{0,1},{1,0},{2,3},{3,2},{4,5},{5,4},{6,7},{7,6},{8,9},{9,8},{10,11... | collective-permute-start | bytes 2359304 | tf_op jit(solution)/shard_map/ppermute | solution.py:22
  69.6 1.1 %shard_map.40 = (bf16[2,384,384]{2,1,0:T(8,128)(2,1)S(1)}, bf16[2,128,384]{2,1,0:T(8,128)(2,1)S(1)}, bf16[400,384]{1,0:T(8,128)(2,1)S(1)}) custom-call(s32[1,1024]{1,0:T(1,128)S(1)} %bitcast.11, bf16[128,2,8,384]{3,2,1,0:T(8,128)(2,1)S(1)} %all-to-all-done.1.piece_ref), custom_call_target="tpu_custom_call" | custom-call | flops 805306368 | bytes 2752512 | tf_op jit(solution)/shard_map/pallas_call | solution.py:210
  70.7 0.4 collective-permute-start.17
  71.2 11.6 %all-to-all-done = bf16[8,16,2,8,128]{4,3,2,1,0:T(8,128)(2,1)S(1)} async-done(((bf16[8,16,2,8,128]{4,3,2,1,0:T(8,128)(2,1)}), bf16[8,16,2,8,128]{4,3,2,1,0:T(8,128)(2,1)S(1)}, u32[]{:S(2)}, u32[]{:S(2)}) %all-to-all-start) | async-done | bytes 524320 | tf_op jit(solution)/shard_map/all_to_all | solution.py:425
  82.8 0.6 shard_map.43.off_narrow
  83.3 2.7 %collective-permute-start.18 = (bf16[2,512,128]{2,1,0:T(8,128)(2,1)S(1)}, bf16[2,512,128]{2,1,0:T(8,128)(2,1)S(1)}, u32[]{:S(2)}, u32[]{:S(2)}) collective-permute-start(bf16[2,512,128]{2,1,0:T(8,128)(2,1)S(1)} %shard_map.43.off_narrow), channel_id=1, source_target_pairs={{0,1},{1,0},{2,3},{3,2},{4,5},{5,4},{6,7},{7,6},{8,9},{9,8},{10,11... | collective-permute-start | bytes 786440 | tf_op jit(solution)/shard_map/ppermute | solution.py:22
  86.0 0.7 shard_map.41
  86.7 0.4 collective-permute-start.15
  87.2 6.0 %collective-permute-done.17.packed_wide = bf16[400,384]{1,0:T(8,128)(2,1)S(1)} collective-permute-done((bf16[400,384]{1,0:T(8,128)(2,1)S(1)}, bf16[400,384]{1,0:T(8,128)(2,1)S(1)}, u32[]{:S(2)}, u32[]{:S(2)}) %collective-permute-start.17) | collective-permute-done | bytes 307232 | tf_op jit(solution)/shard_map/ppermute | solution.py:22
  93.2 5.2 %shard_map.44 = (bf16[1024,1024]{1,0:T(8,128)(2,1)S(1)}, bf16[512,768]{1,0:T(8,128)(2,1)S(1)}, bf16[768,1024]{1,0:T(8,128)(2,1)S(1)}, bf16[384,768]{1,0:T(8,128)...) custom-call(bf16[2,512,512]{2,1,0:T(8,128)(2,1)S(1)} %get-tuple-element.58.own_ref, ...), custom_call_target="tpu_custom_call" | custom-call | flops 3221225472 | bytes 15728640 | tf_op jit(solution)/shard_map/pallas_call | solution.py:312
  98.4 0.4 collective-permute-done.18.their_narrow
  98.8 4.2 %shard_map.45 = (bf16[512,256]{1,0:T(8,128)(2,1)S(1)}, bf16[256,1024]{1,0:T(8,128)(2,1)S(1)}, bf16[512,1024]{1,0:T(8,128)(2,1)S(1)}, f32[128,1024]{1,0:T(8,128)S...) custom-call(bf16[2,512,384]{2,1,0:T(8,128)(2,1)} %shard_map.42.off_wide, ...), custom_call_target="tpu_custom_call" | custom-call | flops 2952790016 | bytes 15728640 | tf_op jit(solution)/shard_map/pallas_call | solution.py:348
  103.0 0.8 collective-permute-done.15.packed_narrow
  103.8 3.7 %shard_map.46 = bf16[2,1,1024,512]{3,2,1,0:T(8,128)(2,1)} custom-call(s32[1]{0:T(128)} %bitcast.col_ref, bf16[304,384]{1,0:T(8,128)(2,1)S(1)} %collective-permute-done.15.packed_narrow, bf16[384,768]{1,0:T(8,128)(2,1)S(1)} %get-tuple-element.60.left_square, bf16[1024,1024]{1,0:T(8,128)(2,1)S(1)} %get-tuple-element.61.right_own, ...), custom_call_target="tpu_custom_call" | custom-call | flops 3221225472 | bytes 15728640 | tf_op jit(solution)/shard_map/pallas_call | solution.py:401
  (37 shorter events, 0.1 us)
Async XLA Ops:
  5.9 54.8 %all-to-all-start.1 = ((bf16[128,2,8,384]{3,2,1,0:T(8,128)(2,1)}), bf16[128,2,8,384]{3,2,1,0:T(8,128)(2,1)S(1)}, u32[]{:S(2)}, u32[]{:S(2)}) async-start(bf16[128,2,8,384]{3,2,1,0:T(8,128)(2,1)} %bitcast.12), calls=%async_computation.1 | async-start | bytes 3145728 | tf_op jit(solution)/shard_map/all_to_all | solution.py:425
  24.1 40.8 %copy-start.15 = (s32[1024]{0:T(1024)S(1)}, s32[1024]{0:T(1024)}, u32[]{:S(2)}) copy-start(s32[1024]{0:T(1024)} %param.4) | copy-start | bytes 12292
  24.1 6.0 %collective-permute-start = (bf16[8,2,8,128]{3,2,1,0:T(8,128)(2,1)}, bf16[8,2,8,128]{3,2,1,0:T(8,128)(2,1)S(1)}, u32[]{:S(2)}, u32[]{:S(2)}) collective-permute-start(bf16[8,2,8,128]{3,2,1,0:T(8,128)(2,1)} %get-tuple-element.40), channel_id=1, source_target_pairs={{0,2},{2,0},{4,6},{6,4},{8,10},{10,8},{12,14},{14,12},{16,18},{18,... | collective-permute-start | bytes 98312 | tf_op jit(solution)/shard_map/ppermute | solution.py:429
  25.1 7.1 %collective-permute-start.1 = (bf16[8,2,8,128]{3,2,1,0:T(8,128)(2,1)}, bf16[8,2,8,128]{3,2,1,0:T(8,128)(2,1)S(1)}, u32[]{:S(2)}, u32[]{:S(2)}) collective-permute-start(bf16[8,2,8,128]{3,2,1,0:T(8,128)(2,1)} %get-tuple-element.41), channel_id=1, source_target_pairs={{0,4},{2,6},{4,0},{6,2},{8,12},{10,14},{12,8},{14,10},{16,20},{18,... | collective-permute-start | bytes 98312 | tf_op jit(solution)/shard_map/ppermute | solution.py:429
  26.0 7.1 %collective-permute-start.2 = (bf16[8,2,8,128]{3,2,1,0:T(8,128)(2,1)}, bf16[8,2,8,128]{3,2,1,0:T(8,128)(2,1)S(1)}, u32[]{:S(2)}, u32[]{:S(2)}) collective-permute-start(bf16[8,2,8,128]{3,2,1,0:T(8,128)(2,1)} %get-tuple-element.42), channel_id=1, source_target_pairs={{0,6},{2,4},{4,2},{6,0},{8,14},{10,12},{12,10},{14,8},{16,22},{18,... | collective-permute-start | bytes 98312 | tf_op jit(solution)/shard_map/ppermute | solution.py:429
  26.8 7.1 %collective-permute-start.3 = (bf16[8,2,8,128]{3,2,1,0:T(8,128)(2,1)}, bf16[8,2,8,128]{3,2,1,0:T(8,128)(2,1)S(1)}, u32[]{:S(2)}, u32[]{:S(2)}) collective-permute-start(bf16[8,2,8,128]{3,2,1,0:T(8,128)(2,1)} %get-tuple-element.43), channel_id=1, source_target_pairs={{0,8},{2,10},{4,12},{6,14},{8,0},{10,2},{12,4},{14,6},{16,24},{18,... | collective-permute-start | bytes 98312 | tf_op jit(solution)/shard_map/ppermute | solution.py:429
  29.2 6.5 %collective-permute-start.4 = (bf16[8,2,8,128]{3,2,1,0:T(8,128)(2,1)}, bf16[8,2,8,128]{3,2,1,0:T(8,128)(2,1)S(1)}, u32[]{:S(2)}, u32[]{:S(2)}) collective-permute-start(bf16[8,2,8,128]{3,2,1,0:T(8,128)(2,1)} %get-tuple-element.44), channel_id=1, source_target_pairs={{0,10},{2,8},{4,14},{6,12},{8,2},{10,0},{12,6},{14,4},{16,26},{18,... | collective-permute-start | bytes 98312 | tf_op jit(solution)/shard_map/ppermute | solution.py:429
  30.1 20.9 %copy-start = (bf16[8,2,8,128]{3,2,1,0:T(8,128)(2,1)}, bf16[8,2,8,128]{3,2,1,0:T(8,128)(2,1)S(1)}, u32[]{:S(2)}) copy-start(bf16[8,2,8,128]{3,2,1,0:T(8,128)(2,1)S(1)} %collective-permute-done.refs_1_) | copy-start | bytes 98308
  30.1 6.4 %collective-permute-start.5 = (bf16[8,2,8,128]{3,2,1,0:T(8,128)(2,1)}, bf16[8,2,8,128]{3,2,1,0:T(8,128)(2,1)S(1)}, u32[]{:S(2)}, u32[]{:S(2)}) collective-permute-start(bf16[8,2,8,128]{3,2,1,0:T(8,128)(2,1)} %get-tuple-element.45), channel_id=1, source_target_pairs={{0,12},{2,14},{4,8},{6,10},{8,4},{10,6},{12,0},{14,2},{16,28},{18,... | collective-permute-start | bytes 98312 | tf_op jit(solution)/shard_map/ppermute | solution.py:429
  32.2 18.8 %copy-start.1 = (bf16[8,2,8,128]{3,2,1,0:T(8,128)(2,1)}, bf16[8,2,8,128]{3,2,1,0:T(8,128)(2,1)S(1)}, u32[]{:S(2)}) copy-start(bf16[8,2,8,128]{3,2,1,0:T(8,128)(2,1)S(1)} %collective-permute-done.1.refs_2_) | copy-start | bytes 98308
  32.2 6.3 %collective-permute-start.6 = (bf16[8,2,8,128]{3,2,1,0:T(8,128)(2,1)}, bf16[8,2,8,128]{3,2,1,0:T(8,128)(2,1)S(1)}, u32[]{:S(2)}, u32[]{:S(2)}) collective-permute-start(bf16[8,2,8,128]{3,2,1,0:T(8,128)(2,1)} %get-tuple-element.46), channel_id=1, source_target_pairs={{0,14},{2,12},{4,10},{6,8},{8,6},{10,4},{12,2},{14,0},{16,30},{18,... | collective-permute-start | bytes 98312 | tf_op jit(solution)/shard_map/ppermute | solution.py:429
  33.1 17.9 %copy-start.2 = (bf16[8,2,8,128]{3,2,1,0:T(8,128)(2,1)}, bf16[8,2,8,128]{3,2,1,0:T(8,128)(2,1)S(1)}, u32[]{:S(2)}) copy-start(bf16[8,2,8,128]{3,2,1,0:T(8,128)(2,1)S(1)} %collective-permute-done.2.refs_3_) | copy-start | bytes 98308
  33.1 7.8 %collective-permute-start.7 = (bf16[8,2,8,128]{3,2,1,0:T(8,128)(2,1)}, bf16[8,2,8,128]{3,2,1,0:T(8,128)(2,1)S(1)}, u32[]{:S(2)}, u32[]{:S(2)}) collective-permute-start(bf16[8,2,8,128]{3,2,1,0:T(8,128)(2,1)} %get-tuple-element.47), channel_id=1, source_target_pairs={{0,16},{2,18},{4,20},{6,22},{8,24},{10,26},{12,28},{14,30},{16,0},... | collective-permute-start | bytes 98312 | tf_op jit(solution)/shard_map/ppermute | solution.py:429
  33.9 17.0 %copy-start.3 = (bf16[8,2,8,128]{3,2,1,0:T(8,128)(2,1)}, bf16[8,2,8,128]{3,2,1,0:T(8,128)(2,1)S(1)}, u32[]{:S(2)}) copy-start(bf16[8,2,8,128]{3,2,1,0:T(8,128)(2,1)S(1)} %collective-permute-done.3.refs_4_) | copy-start | bytes 98308
  33.9 8.6 %collective-permute-start.8 = (bf16[8,2,8,128]{3,2,1,0:T(8,128)(2,1)}, bf16[8,2,8,128]{3,2,1,0:T(8,128)(2,1)S(1)}, u32[]{:S(2)}, u32[]{:S(2)}) collective-permute-start(bf16[8,2,8,128]{3,2,1,0:T(8,128)(2,1)} %get-tuple-element.48), channel_id=1, source_target_pairs={{0,18},{2,16},{4,22},{6,20},{8,26},{10,24},{12,30},{14,28},{16,2},... | collective-permute-start | bytes 98312 | tf_op jit(solution)/shard_map/ppermute | solution.py:429
  35.8 15.2 %copy-start.4 = (bf16[8,2,8,128]{3,2,1,0:T(8,128)(2,1)}, bf16[8,2,8,128]{3,2,1,0:T(8,128)(2,1)S(1)}, u32[]{:S(2)}) copy-start(bf16[8,2,8,128]{3,2,1,0:T(8,128)(2,1)S(1)} %collective-permute-done.4.refs_5_) | copy-start | bytes 98308
  35.8 8.9 %collective-permute-start.9 = (bf16[8,2,8,128]{3,2,1,0:T(8,128)(2,1)}, bf16[8,2,8,128]{3,2,1,0:T(8,128)(2,1)S(1)}, u32[]{:S(2)}, u32[]{:S(2)}) collective-permute-start(bf16[8,2,8,128]{3,2,1,0:T(8,128)(2,1)} %get-tuple-element.49), channel_id=1, source_target_pairs={{0,20},{2,22},{4,16},{6,18},{8,28},{10,30},{12,24},{14,26},{16,4},... | collective-permute-start | bytes 98312 | tf_op jit(solution)/shard_map/ppermute | solution.py:429
  36.5 14.5 %copy-start.5 = (bf16[8,2,8,128]{3,2,1,0:T(8,128)(2,1)}, bf16[8,2,8,128]{3,2,1,0:T(8,128)(2,1)S(1)}, u32[]{:S(2)}) copy-start(bf16[8,2,8,128]{3,2,1,0:T(8,128)(2,1)S(1)} %collective-permute-done.5.refs_6_) | copy-start | bytes 98308
  36.5 10.0 %collective-permute-start.10 = (bf16[8,2,8,128]{3,2,1,0:T(8,128)(2,1)}, bf16[8,2,8,128]{3,2,1,0:T(8,128)(2,1)S(1)}, u32[]{:S(2)}, u32[]{:S(2)}) collective-permute-start(bf16[8,2,8,128]{3,2,1,0:T(8,128)(2,1)} %get-tuple-element.50), channel_id=1, source_target_pairs={{0,22},{2,20},{4,18},{6,16},{8,30},{10,28},{12,26},{14,24},{16,6},... | collective-permute-start | bytes 98312 | tf_op jit(solution)/shard_map/ppermute | solution.py:429
  38.5 12.5 %copy-start.6 = (bf16[8,2,8,128]{3,2,1,0:T(8,128)(2,1)}, bf16[8,2,8,128]{3,2,1,0:T(8,128)(2,1)S(1)}, u32[]{:S(2)}) copy-start(bf16[8,2,8,128]{3,2,1,0:T(8,128)(2,1)S(1)} %collective-permute-done.6.refs_7_) | copy-start | bytes 98308
  38.5 8.0 %collective-permute-start.11 = (bf16[8,2,8,128]{3,2,1,0:T(8,128)(2,1)}, bf16[8,2,8,128]{3,2,1,0:T(8,128)(2,1)S(1)}, u32[]{:S(2)}, u32[]{:S(2)}) collective-permute-start(bf16[8,2,8,128]{3,2,1,0:T(8,128)(2,1)} %get-tuple-element.51), channel_id=1, source_target_pairs={{0,24},{2,26},{4,28},{6,30},{8,16},{10,18},{12,20},{14,22},{16,8},... | collective-permute-start | bytes 98312 | tf_op jit(solution)/shard_map/ppermute | solution.py:429
  40.8 10.2 %copy-start.7 = (bf16[8,2,8,128]{3,2,1,0:T(8,128)(2,1)}, bf16[8,2,8,128]{3,2,1,0:T(8,128)(2,1)S(1)}, u32[]{:S(2)}) copy-start(bf16[8,2,8,128]{3,2,1,0:T(8,128)(2,1)S(1)} %collective-permute-done.7.refs_8_) | copy-start | bytes 98308
  40.8 7.0 %collective-permute-start.12 = (bf16[8,2,8,128]{3,2,1,0:T(8,128)(2,1)}, bf16[8,2,8,128]{3,2,1,0:T(8,128)(2,1)S(1)}, u32[]{:S(2)}, u32[]{:S(2)}) collective-permute-start(bf16[8,2,8,128]{3,2,1,0:T(8,128)(2,1)} %get-tuple-element.52), channel_id=1, source_target_pairs={{0,26},{2,24},{4,30},{6,28},{8,18},{10,16},{12,22},{14,20},{16,10}... | collective-permute-start | bytes 98312 | tf_op jit(solution)/shard_map/ppermute | solution.py:429
  42.6 8.5 %copy-start.8 = (bf16[8,2,8,128]{3,2,1,0:T(8,128)(2,1)}, bf16[8,2,8,128]{3,2,1,0:T(8,128)(2,1)S(1)}, u32[]{:S(2)}) copy-start(bf16[8,2,8,128]{3,2,1,0:T(8,128)(2,1)S(1)} %collective-permute-done.8.refs_9_) | copy-start | bytes 98308
  42.6 5.9 %collective-permute-start.13 = (bf16[8,2,8,128]{3,2,1,0:T(8,128)(2,1)}, bf16[8,2,8,128]{3,2,1,0:T(8,128)(2,1)S(1)}, u32[]{:S(2)}, u32[]{:S(2)}) collective-permute-start(bf16[8,2,8,128]{3,2,1,0:T(8,128)(2,1)} %get-tuple-element.53), channel_id=1, source_target_pairs={{0,28},{2,30},{4,24},{6,26},{8,20},{10,22},{12,16},{14,18},{16,12}... | collective-permute-start | bytes 98312 | tf_op jit(solution)/shard_map/ppermute | solution.py:429
  44.6 6.4 %copy-start.9 = (bf16[8,2,8,128]{3,2,1,0:T(8,128)(2,1)}, bf16[8,2,8,128]{3,2,1,0:T(8,128)(2,1)S(1)}, u32[]{:S(2)}) copy-start(bf16[8,2,8,128]{3,2,1,0:T(8,128)(2,1)S(1)} %collective-permute-done.9.refs_10_) | copy-start | bytes 98308
  44.6 6.3 %collective-permute-start.14 = (bf16[8,2,8,128]{3,2,1,0:T(8,128)(2,1)}, bf16[8,2,8,128]{3,2,1,0:T(8,128)(2,1)S(1)}, u32[]{:S(2)}, u32[]{:S(2)}) collective-permute-start(bf16[8,2,8,128]{3,2,1,0:T(8,128)(2,1)} %get-tuple-element.54), channel_id=1, source_target_pairs={{0,30},{2,28},{4,26},{6,24},{8,22},{10,20},{12,18},{14,16},{16,14}... | collective-permute-start | bytes 98312 | tf_op jit(solution)/shard_map/ppermute | solution.py:429
  46.5 4.5 %copy-start.10 = (bf16[8,2,8,128]{3,2,1,0:T(8,128)(2,1)}, bf16[8,2,8,128]{3,2,1,0:T(8,128)(2,1)S(1)}, u32[]{:S(2)}) copy-start(bf16[8,2,8,128]{3,2,1,0:T(8,128)(2,1)S(1)} %collective-permute-done.10.refs_11_) | copy-start | bytes 98308
  46.5 4.5 %copy-start.11 = (bf16[8,2,8,128]{3,2,1,0:T(8,128)(2,1)}, bf16[8,2,8,128]{3,2,1,0:T(8,128)(2,1)S(1)}, u32[]{:S(2)}) copy-start(bf16[8,2,8,128]{3,2,1,0:T(8,128)(2,1)S(1)} %collective-permute-done.11.refs_12_) | copy-start | bytes 98308
  47.8 3.3 %copy-start.12 = (bf16[8,2,8,128]{3,2,1,0:T(8,128)(2,1)}, bf16[8,2,8,128]{3,2,1,0:T(8,128)(2,1)S(1)}, u32[]{:S(2)}) copy-start(bf16[8,2,8,128]{3,2,1,0:T(8,128)(2,1)S(1)} %collective-permute-done.12.refs_13_) | copy-start | bytes 98308
  48.5 2.6 %copy-start.13 = (bf16[8,2,8,128]{3,2,1,0:T(8,128)(2,1)}, bf16[8,2,8,128]{3,2,1,0:T(8,128)(2,1)S(1)}, u32[]{:S(2)}) copy-start(bf16[8,2,8,128]{3,2,1,0:T(8,128)(2,1)S(1)} %collective-permute-done.13.refs_14_) | copy-start | bytes 98308
  51.0 0.6 copy-start.14
  60.7 22.1 %all-to-all-start = ((bf16[8,16,2,8,128]{4,3,2,1,0:T(8,128)(2,1)}), bf16[8,16,2,8,128]{4,3,2,1,0:T(8,128)(2,1)S(1)}, u32[]{:S(2)}, u32[]{:S(2)}) async-start(bf16[8,16,2,8,128]{4,3,2,1,0:T(8,128)(2,1)} %shard_map.38), calls=%async_computation | async-start | bytes 1048576 | tf_op jit(solution)/shard_map/all_to_all | solution.py:425
  66.9 26.2 %collective-permute-start.16 = (bf16[2,512,384]{2,1,0:T(8,128)(2,1)}, bf16[2,512,384]{2,1,0:T(8,128)(2,1)}, u32[]{:S(2)}, u32[]{:S(2)}) collective-permute-start(bf16[2,512,384]{2,1,0:T(8,128)(2,1)} %shard_map.42.off_wide), channel_id=1, source_target_pairs={{0,1},{1,0},{2,3},{3,2},{4,5},{5,4},{6,7},{7,6},{8,9},{9,8},{10,11... | collective-permute-start | bytes 2359304 | tf_op jit(solution)/shard_map/ppermute | solution.py:22
  70.7 22.5 %collective-permute-start.17 = (bf16[400,384]{1,0:T(8,128)(2,1)S(1)}, bf16[400,384]{1,0:T(8,128)(2,1)S(1)}, u32[]{:S(2)}, u32[]{:S(2)}) collective-permute-start(bf16[400,384]{1,0:T(8,128)(2,1)S(1)} %get-tuple-element.59), channel_id=1, source_target_pairs={{0,1},{1,0},{2,3},{3,2},{4,5},{5,4},{6,7},{7,6},{8,9},{9,8},{10,11... | collective-permute-start | bytes 921608 | tf_op jit(solution)/shard_map/ppermute | solution.py:22
  83.3 15.5 %collective-permute-start.18 = (bf16[2,512,128]{2,1,0:T(8,128)(2,1)S(1)}, bf16[2,512,128]{2,1,0:T(8,128)(2,1)S(1)}, u32[]{:S(2)}, u32[]{:S(2)}) collective-permute-start(bf16[2,512,128]{2,1,0:T(8,128)(2,1)S(1)} %shard_map.43.off_narrow), channel_id=1, source_target_pairs={{0,1},{1,0},{2,3},{3,2},{4,5},{5,4},{6,7},{7,6},{8,9},{9,8},{10,11... | collective-permute-start | bytes 786440 | tf_op jit(solution)/shard_map/ppermute | solution.py:22
  86.7 17.1 %collective-permute-start.15 = (bf16[304,384]{1,0:T(8,128)(2,1)S(1)}, bf16[304,384]{1,0:T(8,128)(2,1)S(1)}, u32[]{:S(2)}, u32[]{:S(2)}) collective-permute-start(bf16[304,384]{1,0:T(8,128)(2,1)S(1)} %get-tuple-element.57), channel_id=1, source_target_pairs={{0,1},{1,0},{2,3},{3,2},{4,5},{5,4},{6,7},{7,6},{8,9},{9,8},{10,11... | collective-permute-start | bytes 700424 | tf_op jit(solution)/shard_map/ppermute | solution.py:22
